TPU v7x, 512 devices: a whole 4x8x8 slice. The times are simulated.
512 devices in a mesh: dom: 8 (over y_hi, core), slab: 64 (over y_lo, z, x).
Axes of the slice: x: 4, y: 8 (y_hi: 4, y_lo: 2; y = y_hi * 2 + y_lo), z: 8, core: 2. Of those that a mesh axis runs over, the one named last changes fastest.
Arguments:
- weights: bfloat16 [64, 256, 64, 128], P('slab', 'dom'), may hold values from 0 to 0.049804688
- moments: bfloat16 [64, 256, 10, 128], P('slab', 'dom'), may hold values from -6 to 6
- block_tile: int32 [64, 256], P('slab', 'dom'), may hold values from 0 to 255, as said below
- block_slab: int32 [64, 256], P('slab', 'dom'), may hold values from 0 to 63, as said below
- block_count: int32 [64, 8], P('slab', 'dom'), may hold values from 8 to 32, as said below
Outputs:
- filtered: float32 [10, 128, 64, 128], P(None, 'slab', 'dom')
Inputs may be any that keep to these rules, and one draw needn't show every extreme that they name: Every device's used blocks are its first block_count slots; in every slab one device uses all 32 slots. `block_slab`: A block's target slab is its own slab or one of the two next to it on the periodic loop. `block_tile`: A block whose target is the next slab names a tile of that slab's first plane (tiles below 128); one whose target is the previous slab a tile of that slab's last plane (tiles from 128).
All inputs are finite; a program needn't handle non-finite values.
Results may differ from a plain program's by a relative error of at most 0.00035.
Values may be sent and summed in bfloat16 or wider, within the bound.
No kernel may reach another device: no remote copies, remote signals or barrier semaphores. Data moves between devices by JAX's collectives and lax.ppermute only.
A program may use at most 64 MiB of HBM per device.

v0:
```python
import jax
import jax.numpy as jnp
from jax import lax
from jax.sharding import PartitionSpec as P

SX = 2
RY = 8
NZ = 128


group_blocks = 8
diffusion = 0.16


def passed_along(block, axis, distance):
    devices = range(lax.axis_size(axis))
    route = [((i - distance) % len(devices), i) for i in devices]
    return lax.ppermute(block, axis, route)


def extended_2(block, sides, width, periodic):
    for axis, dim in sides:
        count = lax.axis_size(axis)
        forward = [(i, i + 1) for i in range(count - 1)]
        if periodic:
            forward.append((count - 1, 0))
        backward = [(target, source) for source, target in forward]
        low = lax.ppermute(
            lax.slice_in_dim(block, block.shape[dim] - width, None, axis=dim), axis, forward
        )
        high = lax.ppermute(lax.slice_in_dim(block, 0, width, axis=dim), axis, backward)
        block = jnp.concatenate([low, block, high], axis=dim)
    return block


def smooth_padded(padded):
    center = padded[:, 1:-1, 1:-1]
    zpadded = jnp.pad(center, ((0, 0), (0, 0), (0, 0), (1, 1)))
    adjacent_cell = padded[:, 2:, 1:-1] + padded[:, :-2, 1:-1]
    adjacent_cell = adjacent_cell + padded[:, 1:-1, 2:] + padded[:, 1:-1, :-2]
    adjacent_cell = adjacent_cell + zpadded[:, :, :, 2:] + zpadded[:, :, :, :-2]
    return center + diffusion * (adjacent_cell - 6.0 * center)


def add_group(accum, weight_group, moment_group, tile_grp):
    term_list = jnp.einsum(
        "ixb,iab->ixa", moment_group, weight_group, preferred_element_type=jnp.float32
    )
    term_list = term_list.reshape(term_list.shape[0], term_list.shape[1] * term_list.shape[2])
    term_list = jnp.where((tile_grp >= 0)[:, None], term_list, 0.0)
    return accum.at[jnp.maximum(tile_grp, 0)].add(term_list)


def local(weights, moments, block_tile, block_slab, block_count):
    weight_loc = weights[0]
    moment_loc = moments[0]
    tile_loc = block_tile[0]
    slab_loc = block_slab[0]
    used = block_count[0, 0]
    n_slabs = lax.axis_size("slab")
    n_doms = lax.axis_size("dom")
    my_slab = lax.axis_index("slab")
    slot_total, tile_cells, particles = weight_loc.shape
    moment_count = moment_loc.shape[1]
    rows_all = RY * n_doms
    z_tiles = NZ // tile_cells
    plane_tiles = rows_all * z_tiles
    offset = jnp.mod(slab_loc - my_slab + 1, n_slabs) - 1
    ext_tile = jnp.where(
        offset == 0,
        tile_loc + plane_tiles,
        jnp.where(
            offset == 1, tile_loc + (SX + 1) * plane_tiles, tile_loc - (SX - 1) * plane_tiles
        ),
    )
    slot_ids = jnp.arange(slot_total, dtype=jnp.int32)
    ext_tile = jnp.where(slot_ids < used, ext_tile, -1)
    accum = jnp.zeros(((SX + 2) * plane_tiles, moment_count * tile_cells), jnp.float32)
    group_steps = (used + group_blocks - 1) // group_blocks

    def local_step(step_index, accum_now):
        first = step_index * group_blocks
        weight_group = lax.dynamic_slice_in_dim(weight_loc, first, group_blocks, 0)
        moment_group = lax.dynamic_slice_in_dim(moment_loc, first, group_blocks, 0)
        tile_grp = lax.dynamic_slice_in_dim(ext_tile, first, group_blocks, 0)
        return add_group(accum_now, weight_group, moment_group, tile_grp)

    accum = lax.fori_loop(0, group_steps, local_step, accum)
    extended = accum.reshape(SX + 2, rows_all, z_tiles, moment_count, tile_cells)
    extended = extended.transpose(3, 0, 1, 2, 4).reshape(moment_count, SX + 2, rows_all, NZ)
    from_next = passed_along(extended[:, 0], "slab", -1)
    from_prev = passed_along(extended[:, SX + 1], "slab", 1)
    summed = extended[:, 1 : SX + 1]
    summed = summed.at[:, SX - 1].add(from_next)
    summed = summed.at[:, 0].add(from_prev)
    owned = lax.psum_scatter(summed, "dom", scatter_dimension=2, tiled=True)
    result = owned
    for pass_number in range(2):
        padded = extended_2(result, (("slab", 1),), 1, True)
        padded = extended_2(padded, (("dom", 2),), 1, False)
        result = smooth_padded(padded)
    return result


def solution(mesh):
    return jax.shard_map(
        local,
        mesh=mesh,
        in_specs=(
            P("slab", "dom", None, None),
            P("slab", "dom", None, None),
            P("slab", "dom"),
            P("slab", "dom"),
            P("slab", "dom"),
        ),
        out_specs=P(None, "slab", "dom", None),
        check_vma=False,
    )
```

profile of v0, /device:TPU:40, one launch (start us, length us, event | category | flops | bytes accessed | tf_op | source)
XLA Modules:
  0.0 140.0 jit_solution(15659952232683660968)
XLA Ops:
  8.9 5.1 %while.12 = (s32[]{:T(128)}, f32[512,640]{1,0:T(8,128)S(1)}, s32[]{:T(128)}, s32[32]{0:T(128)S(1)}, bf16[32,10,128]{2,1,0:T(8,128)(2,1)S(1)}, /*index=5*/bf16[32...) while((s32[]{:T(128)}, f32[512,640]{1,0:T(8,128)S(1)}, ...), condition=%wide.region_2.3_spmd, body=%wide.region_0.2_spmd.sunk | while | flops 1320982 | bytes 1558287 | solution.py:88
  10.3 1.2 scatter_custom_fusion.5
  12.8 1.2 scatter_custom_fusion.5
  14.1 2.4 %reshape.92 = f32[4,64,2,10,64]{4,3,2,1,0:T(8,128)} reshape(f32[512,640]{1,0:T(8,128)S(1)} %get-tuple-element.62) | data formatting | bytes 2621440 | tf_op jit(solution)/shard_map/reshape | solution.py:89
  16.5 3.5 %copy.14 = f32[10,4,64,2,64]{4,3,2,1,0:T(2,128)S(1)} copy(f32[10,4,64,2,64]{4,0,3,2,1:T(8,128)} %bitcast.32) | data formatting | bytes 2621440 | tf_op jit(solution)/shard_map/transpose | solution.py:90
  20.0 2.5 %reshape.93 = f32[10,4,64,128]{3,2,1,0:T(8,128)} reshape(f32[10,4,64,2,64]{4,3,2,1,0:T(2,128)S(1)} %copy.14) | data formatting | bytes 2621440 | tf_op jit(solution)/shard_map/reshape | solution.py:90
  22.5 1.2 slice_bitcast_fusion
  23.7 13.9 %collective-permute-start = (f32[10,64,128]{2,1,0:T(8,128)S(1)}, f32[10,64,128]{2,1,0:T(8,128)S(1)}, u32[]{:S(2)}, u32[]{:S(2)}) collective-permute-start(f32[10,64,128]{2,1,0:T(8,128)S(1)} %get-tuple-element.76), channel_id=1, source_target_pairs={{1,0},{2,1},{3,2},{4,3},{5,4},{6,5},{7,6},{8,7},{9,8},{10,9},{11,1... | collective-permute-start | bytes 983048 | tf_op jit(solution)/shard_map/ppermute | solution.py:18
  37.7 2.1 %collective-permute-start.1 = (f32[10,64,128]{2,1,0:T(8,128)S(1)}, f32[10,64,128]{2,1,0:T(8,128)S(1)}, u32[]{:S(2)}, u32[]{:S(2)}) collective-permute-start(f32[10,64,128]{2,1,0:T(8,128)S(1)} %get-tuple-element.75), channel_id=1, source_target_pairs={{63,0},{0,1},{1,2},{2,3},{3,4},{4,5},{5,6},{6,7},{7,8},{8,9},{9,10... | collective-permute-start | bytes 983048 | tf_op jit(solution)/shard_map/ppermute | solution.py:18
  39.8 4.8 %collective-permute-done = f32[10,64,128]{2,1,0:T(8,128)S(1)} collective-permute-done((f32[10,64,128]{2,1,0:T(8,128)S(1)}, f32[10,64,128]{2,1,0:T(8,128)S(1)}, u32[]{:S(2)}, u32[]{:S(2)}) %collective-permute-start) | collective-permute-done | bytes 327712 | tf_op jit(solution)/shard_map/ppermute | solution.py:18
  44.7 8.4 %collective-permute-done.1 = f32[10,64,128]{2,1,0:T(8,128)S(1)} collective-permute-done((f32[10,64,128]{2,1,0:T(8,128)S(1)}, f32[10,64,128]{2,1,0:T(8,128)S(1)}, u32[]{:S(2)}, u32[]{:S(2)}) %collective-permute-start.1) | collective-permute-done | bytes 327712 | tf_op jit(solution)/shard_map/ppermute | solution.py:18
  54.0 31.9 %reduce-scatter.2.cloned.1.call-done = f32[10,2,8,128]{3,2,0,1:T(8,128)} async-done(((f32[10,2,64,128]{3,2,0,1:T(8,128)}), f32[10,2,8,128]{3,2,0,1:T(8,128)}) %reduce-scatter.2.cloned.1.call-update) | async-done | bytes 81936 | tf_op jit(solution)/shard_map/reduce_scatter | solution.py:96
  86.8 3.6 %collective-permute-start.3 = (f32[10,1,8,128]{3,2,0,1:T(8,128)S(1)}, f32[10,1,8,128]{3,2,0,1:T(8,128)S(1)}, u32[]{:S(2)}, u32[]{:S(2)}) collective-permute-start(f32[10,1,8,128]{3,2,0,1:T(8,128)S(1)} %get-tuple-element.84), channel_id=1, source_target_pairs={{0,1},{1,2},{2,3},{3,4},{4,5},{5,6},{6,7},{7,8},{8,9},{9,10},{10,1... | collective-permute-start | bytes 122888 | tf_op jit(solution)/shard_map/ppermute | solution.py:28
  90.4 6.5 %collective-permute-start.2 = (f32[10,1,8,128]{3,2,0,1:T(8,128)S(1)}, f32[10,1,8,128]{3,2,0,1:T(8,128)S(1)}, u32[]{:S(2)}, u32[]{:S(2)}) collective-permute-start(f32[10,1,8,128]{3,2,0,1:T(8,128)S(1)} %get-tuple-element.83), channel_id=1, source_target_pairs={{1,0},{2,1},{3,2},{4,3},{5,4},{6,5},{7,6},{8,7},{9,8},{10,9},{11,1... | collective-permute-start | bytes 122888 | tf_op jit(solution)/shard_map/ppermute | solution.py:31
  98.5 4.2 %collective-permute-start.4 = (f32[10,4,1,128]{3,2,0,1:T(1,128)S(1)}, f32[10,4,1,128]{3,2,0,1:T(1,128)S(1)}, u32[]{:S(2)}, u32[]{:S(2)}) collective-permute-start(f32[10,4,1,128]{3,2,0,1:T(1,128)S(1)} %get-tuple-element.79), channel_id=1, source_target_pairs={{64,0},{128,64},{192,128},{256,192},{320,256},{384,320},{448,384},... | collective-permute-start | bytes 61448 | tf_op jit(solution)/shard_map/ppermute | solution.py:31
  102.7 1.9 %collective-permute-start.5 = (f32[10,4,1,128]{3,2,0,1:T(1,128)S(1)}, f32[10,4,1,128]{3,2,0,1:T(1,128)S(1)}, u32[]{:S(2)}, u32[]{:S(2)}) collective-permute-start(f32[10,4,1,128]{3,2,0,1:T(1,128)S(1)} %get-tuple-element.80), channel_id=1, source_target_pairs={{0,64},{64,128},{128,192},{192,256},{256,320},{320,384},{384,448},... | collective-permute-start | bytes 61448 | tf_op jit(solution)/shard_map/ppermute | solution.py:28
  104.7 5.5 %collective-permute-done.5 = f32[10,4,1,128]{3,2,0,1:T(1,128)S(1)} collective-permute-done((f32[10,4,1,128]{3,2,0,1:T(1,128)S(1)}, f32[10,4,1,128]{3,2,0,1:T(1,128)S(1)}, u32[]{:S(2)}, u32[]{:S(2)}) %collective-permute-start.5) | collective-permute-done | bytes 20512 | tf_op jit(solution)/shard_map/ppermute | solution.py:28
  110.1 1.2 fusion.15
  111.4 1.9 %collective-permute-start.7 = (f32[10,1,8,128]{3,2,0,1:T(8,128)S(1)}, f32[10,1,8,128]{3,2,0,1:T(8,128)S(1)}, u32[]{:S(2)}, u32[]{:S(2)}) collective-permute-start(f32[10,1,8,128]{3,2,0,1:T(8,128)S(1)} %get-tuple-element.81), channel_id=1, source_target_pairs={{0,1},{1,2},{2,3},{3,4},{4,5},{5,6},{6,7},{7,8},{8,9},{9,10},{10,1... | collective-permute-start | bytes 122888 | tf_op jit(solution)/shard_map/ppermute | solution.py:28
  113.3 8.1 %collective-permute-start.6 = (f32[10,1,8,128]{3,2,0,1:T(8,128)S(1)}, f32[10,1,8,128]{3,2,0,1:T(8,128)S(1)}, u32[]{:S(2)}, u32[]{:S(2)}) collective-permute-start(f32[10,1,8,128]{3,2,0,1:T(8,128)S(1)} %get-tuple-element.82), channel_id=1, source_target_pairs={{1,0},{2,1},{3,2},{4,3},{5,4},{6,5},{7,6},{8,7},{9,8},{10,9},{11,1... | collective-permute-start | bytes 122888 | tf_op jit(solution)/shard_map/ppermute | solution.py:31
  121.5 1.6 %collective-permute-done.6 = f32[10,1,8,128]{3,2,0,1:T(8,128)S(1)} collective-permute-done((f32[10,1,8,128]{3,2,0,1:T(8,128)S(1)}, f32[10,1,8,128]{3,2,0,1:T(8,128)S(1)}, u32[]{:S(2)}, u32[]{:S(2)}) %collective-permute-start.6) | collective-permute-done | bytes 40992 | tf_op jit(solution)/shard_map/ppermute | solution.py:31
  123.1 1.9 %collective-permute-start.8 = (f32[10,4,1,128]{3,2,0,1:T(1,128)S(1)}, f32[10,4,1,128]{3,2,0,1:T(1,128)S(1)}, u32[]{:S(2)}, u32[]{:S(2)}) collective-permute-start(f32[10,4,1,128]{3,2,0,1:T(1,128)S(1)} %get-tuple-element.77), channel_id=1, source_target_pairs={{64,0},{128,64},{192,128},{256,192},{320,256},{384,320},{448,384},... | collective-permute-start | bytes 61448 | tf_op jit(solution)/shard_map/ppermute | solution.py:31
  125.0 2.4 %collective-permute-start.9 = (f32[10,4,1,128]{3,2,0,1:T(1,128)S(1)}, f32[10,4,1,128]{3,2,0,1:T(1,128)S(1)}, u32[]{:S(2)}, u32[]{:S(2)}) collective-permute-start(f32[10,4,1,128]{3,2,0,1:T(1,128)S(1)} %get-tuple-element.78), channel_id=1, source_target_pairs={{0,64},{64,128},{128,192},{192,256},{256,320},{320,384},{384,448},... | collective-permute-start | bytes 61448 | tf_op jit(solution)/shard_map/ppermute | solution.py:28
  127.5 4.9 %collective-permute-done.9 = f32[10,4,1,128]{3,2,0,1:T(1,128)S(1)} collective-permute-done((f32[10,4,1,128]{3,2,0,1:T(1,128)S(1)}, f32[10,4,1,128]{3,2,0,1:T(1,128)S(1)}, u32[]{:S(2)}, u32[]{:S(2)}) %collective-permute-start.9) | collective-permute-done | bytes 20512 | tf_op jit(solution)/shard_map/ppermute | solution.py:28
  (36 shorter events, 8.7 us)
Async XLA Ops:
  6.5 79.5 %reduce-scatter.2.cloned.1.call-start = ((), (), s32[]{:S(2)}) async-start(), calls=%async_computation.1 | async-start | bytes 737280 | tf_op jit(solution)/shard_map/reduce_scatter | solution.py:96
  22.5 17.2 %slice-start = ((f32[10,4,64,128]{3,2,1,0:T(8,128)}), f32[10,2,64,128]{3,2,1,0:T(8,128)S(1)}, s32[]{:S(2)}) async-start(f32[10,4,64,128]{3,2,1,0:T(8,128)} %reshape.93), calls=%async_computation.2 | async-start | bytes 1310720 | tf_op jit(solution)/shard_map/slice | solution.py:93
  23.7 20.9 %collective-permute-start = (f32[10,64,128]{2,1,0:T(8,128)S(1)}, f32[10,64,128]{2,1,0:T(8,128)S(1)}, u32[]{:S(2)}, u32[]{:S(2)}) collective-permute-start(f32[10,64,128]{2,1,0:T(8,128)S(1)} %get-tuple-element.76), channel_id=1, source_target_pairs={{1,0},{2,1},{3,2},{4,3},{5,4},{6,5},{7,6},{8,7},{9,8},{10,9},{11,1... | collective-permute-start | bytes 983048 | tf_op jit(solution)/shard_map/ppermute | solution.py:18
  37.7 7.0 %copy-start = (f32[10,4,64,128]{3,2,1,0:T(8,128)S(1)}, f32[10,4,64,128]{3,2,1,0:T(8,128)}, u32[]{:S(2)}) copy-start(f32[10,4,64,128]{3,2,1,0:T(8,128)} %reshape.93) | copy-start | bytes 3932164
  37.7 15.4 %collective-permute-start.1 = (f32[10,64,128]{2,1,0:T(8,128)S(1)}, f32[10,64,128]{2,1,0:T(8,128)S(1)}, u32[]{:S(2)}, u32[]{:S(2)}) collective-permute-start(f32[10,64,128]{2,1,0:T(8,128)S(1)} %get-tuple-element.75), channel_id=1, source_target_pairs={{63,0},{0,1},{1,2},{2,3},{3,4},{4,5},{5,6},{6,7},{7,8},{8,9},{9,10... | collective-permute-start | bytes 983048 | tf_op jit(solution)/shard_map/ppermute | solution.py:18
  53.2 0.8 copy-start.1
  86.8 10.1 %collective-permute-start.3 = (f32[10,1,8,128]{3,2,0,1:T(8,128)S(1)}, f32[10,1,8,128]{3,2,0,1:T(8,128)S(1)}, u32[]{:S(2)}, u32[]{:S(2)}) collective-permute-start(f32[10,1,8,128]{3,2,0,1:T(8,128)S(1)} %get-tuple-element.84), channel_id=1, source_target_pairs={{0,1},{1,2},{2,3},{3,4},{4,5},{5,6},{6,7},{7,8},{8,9},{9,10},{10,1... | collective-permute-start | bytes 122888 | tf_op jit(solution)/shard_map/ppermute | solution.py:28
  90.4 8.1 %collective-permute-start.2 = (f32[10,1,8,128]{3,2,0,1:T(8,128)S(1)}, f32[10,1,8,128]{3,2,0,1:T(8,128)S(1)}, u32[]{:S(2)}, u32[]{:S(2)}) collective-permute-start(f32[10,1,8,128]{3,2,0,1:T(8,128)S(1)} %get-tuple-element.83), channel_id=1, source_target_pairs={{1,0},{2,1},{3,2},{4,3},{5,4},{6,5},{7,6},{8,7},{9,8},{10,9},{11,1... | collective-permute-start | bytes 122888 | tf_op jit(solution)/shard_map/ppermute | solution.py:31
  98.5 6.1 %collective-permute-start.4 = (f32[10,4,1,128]{3,2,0,1:T(1,128)S(1)}, f32[10,4,1,128]{3,2,0,1:T(1,128)S(1)}, u32[]{:S(2)}, u32[]{:S(2)}) collective-permute-start(f32[10,4,1,128]{3,2,0,1:T(1,128)S(1)} %get-tuple-element.79), channel_id=1, source_target_pairs={{64,0},{128,64},{192,128},{256,192},{320,256},{384,320},{448,384},... | collective-permute-start | bytes 61448 | tf_op jit(solution)/shard_map/ppermute | solution.py:31
  102.7 7.4 %collective-permute-start.5 = (f32[10,4,1,128]{3,2,0,1:T(1,128)S(1)}, f32[10,4,1,128]{3,2,0,1:T(1,128)S(1)}, u32[]{:S(2)}, u32[]{:S(2)}) collective-permute-start(f32[10,4,1,128]{3,2,0,1:T(1,128)S(1)} %get-tuple-element.80), channel_id=1, source_target_pairs={{0,64},{64,128},{128,192},{192,256},{256,320},{320,384},{384,448},... | collective-permute-start | bytes 61448 | tf_op jit(solution)/shard_map/ppermute | solution.py:28
  111.4 10.1 %collective-permute-start.7 = (f32[10,1,8,128]{3,2,0,1:T(8,128)S(1)}, f32[10,1,8,128]{3,2,0,1:T(8,128)S(1)}, u32[]{:S(2)}, u32[]{:S(2)}) collective-permute-start(f32[10,1,8,128]{3,2,0,1:T(8,128)S(1)} %get-tuple-element.81), channel_id=1, source_target_pairs={{0,1},{1,2},{2,3},{3,4},{4,5},{5,6},{6,7},{7,8},{8,9},{9,10},{10,1... | collective-permute-start | bytes 122888 | tf_op jit(solution)/shard_map/ppermute | solution.py:28
  113.3 9.8 %collective-permute-start.6 = (f32[10,1,8,128]{3,2,0,1:T(8,128)S(1)}, f32[10,1,8,128]{3,2,0,1:T(8,128)S(1)}, u32[]{:S(2)}, u32[]{:S(2)}) collective-permute-start(f32[10,1,8,128]{3,2,0,1:T(8,128)S(1)} %get-tuple-element.82), channel_id=1, source_target_pairs={{1,0},{2,1},{3,2},{4,3},{5,4},{6,5},{7,6},{8,7},{9,8},{10,9},{11,1... | collective-permute-start | bytes 122888 | tf_op jit(solution)/shard_map/ppermute | solution.py:31
  123.1 4.3 %collective-permute-start.8 = (f32[10,4,1,128]{3,2,0,1:T(1,128)S(1)}, f32[10,4,1,128]{3,2,0,1:T(1,128)S(1)}, u32[]{:S(2)}, u32[]{:S(2)}) collective-permute-start(f32[10,4,1,128]{3,2,0,1:T(1,128)S(1)} %get-tuple-element.77), channel_id=1, source_target_pairs={{64,0},{128,64},{192,128},{256,192},{320,256},{384,320},{448,384},... | collective-permute-start | bytes 61448 | tf_op jit(solution)/shard_map/ppermute | solution.py:31
  125.0 7.4 %collective-permute-start.9 = (f32[10,4,1,128]{3,2,0,1:T(1,128)S(1)}, f32[10,4,1,128]{3,2,0,1:T(1,128)S(1)}, u32[]{:S(2)}, u32[]{:S(2)}) collective-permute-start(f32[10,4,1,128]{3,2,0,1:T(1,128)S(1)} %get-tuple-element.78), channel_id=1, source_target_pairs={{0,64},{64,128},{128,192},{192,256},{256,320},{320,384},{384,448},... | collective-permute-start | bytes 61448 | tf_op jit(solution)/shard_map/ppermute | solution.py:28
Sparse Core Ops, SparseCore 0:
  54.2 31.7 reduce-scatter.1
where the time goes:
time: 141 us; the launch traced here: 140 us
  waiting for transfers between devices  58 us (41%)
  starting transfers between devices  46.5 us (33%)
  between operations  14.3 us (10%)
  local copies, waits for them, and re-layouts  14.2 us (10%)
  other arithmetic  4.87 us (3%)
  matrix products  2.11 us (1%)
    reduce_scatter x1, waiting for transfers between devices, local(): owned = lax.psum_scatter(summed, 'dom', scatter_dimension=2, tiled=True)  31.9 us
    ppermute x4, starting transfers between devices, extended_2(): lax.ppermute(lax.slice_in_dim(block, 0, width, axis=dim), axis, backward)  20.7 us
    ppermute x2, starting transfers between devices, passed_along(): return lax.ppermute(block, axis, route)  16 us
    ppermute x2, waiting for transfers between devices, passed_along(): return lax.ppermute(block, axis, route)  13.2 us
    ppermute x4, waiting for transfers between devices, extended_2(): lax.ppermute(lax.slice_in_dim(block, block.shape[dim] - width, None, axis...  10.5 us
    ppermute x4, starting transfers between devices, extended_2(): lax.ppermute(lax.slice_in_dim(block, block.shape[dim] - width, None, axis...  9.82 us
    transpose x1, local copies, waits for them, and re-layouts, local(): extended.transpose(3, 0, 1, 2, 4)  3.54 us
  transfers between devices with their start and end apart: 11, of which 7 were waited for; matrix products, arithmetic and copies ran while one was open for 1% of the time, Pallas kernels for 0%

commit v1 on v0

v1 whole, which is shorter than its diff:
```python
import jax
import jax.numpy as jnp
from jax import lax
from jax.experimental import pallas as pl
from jax.experimental.pallas import tpu as pltpu
from jax.sharding import PartitionSpec as P

MOM = 10
BLK = 32
TC = 64
NZ = 128
NY = 64
RY = 8
CHIP_ROWS = 2 * RY
HALO = 4
WIN = CHIP_ROWS + 2 * HALO
PLANES = 4
ROWS = 80
COLS = MOM * TC
diffusion = 0.16
keep_weight = 1.0 - 6.0 * diffusion


def iota(shape, dim):
    return lax.broadcasted_iota(jnp.int32, shape, dim)


def terms_kernel(place_ref, count_ref, tile_ref, slab_ref, weight_ref, moment_ref, out_ref, term_ref):
    my_slab, my_dom, n_slabs = place_ref[0], place_ref[1], place_ref[2]
    for b in range(BLK):
        w = weight_ref[b]
        both = jnp.concatenate([w, w], axis=0)
        term_ref[pl.ds(16 * b, MOM), :] = lax.dot_general(
            moment_ref[b], both, (((1,), (1,)), ((), ())), preferred_element_type=jnp.float32
        )
    low_half = iota((BLK, NZ), 1) < TC
    for j in range(MOM // 2):
        even = term_ref[pl.ds(2 * j, BLK, stride=16), :]
        odd = term_ref[pl.ds(2 * j + 1, BLK, stride=16), :]
        term = jnp.where(low_half, even, odd)
        high = term.astype(jnp.bfloat16)
        low = (term - high.astype(jnp.float32)).astype(jnp.bfloat16)
        out_ref[0:BLK, NZ * j : NZ * (j + 1)] = high
        out_ref[BLK : 2 * BLK, NZ * j : NZ * (j + 1)] = low
    tile, slab = tile_ref[...], slab_ref[...]
    step = slab - my_slab
    step = jnp.where(step == n_slabs - 1, -1, jnp.where(step == 1 - n_slabs, 1, step))
    plane = 1 + lax.shift_right_logical(tile, 7) + 2 * step
    row = lax.shift_right_logical(tile & 127, 1)
    used = iota((1, BLK), 1) < count_ref[0, 0]
    code = jnp.where(used, plane * NY + row + 1, 0).astype(jnp.float32).astype(jnp.bfloat16)
    half = (tile & 1).astype(jnp.float32).astype(jnp.bfloat16)
    slot = iota((BLK, COLS), 0)
    lane = iota((BLK, COLS), 1) - my_dom * ROWS
    spread = jnp.where((lane == slot) | (lane == slot + BLK), 1.0, 0.0).astype(jnp.bfloat16)
    code_row = jnp.dot(code, spread, preferred_element_type=jnp.float32)
    half_row = jnp.dot(half, spread, preferred_element_type=jnp.float32)
    sub = iota((ROWS - 2 * BLK, COLS), 0)
    codes = jnp.where(sub == 0, code_row, jnp.where(sub == 1, half_row, 0.0))
    out_ref[2 * BLK : ROWS, :] = codes.astype(jnp.bfloat16)


def field_kernel(place_ref, x_ref, first_ref, second_ref, own_ref, part_ref):
    my_slab, my_dom = place_ref[0], place_ref[1]
    core = lax.rem(my_dom, 2)
    top_row = (my_dom - core) * RY
    codes = x_ref[2 * BLK : ROWS, :].astype(jnp.float32)
    for k in range(1, 8):
        codes += x_ref[ROWS * k + 2 * BLK : ROWS * (k + 1), :].astype(jnp.float32)
    code = codes[0:1, :].astype(jnp.int32) - 1
    half = codes[1:2, :].astype(jnp.int32)
    plane = lax.shift_right_arithmetic(code, 6)
    rel = (code & (NY - 1)) - top_row
    valid = (code >= 0) & (rel >= -HALO) & (rel < CHIP_ROWS + HALO)
    spot = (half * PLANES + plane) * WIN + jnp.where(rel < 0, rel + WIN, rel)
    spot = jnp.where(valid, spot, -1)
    chosen = jnp.where(iota((2 * PLANES * WIN, COLS), 0) == spot, 1.0, 0.0).astype(jnp.bfloat16)
    cells = jnp.dot(chosen, x_ref[...], preferred_element_type=jnp.float32)

    lane = iota((WIN, NZ), 1)
    ring = iota((WIN, NZ), 0)
    at_row = top_row + jnp.where(ring < CHIP_ROWS + HALO, ring, ring - WIN)
    inside = (at_row >= 0) & (at_row < NY)

    def in_plane(f):
        z = jnp.where(lane == 0, 0.0, pltpu.roll(f, 1, 1)) + jnp.where(
            lane == NZ - 1, 0.0, pltpu.roll(f, NZ - 1, 1)
        )
        y = pltpu.roll(f, 1, 0) + pltpu.roll(f, WIN - 1, 0)
        return keep_weight * f + diffusion * (y + z)

    def filter_pass(planes):
        n = len(planes)
        out = []
        for i in range(-1, n + 1):
            value = in_plane(planes[i]) if 0 <= i < n else None
            for k in (i - 1, i + 1):
                if 0 <= k < n:
                    side = diffusion * planes[k]
                    value = side if value is None else value + side
            out.append(value)
        return out

    half_rows = PLANES * WIN
    for m in range(MOM):
        chunk = slice(NZ * (m // 2), NZ * (m // 2 + 1))
        planes = []
        for q in range(PLANES):
            lower = cells[WIN * q : WIN * (q + 1), chunk]
            upper = cells[half_rows + WIN * q : half_rows + WIN * (q + 1), chunk]
            if m % 2 == 0:
                upper = pltpu.roll(upper, TC, 1)
            else:
                lower = pltpu.roll(lower, TC, 1)
            planes.append(jnp.where(lane < TC, lower, upper))
        once = [jnp.where(inside, f, 0.0) for f in filter_pass(planes)]
        for i, f in enumerate(filter_pass(once)):
            part_ref[i, m, 0] = f[0:RY]
            part_ref[i, m, 1] = f[RY : 2 * RY]
    part_ref[8] = jnp.zeros((MOM, 2, RY, NZ), jnp.float32)

    for ref, odd_up in ((first_ref, 1), (second_ref, 0)):
        near_up = lax.rem(my_slab, 2) == odd_up
        far_up = lax.rem(lax.div(my_slab, 2), 2) == odd_up
        near = jnp.where(near_up, 5, 1)
        a = jnp.where(core == 1, near, jnp.where(far_up, 7, 8))
        b = jnp.where(core == 1, near + 1, jnp.where(far_up, 8, 0))
        for p, i in ((0, a), (1, b)):
            for h in range(2):
                ref[h, :, p] = part_ref[i, :, h]
    for p in range(2):
        own_ref[:, p] = part_ref[3 + p, :, core]


def swap_pairs(n_slabs, n_doms, odd_up):
    pairs = []
    for s in range(n_slabs):
        for d in range(n_doms):
            if d % 2 == 1:
                t = s + 1 if s % 2 == odd_up else s - 1
            else:
                t = s + 2 if (s // 2) % 2 == odd_up else s - 2
            pairs.append((d * n_slabs + s, d * n_slabs + t % n_slabs))
    return pairs


def local(weights, moments, block_tile, block_slab, block_count):
    n_slabs = lax.axis_size("slab")
    n_doms = lax.axis_size("dom")
    my_dom = lax.axis_index("dom")
    place = jnp.stack([lax.axis_index("slab"), my_dom, jnp.int32(n_slabs)]).astype(jnp.int32)
    smem = pl.BlockSpec(memory_space=pltpu.SMEM)
    vmem = pl.BlockSpec(memory_space=pltpu.VMEM)
    x = pl.pallas_call(
        terms_kernel,
        out_shape=jax.ShapeDtypeStruct((ROWS, COLS), jnp.bfloat16),
        in_specs=[smem, smem, vmem, vmem, vmem, vmem],
        out_specs=vmem,
        scratch_shapes=[pltpu.VMEM((16 * BLK, NZ), jnp.float32)],
        name="terms",
    )(place, block_count, block_tile, block_slab, weights[0], moments[0])
    gathered = lax.all_gather(x, "dom", tiled=True)
    message = jax.ShapeDtypeStruct((2, MOM, 2, RY, NZ), jnp.float32)
    first, second, own = pl.pallas_call(
        field_kernel,
        out_shape=(message, message, jax.ShapeDtypeStruct((MOM, 2, RY, NZ), jnp.float32)),
        in_specs=[smem, vmem],
        out_specs=(vmem, vmem, vmem),
        scratch_shapes=[pltpu.VMEM((9, MOM, 2, RY, NZ), jnp.float32)],
        name="field",
    )(place, gathered)
    first = lax.ppermute(first, ("dom", "slab"), swap_pairs(n_slabs, n_doms, 1))
    second = lax.ppermute(second, ("dom", "slab"), swap_pairs(n_slabs, n_doms, 0))
    arrived = first + second
    core = lax.rem(my_dom, 2)
    mine = lax.dynamic_index_in_dim(arrived, core, 0, keepdims=False) + own
    other = lax.dynamic_index_in_dim(arrived, 1 - core, 0, keepdims=False)
    other = lax.ppermute(other, "dom", [(i, i ^ 1) for i in range(n_doms)])
    return mine + other


def solution(mesh):
    return jax.shard_map(
        local,
        mesh=mesh,
        in_specs=(
            P("slab", "dom", None, None),
            P("slab", "dom", None, None),
            P("slab", "dom"),
            P("slab", "dom"),
            P("slab", "dom"),
        ),
        out_specs=P(None, "slab", "dom", None),
        check_vma=False,
    )
```

time: 141 us -> 56.4 us (0.40)
  the two profiles are of different devices: /device:TPU:40 before, /device:TPU:1 now
where the time goes in v1:
time: 56.4 us; the launch traced here: 56.1 us
  blocking collectives  23.6 us (42%)
  starting transfers between devices  16.2 us (29%)
  waiting for transfers between devices  7.01 us (12%)
  Pallas kernels  5.71 us (10%)
  local copies, waits for them, and re-layouts  1.6 us (3%)
  other arithmetic  1.25 us (2%)
  between operations  0.71 us (1%)
    all_gather x1, blocking collectives, local(): gathered = lax.all_gather(x, 'dom', tiled=True)  23.6 us
    ppermute x1, starting transfers between devices, local(): first = lax.ppermute(first, ('dom', 'slab'), swap_pairs(n_slabs, n_doms, 1))  10.9 us
    ppermute x1, starting transfers between devices, local(): other = lax.ppermute(other, 'dom', [(i, i ^ 1) for i in range(n_doms)])  3.47 us
    pallas_call x1, Pallas kernels, local(): pl.pallas_call(field_kernel, out_shape=(message, message, jax.ShapeDtypeS...  3.28 us
    ppermute x1, waiting for transfers between devices, local(): lax.ppermute(second, ('dom', 'slab'), swap_pairs(n_slabs, n_doms, 0))  3.25 us
    ppermute x1, waiting for transfers between devices, local(): first = lax.ppermute(first, ('dom', 'slab'), swap_pairs(n_slabs, n_doms, 1))  2.86 us
    pallas_call x1, Pallas kernels, local(): pl.pallas_call(terms_kernel, out_shape=jax.ShapeDtypeStruct((ROWS, COLS),...  2.43 us
    ppermute x1, starting transfers between devices, local(): lax.ppermute(second, ('dom', 'slab'), swap_pairs(n_slabs, n_doms, 0))  1.92 us
  transfers between devices with their start and end apart: 3, of which 3 were waited for; matrix products, arithmetic and copies ran while one was open for 0% of the time, Pallas kernels for 0%

profile of v1, /device:TPU:1, one launch (start us, length us, event | category | flops | bytes accessed | tf_op | source)
XLA Modules:
  0.0 56.1 jit_solution(15048568931831490615)
XLA Ops:
  0.7 1.6 %copy.8 = bf16[1,32,10,128]{3,2,1,0:T(8,128)(2,1)} copy(bf16[1,32,10,128]{3,1,2,0:T(8,128)(2,1)} %param.6) | data formatting | bytes 163840 | tf_op args[1]
  2.2 0.6 %pad_add_fusion.place_ref = s32[3]{0:T(128)} fusion(s32[1]{0:T(128)} %constant.21.clone.1, s32[1]{0:T(128)} %bitcast.1, s32[1]{0:T(128)} %bitcast), kind=kLoop, calls=%fused_computation.4 | loop fusion | flops 6 | bytes 24 | tf_op jit(solution)/shard_map/stack | solution.py:151
  2.8 2.4 %terms.1 = bf16[80,640]{1,0:T(8,128)(2,1)} custom-call(s32[3]{0:T(128)} %pad_add_fusion.place_ref, s32[1,1]{1,0:T(1,128)S(6)} %copy.9.count_ref, s32[1,32]{1,0:T(1,128)} %tile_ref.1, s32[1,32]{1,0:T(1,128)} %slab_ref.1, bf16[32,64,128]{2,1,0:T(8,128)(2,1)} %bitcast.12, bf16[32,10,128]{2,1,0:T(8,128)(2,1)} %bitcast.13), custom_call_target="tpu_custom_call" | custom-call | tf_op jit(solution)/shard_map/terms/pallas_call | solution.py:154
  5.2 23.6 %all_gather.3.x_ref = bf16[640,640]{1,0:T(8,128)(2,1)} all-gather(bf16[80,640]{1,0:T(8,128)(2,1)} %terms.1), channel_id=1, replica_groups=mesh['dom'=8,'slab'=64] {'dom'}, dimensions={0}, use_global_device_ids=true | all-gather | bytes 921600 | tf_op jit(solution)/shard_map/all_gather | solution.py:162
  28.9 3.3 %field.1 = (f32[2,10,2,8,128]{4,3,2,1,0:T(8,128)}, f32[2,10,2,8,128]{4,3,2,1,0:T(8,128)}, f32[10,2,8,128]{3,2,1,0:T(8,128)}) custom-call(s32[3]{0:T(128)} %pad_add_fusion.place_ref, bf16[640,640]{1,0:T(8,128)(2,1)} %all_gather.3.x_ref), custom_call_target="tpu_custom_call" | custom-call | tf_op jit(solution)/shard_map/field/pallas_call | solution.py:164
  32.1 10.9 %collective-permute-start = (f32[2,10,2,8,128]{4,3,2,1,0:T(8,128)}, f32[2,10,2,8,128]{4,3,2,1,0:T(8,128)S(1)}, u32[]{:S(2)}, u32[]{:S(2)}) collective-permute-start(f32[2,10,2,8,128]{4,3,2,1,0:T(8,128)} %get-tuple-element.8), channel_id=1, source_target_pairs={{0,62},{64,127},{128,190},{192,255},{256,318},{320,383},{384,446},... | collective-permute-start | bytes 491528 | tf_op jit(solution)/shard_map/ppermute | solution.py:172
  43.0 1.9 %collective-permute-start.1 = (f32[2,10,2,8,128]{4,3,2,1,0:T(8,128)}, f32[2,10,2,8,128]{4,3,2,1,0:T(8,128)S(1)}, u32[]{:S(2)}, u32[]{:S(2)}) collective-permute-start(f32[2,10,2,8,128]{4,3,2,1,0:T(8,128)} %get-tuple-element.9), channel_id=1, source_target_pairs={{0,2},{64,65},{128,130},{192,193},{256,258},{320,321},{384,386},{4... | collective-permute-start | bytes 491528 | tf_op jit(solution)/shard_map/ppermute | solution.py:173
  44.9 2.9 %collective-permute-done = f32[2,10,2,8,128]{4,3,2,1,0:T(8,128)S(1)} collective-permute-done((f32[2,10,2,8,128]{4,3,2,1,0:T(8,128)}, f32[2,10,2,8,128]{4,3,2,1,0:T(8,128)S(1)}, u32[]{:S(2)}, u32[]{:S(2)}) %collective-permute-start) | collective-permute-done | bytes 163872 | tf_op jit(solution)/shard_map/ppermute | solution.py:172
  47.8 3.3 %collective-permute-done.1 = f32[2,10,2,8,128]{4,3,2,1,0:T(8,128)S(1)} collective-permute-done((f32[2,10,2,8,128]{4,3,2,1,0:T(8,128)}, f32[2,10,2,8,128]{4,3,2,1,0:T(8,128)S(1)}, u32[]{:S(2)}, u32[]{:S(2)}) %collective-permute-start.1) | collective-permute-done | bytes 163872 | tf_op jit(solution)/shard_map/ppermute | solution.py:173
  51.1 0.0 copy-start
  51.1 3.5 %collective-permute-start.2 = (f32[10,2,8,128]{3,2,1,0:T(8,128)S(1)}, f32[10,2,8,128]{3,2,1,0:T(8,128)S(1)}, u32[]{:S(2)}, u32[]{:S(2)}) collective-permute-start(f32[10,2,8,128]{3,2,1,0:T(8,128)S(1)} %dynamic-slice_bitcast_fusion), channel_id=1, source_target_pairs={{0,64},{64,0},{128,192},{192,128},{256,320},{320,256},{384,448},{4... | collective-permute-start | bytes 245768 | tf_op jit(solution)/shard_map/ppermute | solution.py:178
  54.6 0.9 %collective-permute-done.2 = f32[10,2,8,128]{3,2,1,0:T(8,128)S(1)} collective-permute-done((f32[10,2,8,128]{3,2,1,0:T(8,128)S(1)}, f32[10,2,8,128]{3,2,1,0:T(8,128)S(1)}, u32[]{:S(2)}, u32[]{:S(2)}) %collective-permute-start.2) | collective-permute-done | bytes 81952 | tf_op jit(solution)/shard_map/ppermute | solution.py:178
  55.5 0.0 copy-done
  55.5 0.6 %fusion = f32[10,2,8,128]{3,2,1,0:T(8,128)} fusion(f32[10,2,8,128]{3,2,1,0:T(8,128)S(1)} %collective-permute-done.2, f32[10,2,8,128]{3,2,1,0:T(8,128)S(1)} %copy-done, f32[2,10,2,8,128]{4,3,2,1,0:T(8,128)S(1)} %add.17, s32[]{:T(128)S(6)} %select_n.7), kind=kLoop, calls=%fused_computation.2 | loop fusion | flops 40960 | bytes 327684 | tf_op jit(solution)/shard_map/add | solution.py:179
  (2 shorter events, 0.0 us)
Async XLA Ops:
  32.1 15.7 %collective-permute-start = (f32[2,10,2,8,128]{4,3,2,1,0:T(8,128)}, f32[2,10,2,8,128]{4,3,2,1,0:T(8,128)S(1)}, u32[]{:S(2)}, u32[]{:S(2)}) collective-permute-start(f32[2,10,2,8,128]{4,3,2,1,0:T(8,128)} %get-tuple-element.8), channel_id=1, source_target_pairs={{0,62},{64,127},{128,190},{192,255},{256,318},{320,383},{384,446},... | collective-permute-start | bytes 491528 | tf_op jit(solution)/shard_map/ppermute | solution.py:172
  43.0 8.0 %collective-permute-start.1 = (f32[2,10,2,8,128]{4,3,2,1,0:T(8,128)}, f32[2,10,2,8,128]{4,3,2,1,0:T(8,128)S(1)}, u32[]{:S(2)}, u32[]{:S(2)}) collective-permute-start(f32[2,10,2,8,128]{4,3,2,1,0:T(8,128)} %get-tuple-element.9), channel_id=1, source_target_pairs={{0,2},{64,65},{128,130},{192,193},{256,258},{320,321},{384,386},{4... | collective-permute-start | bytes 491528 | tf_op jit(solution)/shard_map/ppermute | solution.py:173
  51.1 4.4 %copy-start = (f32[10,2,8,128]{3,2,1,0:T(8,128)S(1)}, f32[10,2,8,128]{3,2,1,0:T(8,128)}, u32[]{:S(2)}) copy-start(f32[10,2,8,128]{3,2,1,0:T(8,128)} %get-tuple-element.10) | copy-start | bytes 245764
  51.1 4.4 %collective-permute-start.2 = (f32[10,2,8,128]{3,2,1,0:T(8,128)S(1)}, f32[10,2,8,128]{3,2,1,0:T(8,128)S(1)}, u32[]{:S(2)}, u32[]{:S(2)}) collective-permute-start(f32[10,2,8,128]{3,2,1,0:T(8,128)S(1)} %dynamic-slice_bitcast_fusion), channel_id=1, source_target_pairs={{0,64},{64,0},{128,192},{192,128},{256,320},{320,256},{384,448},{4... | collective-permute-start | bytes 245768 | tf_op jit(solution)/shard_map/ppermute | solution.py:178

commit v2 on v1

v2 whole, which is shorter than its diff:
```python
import jax
import jax.numpy as jnp
from jax import lax
from jax.experimental import pallas as pl
from jax.experimental.pallas import tpu as pltpu
from jax.sharding import PartitionSpec as P

MOM = 10
BLK = 32
TC = 64
NZ = 128
NY = 64
RY = 8
CHIP_ROWS = 2 * RY
HALO = 4
WIN = CHIP_ROWS + 2 * HALO
PLANES = 4
ROWS = 80
COLS = MOM * TC
CHUNKS = 4
diffusion = 0.16
keep_weight = 1.0 - 6.0 * diffusion


def iota(shape, dim):
    return lax.broadcasted_iota(jnp.int32, shape, dim)


def terms_kernel(count_ref, tile_ref, slab_ref, weight_hbm, moment_ref, out_ref, weight_ref, term_ref, mom_ref, sems):
    my_slab, my_dom, n_slabs = lax.axis_index("slab"), lax.axis_index("dom"), lax.axis_size("slab")
    size = BLK // CHUNKS
    copies = []
    for c in range(CHUNKS):
        part = pl.ds(c * size, size)
        copies.append(pltpu.make_async_copy(weight_hbm.at[part], weight_ref.at[part], sems.at[c]))
        copies[c].start()
    for m in range(MOM):
        mom_ref[BLK * m : BLK * (m + 1), :] = moment_ref[m].astype(jnp.float32)
    tile, slab = tile_ref[...], slab_ref[...]
    step = slab - my_slab
    step = jnp.where(step == n_slabs - 1, -1, jnp.where(step == 1 - n_slabs, 1, step))
    plane = 1 + lax.shift_right_logical(tile, 7) + 2 * step
    row = lax.shift_right_logical(tile & 127, 1)
    used = iota((1, BLK), 1) < count_ref[0, 0]
    code = jnp.where(used, plane * NY + row + 1, 0).astype(jnp.float32)
    half = (tile & 1).astype(jnp.float32)
    both = jnp.where(iota((8, BLK), 0) == 0, code, half).astype(jnp.bfloat16)
    slot = iota((BLK, COLS), 0)
    lane = iota((BLK, COLS), 1) - my_dom * ROWS
    spread = jnp.where((lane == slot) | (lane == slot + BLK), 1.0, 0.0).astype(jnp.bfloat16)
    codes = jnp.dot(both, spread, preferred_element_type=jnp.float32).astype(jnp.bfloat16)
    out_ref[2 * BLK : ROWS, :] = jnp.concatenate([codes, codes], axis=0)
    for b in range(BLK):
        if b % size == 0:
            copies[b // size].wait()
        w = weight_ref[b]
        pair = jnp.concatenate([w, w], axis=0)
        mom = mom_ref[pl.ds(b, MOM, stride=BLK), :].astype(jnp.bfloat16)
        term_ref[pl.ds(16 * b, MOM), :] = lax.dot_general(
            mom, pair, (((1,), (1,)), ((), ())), preferred_element_type=jnp.float32
        )
    low_half = iota((BLK, NZ), 1) < TC
    for j in range(MOM // 2):
        even = term_ref[pl.ds(2 * j, BLK, stride=16), :]
        odd = term_ref[pl.ds(2 * j + 1, BLK, stride=16), :]
        term = jnp.where(low_half, even, odd)
        high = term.astype(jnp.bfloat16)
        low = (term - high.astype(jnp.float32)).astype(jnp.bfloat16)
        out_ref[0:BLK, NZ * j : NZ * (j + 1)] = high
        out_ref[BLK : 2 * BLK, NZ * j : NZ * (j + 1)] = low


def deposit(x_ref, top_row):
    codes = x_ref[2 * BLK : ROWS, :].astype(jnp.float32)
    for k in range(1, 8):
        codes += x_ref[ROWS * k + 2 * BLK : ROWS * (k + 1), :].astype(jnp.float32)
    code = codes[0:1, :].astype(jnp.int32) - 1
    half = codes[1:2, :].astype(jnp.int32)
    plane = lax.shift_right_arithmetic(code, 6)
    rel = (code & (NY - 1)) - top_row
    valid = (code >= 0) & (rel >= -HALO) & (rel < CHIP_ROWS + HALO)
    spot = (half * PLANES + plane) * WIN + jnp.where(rel < 0, rel + WIN, rel)
    spot = jnp.where(valid, spot, -1)
    chosen = jnp.where(iota((2 * PLANES * WIN, COLS), 0) == spot, 1.0, 0.0).astype(jnp.bfloat16)
    return jnp.dot(chosen, x_ref[...], preferred_element_type=jnp.float32)


class Stencil:
    def __init__(self, top_row):
        self.lane = iota((WIN, NZ), 1)
        ring = iota((WIN, NZ), 0)
        at_row = top_row + jnp.where(ring < CHIP_ROWS + HALO, ring, ring - WIN)
        self.inside = (at_row >= 0) & (at_row < NY)

    def planes(self, cells, m):
        chunk = slice(NZ * (m // 2), NZ * (m // 2 + 1))
        out = []
        for q in range(PLANES):
            lower = cells[WIN * q : WIN * (q + 1), chunk]
            upper = cells[WIN * (PLANES + q) : WIN * (PLANES + q + 1), chunk]
            if m % 2 == 0:
                upper = pltpu.roll(upper, TC, 1)
            else:
                lower = pltpu.roll(lower, TC, 1)
            out.append(jnp.where(self.lane < TC, lower, upper))
        return out

    def flat(self, f):
        z = jnp.where(self.lane == 0, 0.0, pltpu.roll(f, 1, 1)) + jnp.where(
            self.lane == NZ - 1, 0.0, pltpu.roll(f, NZ - 1, 1)
        )
        y = pltpu.roll(f, 1, 0) + pltpu.roll(f, WIN - 1, 0)
        return keep_weight * f + diffusion * (y + z)

    def kept(self, f):
        return jnp.where(self.inside, f, 0.0)


def send_kernel(x_ref, first_ref, second_ref, part_ref):
    my_slab, my_dom = lax.axis_index("slab"), lax.axis_index("dom")
    core = lax.rem(my_dom, 2)
    top_row = (my_dom - core) * RY
    cells = deposit(x_ref, top_row)
    st = Stencil(top_row)

    def put(i, m, f):
        part_ref[i, m, 0] = f[0:RY]
        part_ref[i, m, 1] = f[RY : 2 * RY]

    for m in range(MOM):
        g = st.planes(cells, m)
        put(0, m, diffusion * diffusion * g[0])
        put(5, m, diffusion * diffusion * g[3])

        def near(g0, g1, g2, i_far, i_near):
            l0 = st.flat(g0)
            once0 = st.kept(l0 + diffusion * g1)
            once1 = st.kept(st.flat(g1) + diffusion * (g0 + g2))
            put(i_far, m, diffusion * (l0 + once0))
            put(i_near, m, st.flat(once0) + diffusion * (diffusion * g0 + once1))

        near(g[0], g[1], g[2], 1, 2)
        near(g[3], g[2], g[1], 4, 3)
    part_ref[6] = jnp.zeros((MOM, 2, RY, NZ), jnp.float32)

    for ref, odd_up in ((first_ref, 1), (second_ref, 0)):
        near_up = lax.rem(my_slab, 2) == odd_up
        far_up = lax.rem(lax.div(my_slab, 2), 2) == odd_up
        at = jnp.where(near_up, 3, 1)
        a = jnp.where(core == 1, at, jnp.where(far_up, 5, 6))
        b = jnp.where(core == 1, at + 1, jnp.where(far_up, 6, 0))
        for p, i in ((0, a), (1, b)):
            for h in range(2):
                ref[h, :, p] = part_ref[i, :, h]


def own_kernel(x_ref, own_ref, part_ref):
    my_dom = lax.axis_index("dom")
    core = lax.rem(my_dom, 2)
    top_row = (my_dom - core) * RY
    cells = deposit(x_ref, top_row)
    st = Stencil(top_row)
    for m in range(MOM):
        g = st.planes(cells, m)
        flats = [st.flat(f) for f in g]
        once = [st.kept(flats[0] + diffusion * g[1])]
        once.append(st.kept(flats[1] + diffusion * (g[0] + g[2])))
        once.append(st.kept(flats[2] + diffusion * (g[1] + g[3])))
        once.append(st.kept(flats[3] + diffusion * g[2]))
        for p in range(2):
            f = st.flat(once[1 + p]) + diffusion * (once[p] + once[2 + p])
            part_ref[m, p, 0] = f[0:RY]
            part_ref[m, p, 1] = f[RY : 2 * RY]
    own_ref[...] = part_ref[:, :, core]


def swap_pairs(n_slabs, n_doms, odd_up):
    pairs = []
    for s in range(n_slabs):
        for d in range(n_doms):
            if d % 2 == 1:
                t = s + 1 if s % 2 == odd_up else s - 1
            else:
                t = s + 2 if (s // 2) % 2 == odd_up else s - 2
            pairs.append((d * n_slabs + s, d * n_slabs + t % n_slabs))
    return pairs


smem = pl.BlockSpec(memory_space=pltpu.SMEM)
vmem = pl.BlockSpec(memory_space=pltpu.VMEM)
anywhere = pl.BlockSpec(memory_space=pl.ANY)


def make_terms(weights, moments, block_tile, block_slab, block_count):
    return pl.pallas_call(
        terms_kernel,
        out_shape=jax.ShapeDtypeStruct((ROWS, COLS), jnp.bfloat16),
        in_specs=[smem, vmem, vmem, anywhere, vmem],
        out_specs=vmem,
        scratch_shapes=[
            pltpu.VMEM((BLK, TC, NZ), jnp.bfloat16),
            pltpu.VMEM((16 * BLK, NZ), jnp.float32),
            pltpu.VMEM((MOM * BLK, NZ), jnp.float32),
            pltpu.SemaphoreType.DMA((CHUNKS,)),
        ],
        name="terms",
    )(block_count, block_tile, block_slab, weights[0], moments[0].transpose(1, 0, 2))


def make_send(gathered):
    message = jax.ShapeDtypeStruct((2, MOM, 2, RY, NZ), jnp.float32)
    return pl.pallas_call(
        send_kernel,
        out_shape=(message, message),
        in_specs=[vmem],
        out_specs=(vmem, vmem),
        scratch_shapes=[pltpu.VMEM((7, MOM, 2, RY, NZ), jnp.float32)],
        name="send",
    )(gathered)


def make_own(gathered):
    return pl.pallas_call(
        own_kernel,
        out_shape=jax.ShapeDtypeStruct((MOM, 2, RY, NZ), jnp.float32),
        in_specs=[vmem],
        out_specs=vmem,
        scratch_shapes=[pltpu.VMEM((MOM, 2, 2, RY, NZ), jnp.float32)],
        cost_estimate=pl.CostEstimate(flops=400_000_000, bytes_accessed=8_000_000, transcendentals=0),
        name="own",
    )(gathered)


def local(weights, moments, block_tile, block_slab, block_count):
    n_slabs = lax.axis_size("slab")
    n_doms = lax.axis_size("dom")
    core = lax.rem(lax.axis_index("dom"), 2)
    x = make_terms(weights, moments, block_tile, block_slab, block_count)
    gathered = lax.all_gather(x, "dom", tiled=True)
    first, second = make_send(gathered)
    first = lax.ppermute(first, ("dom", "slab"), swap_pairs(n_slabs, n_doms, 1))
    second = lax.ppermute(second, ("dom", "slab"), swap_pairs(n_slabs, n_doms, 0))
    own = make_own(gathered)
    first, second, own = lax.optimization_barrier((first, second, own))
    arrived = first + second
    mine = lax.dynamic_index_in_dim(arrived, core, 0, keepdims=False) + own
    other = lax.dynamic_index_in_dim(arrived, 1 - core, 0, keepdims=False)
    other = lax.ppermute(other, "dom", [(i, i ^ 1) for i in range(n_doms)])
    return mine + other


def solution(mesh):
    return jax.shard_map(
        local,
        mesh=mesh,
        in_specs=(
            P("slab", "dom", None, None),
            P("slab", "dom", None, None),
            P("slab", "dom"),
            P("slab", "dom"),
            P("slab", "dom"),
        ),
        out_specs=P(None, "slab", "dom", None),
        check_vma=False,
    )
```

time: 56.4 us -> 54.9 us (0.973)
  Pallas kernels: 5.71 us -> 8.92 us
  waiting for transfers between devices: 7.01 us -> 4.38 us
  local copies, waits for them, and re-layouts: 1.6 us -> 0.02 us
  other arithmetic: 1.25 us -> 0.67 us
    pallas_call x2 -> x3, Pallas kernels: 5.71 us -> 8.92 us  [the longest x1 3.52 us: make_terms(): pl.pallas_call(terms_kernel, out_shape=jax.ShapeDtypeStruct((ROWS, COLS),...]
    ppermute x1, waiting for transfers between devices: 2.86 us -> 0.22 us  [local(): first = lax.ppermute(first, ('dom', 'slab'), swap_pairs(n_slabs, n_doms, 1))]
    unnamed x3 -> x2, local copies, waits for them, and re-layouts: 1.58 us -> 0.01 us
    another operation x1 -> x0, other arithmetic: 0.58 us -> none  [local(): jnp.stack([lax.axis_index('slab'), my_dom, jnp.int32(n_slabs)])]
  transfers between devices with their start and end apart: 3 -> 3, of which waited for: 3 -> 3; matrix products, arithmetic and copies ran while one was open for 0% -> 0% of each run, Pallas kernels for 0% -> 5%
where the time goes in v2:
time: 54.9 us; the launch traced here: 54.6 us
  blocking collectives  23.6 us (43%)
  starting transfers between devices  16.3 us (30%)
  Pallas kernels  8.92 us (16%)
  waiting for transfers between devices  4.38 us (8%)
  between operations  0.72 us (1%)
  other arithmetic  0.67 us (1%)
    all_gather x1, blocking collectives, local(): gathered = lax.all_gather(x, 'dom', tiled=True)  23.6 us
    ppermute x1, starting transfers between devices, local(): first = lax.ppermute(first, ('dom', 'slab'), swap_pairs(n_slabs, n_doms, 1))  10.9 us
    pallas_call x1, Pallas kernels, make_terms(): pl.pallas_call(terms_kernel, out_shape=jax.ShapeDtypeStruct((ROWS, COLS),...  3.52 us
    ppermute x1, starting transfers between devices, local(): other = lax.ppermute(other, 'dom', [(i, i ^ 1) for i in range(n_doms)])  3.47 us
    ppermute x1, waiting for transfers between devices, local(): lax.ppermute(second, ('dom', 'slab'), swap_pairs(n_slabs, n_doms, 0))  3.26 us
    pallas_call x1, Pallas kernels, make_send(): pl.pallas_call(send_kernel, out_shape=(message, message), in_specs=[vmem]...  2.76 us
    pallas_call x1, Pallas kernels, make_own(): pl.pallas_call(own_kernel, out_shape=jax.ShapeDtypeStruct((MOM, 2, RY, NZ...  2.64 us
    ppermute x1, starting transfers between devices, local(): lax.ppermute(second, ('dom', 'slab'), swap_pairs(n_slabs, n_doms, 0))  1.92 us
  transfers between devices with their start and end apart: 3, of which 3 were waited for; matrix products, arithmetic and copies ran while one was open for 0% of the time, Pallas kernels for 5%

profile of v2, /device:TPU:1, one launch (start us, length us, event | category | flops | bytes accessed | tf_op | source)
XLA Modules:
  0.0 54.6 jit_solution(14454272980806963585)
XLA Ops:
  0.7 3.5 %terms.1 = bf16[80,640]{1,0:T(8,128)(2,1)} custom-call(s32[1,1]{1,0:T(1,128)S(6)} %copy.6.count_ref, s32[1,32]{1,0:T(1,128)} %tile_ref.1, s32[1,32]{1,0:T(1,128)} %slab_ref.1, bf16[32,64,128]{2,1,0:T(8,128)(2,1)} %bitcast.10, bf16[10,32,128]{2,1,0:T(8,128)(2,1)} %bitcast.11), custom_call_target="tpu_custom_call" | custom-call | tf_op jit(solution)/shard_map/terms/pallas_call | solution.py:195
  4.2 23.6 %all_gather.3.x_ref = bf16[640,640]{1,0:T(8,128)(2,1)} all-gather(bf16[80,640]{1,0:T(8,128)(2,1)} %terms.1), channel_id=1, replica_groups=mesh['dom'=8,'slab'=64] {'dom'}, dimensions={0}, use_global_device_ids=true | all-gather | bytes 921600 | tf_op jit(solution)/shard_map/all_gather | solution.py:239
  27.8 2.8 %send.1 = (f32[2,10,2,8,128]{4,3,2,1,0:T(8,128)}, f32[2,10,2,8,128]{4,3,2,1,0:T(8,128)}) custom-call(bf16[640,640]{1,0:T(8,128)(2,1)} %all_gather.3.x_ref), custom_call_target="tpu_custom_call" | custom-call | tf_op jit(solution)/shard_map/send/pallas_call | solution.py:212
  30.6 10.9 %collective-permute-start = (f32[2,10,2,8,128]{4,3,2,1,0:T(8,128)}, f32[2,10,2,8,128]{4,3,2,1,0:T(8,128)S(1)}, u32[]{:S(2)}, u32[]{:S(2)}) collective-permute-start(f32[2,10,2,8,128]{4,3,2,1,0:T(8,128)} %get-tuple-element.10), channel_id=1, source_target_pairs={{0,62},{64,127},{128,190},{192,255},{256,318},{320,383},{384,446},... | collective-permute-start | bytes 491528 | tf_op jit(solution)/shard_map/ppermute | solution.py:241
  41.4 1.9 %collective-permute-start.1 = (f32[2,10,2,8,128]{4,3,2,1,0:T(8,128)}, f32[2,10,2,8,128]{4,3,2,1,0:T(8,128)S(1)}, u32[]{:S(2)}, u32[]{:S(2)}) collective-permute-start(f32[2,10,2,8,128]{4,3,2,1,0:T(8,128)} %get-tuple-element.11), channel_id=1, source_target_pairs={{0,2},{64,65},{128,130},{192,193},{256,258},{320,321},{384,386},{4... | collective-permute-start | bytes 491528 | tf_op jit(solution)/shard_map/ppermute | solution.py:242
  43.4 2.6 %own.1 = f32[10,2,8,128]{3,2,1,0:T(8,128)} custom-call(bf16[640,640]{1,0:T(8,128)(2,1)} %all_gather.3.x_ref), custom_call_target="tpu_custom_call" | custom-call | flops 400000000 | bytes 8000000 | tf_op jit(solution)/shard_map/own/pallas_call | solution.py:223
  46.0 0.2 collective-permute-done
  46.2 3.3 %collective-permute-done.1 = f32[2,10,2,8,128]{4,3,2,1,0:T(8,128)S(1)} collective-permute-done((f32[2,10,2,8,128]{4,3,2,1,0:T(8,128)}, f32[2,10,2,8,128]{4,3,2,1,0:T(8,128)S(1)}, u32[]{:S(2)}, u32[]{:S(2)}) %collective-permute-start.1) | collective-permute-done | bytes 163872 | tf_op jit(solution)/shard_map/ppermute | solution.py:242
  49.5 0.0 copy-start
  49.6 3.5 %collective-permute-start.2 = (f32[10,2,8,128]{3,2,1,0:T(8,128)S(1)}, f32[10,2,8,128]{3,2,1,0:T(8,128)S(1)}, u32[]{:S(2)}, u32[]{:S(2)}) collective-permute-start(f32[10,2,8,128]{3,2,1,0:T(8,128)S(1)} %dynamic-slice_bitcast_fusion), channel_id=1, source_target_pairs={{0,64},{64,0},{128,192},{192,128},{256,320},{320,256},{384,448},{4... | collective-permute-start | bytes 245768 | tf_op jit(solution)/shard_map/ppermute | solution.py:248
  53.0 0.9 %collective-permute-done.2 = f32[10,2,8,128]{3,2,1,0:T(8,128)S(1)} collective-permute-done((f32[10,2,8,128]{3,2,1,0:T(8,128)S(1)}, f32[10,2,8,128]{3,2,1,0:T(8,128)S(1)}, u32[]{:S(2)}, u32[]{:S(2)}) %collective-permute-start.2) | collective-permute-done | bytes 81952 | tf_op jit(solution)/shard_map/ppermute | solution.py:248
  53.9 0.0 copy-done
  53.9 0.6 %fusion = f32[10,2,8,128]{3,2,1,0:T(8,128)} fusion(f32[10,2,8,128]{3,2,1,0:T(8,128)S(1)} %collective-permute-done.2, f32[10,2,8,128]{3,2,1,0:T(8,128)S(1)} %copy-done, f32[2,10,2,8,128]{4,3,2,1,0:T(8,128)S(1)} %add.17, s32[]{:T(128)S(6)} %select_n.7), kind=kLoop, calls=%fused_computation.1 | loop fusion | flops 40960 | bytes 327684 | tf_op jit(solution)/shard_map/add | solution.py:249
  (2 shorter events, 0.0 us)
Async XLA Ops:
  30.6 15.7 %collective-permute-start = (f32[2,10,2,8,128]{4,3,2,1,0:T(8,128)}, f32[2,10,2,8,128]{4,3,2,1,0:T(8,128)S(1)}, u32[]{:S(2)}, u32[]{:S(2)}) collective-permute-start(f32[2,10,2,8,128]{4,3,2,1,0:T(8,128)} %get-tuple-element.10), channel_id=1, source_target_pairs={{0,62},{64,127},{128,190},{192,255},{256,318},{320,383},{384,446},... | collective-permute-start | bytes 491528 | tf_op jit(solution)/shard_map/ppermute | solution.py:241
  41.4 8.1 %collective-permute-start.1 = (f32[2,10,2,8,128]{4,3,2,1,0:T(8,128)}, f32[2,10,2,8,128]{4,3,2,1,0:T(8,128)S(1)}, u32[]{:S(2)}, u32[]{:S(2)}) collective-permute-start(f32[2,10,2,8,128]{4,3,2,1,0:T(8,128)} %get-tuple-element.11), channel_id=1, source_target_pairs={{0,2},{64,65},{128,130},{192,193},{256,258},{320,321},{384,386},{4... | collective-permute-start | bytes 491528 | tf_op jit(solution)/shard_map/ppermute | solution.py:242
  49.5 4.4 %copy-start = (f32[10,2,8,128]{3,2,1,0:T(8,128)S(1)}, f32[10,2,8,128]{3,2,1,0:T(8,128)}, u32[]{:S(2)}) copy-start(f32[10,2,8,128]{3,2,1,0:T(8,128)} %own.1) | copy-start | bytes 245764
  49.6 4.4 %collective-permute-start.2 = (f32[10,2,8,128]{3,2,1,0:T(8,128)S(1)}, f32[10,2,8,128]{3,2,1,0:T(8,128)S(1)}, u32[]{:S(2)}, u32[]{:S(2)}) collective-permute-start(f32[10,2,8,128]{3,2,1,0:T(8,128)S(1)} %dynamic-slice_bitcast_fusion), channel_id=1, source_target_pairs={{0,64},{64,0},{128,192},{192,128},{256,320},{320,256},{384,448},{4... | collective-permute-start | bytes 245768 | tf_op jit(solution)/shard_map/ppermute | solution.py:248

commit v3 on v2

--- a/solution.py
+++ b/solution.py
@@ -26,14 +26,26 @@
     return lax.broadcasted_iota(jnp.int32, shape, dim)
 
 
-def terms_kernel(count_ref, tile_ref, slab_ref, weight_hbm, moment_ref, out_ref, weight_ref, term_ref, mom_ref, sems):
+def terms_kernel(
+    count_hbm, tile_hbm, slab_hbm, weight_hbm, moment_hbm, out_ref,
+    count_ref, tile_ref, slab_ref, weight_ref, moment_ref, term_ref, mom_ref, sems,
+):
     my_slab, my_dom, n_slabs = lax.axis_index("slab"), lax.axis_index("dom"), lax.axis_size("slab")
     size = BLK // CHUNKS
+    small = [
+        pltpu.make_async_copy(moment_hbm, moment_ref, sems.at[CHUNKS]),
+        pltpu.make_async_copy(tile_hbm, tile_ref, sems.at[CHUNKS + 1]),
+        pltpu.make_async_copy(slab_hbm, slab_ref, sems.at[CHUNKS + 2]),
+        pltpu.make_async_copy(count_hbm, count_ref, sems.at[CHUNKS + 3]),
+    ]
     copies = []
     for c in range(CHUNKS):
         part = pl.ds(c * size, size)
         copies.append(pltpu.make_async_copy(weight_hbm.at[part], weight_ref.at[part], sems.at[c]))
-        copies[c].start()
+    for copy in small + copies:
+        copy.start()
+    for copy in small:
+        copy.wait()
     for m in range(MOM):
         mom_ref[BLK * m : BLK * (m + 1), :] = moment_ref[m].astype(jnp.float32)
     tile, slab = tile_ref[...], slab_ref[...]
@@ -41,7 +53,7 @@
     step = jnp.where(step == n_slabs - 1, -1, jnp.where(step == 1 - n_slabs, 1, step))
     plane = 1 + lax.shift_right_logical(tile, 7) + 2 * step
     row = lax.shift_right_logical(tile & 127, 1)
-    used = iota((1, BLK), 1) < count_ref[0, 0]
+    used = iota((1, BLK), 1) < count_ref[...]
     code = jnp.where(used, plane * NY + row + 1, 0).astype(jnp.float32)
     half = (tile & 1).astype(jnp.float32)
     both = jnp.where(iota((8, BLK), 0) == 0, code, half).astype(jnp.bfloat16)
@@ -116,7 +128,7 @@
         return jnp.where(self.inside, f, 0.0)
 
 
-def send_kernel(x_ref, first_ref, second_ref, part_ref):
+def send_kernel(x_ref, early_ref, outer_ref, late_ref, part_ref):
     my_slab, my_dom = lax.axis_index("slab"), lax.axis_index("dom")
     core = lax.rem(my_dom, 2)
     top_row = (my_dom - core) * RY
@@ -143,7 +155,7 @@
         near(g[3], g[2], g[1], 4, 3)
     part_ref[6] = jnp.zeros((MOM, 2, RY, NZ), jnp.float32)
 
-    for ref, odd_up in ((first_ref, 1), (second_ref, 0)):
+    for refs, odd_up in (((outer_ref,), 1), ((early_ref, late_ref), 0)):
         near_up = lax.rem(my_slab, 2) == odd_up
         far_up = lax.rem(lax.div(my_slab, 2), 2) == odd_up
         at = jnp.where(near_up, 3, 1)
@@ -151,7 +163,8 @@
         b = jnp.where(core == 1, at + 1, jnp.where(far_up, 6, 0))
         for p, i in ((0, a), (1, b)):
             for h in range(2):
-                ref[h, :, p] = part_ref[i, :, h]
+                for ref in refs:
+                    ref[h, :, p] = part_ref[i, :, h]
 
 
 def own_kernel(x_ref, own_ref, part_ref):
@@ -174,10 +187,12 @@
     own_ref[...] = part_ref[:, :, core]
 
 
-def swap_pairs(n_slabs, n_doms, odd_up):
+def swap_pairs(n_slabs, n_doms, odd_up, chosen):
     pairs = []
     for s in range(n_slabs):
         for d in range(n_doms):
+            if not chosen(s):
+                continue
             if d % 2 == 1:
                 t = s + 1 if s % 2 == odd_up else s - 1
             else:
@@ -186,23 +201,29 @@
     return pairs
 
 
-smem = pl.BlockSpec(memory_space=pltpu.SMEM)
+limited = pltpu.CompilerParams(vmem_limit_bytes=16 * 1024 * 1024)
+alone = pltpu.CompilerParams(vmem_limit_bytes=60 * 1024 * 1024)
+hbm = pl.BlockSpec(memory_space=pltpu.HBM)
 vmem = pl.BlockSpec(memory_space=pltpu.VMEM)
-anywhere = pl.BlockSpec(memory_space=pl.ANY)
 
 
 def make_terms(weights, moments, block_tile, block_slab, block_count):
     return pl.pallas_call(
         terms_kernel,
         out_shape=jax.ShapeDtypeStruct((ROWS, COLS), jnp.bfloat16),
-        in_specs=[smem, vmem, vmem, anywhere, vmem],
+        in_specs=[hbm] * 5,
         out_specs=vmem,
         scratch_shapes=[
+            pltpu.VMEM((1, 1), jnp.int32),
+            pltpu.VMEM((1, BLK), jnp.int32),
+            pltpu.VMEM((1, BLK), jnp.int32),
             pltpu.VMEM((BLK, TC, NZ), jnp.bfloat16),
+            pltpu.VMEM((MOM, BLK, NZ), jnp.bfloat16),
             pltpu.VMEM((16 * BLK, NZ), jnp.float32),
             pltpu.VMEM((MOM * BLK, NZ), jnp.float32),
-            pltpu.SemaphoreType.DMA((CHUNKS,)),
+            pltpu.SemaphoreType.DMA((CHUNKS + 4,)),
         ],
+        compiler_params=alone,
         name="terms",
     )(block_count, block_tile, block_slab, weights[0], moments[0].transpose(1, 0, 2))
 
@@ -211,10 +232,11 @@
     message = jax.ShapeDtypeStruct((2, MOM, 2, RY, NZ), jnp.float32)
     return pl.pallas_call(
         send_kernel,
-        out_shape=(message, message),
+        out_shape=(message,) * 3,
         in_specs=[vmem],
-        out_specs=(vmem, vmem),
+        out_specs=(vmem,) * 3,
         scratch_shapes=[pltpu.VMEM((7, MOM, 2, RY, NZ), jnp.float32)],
+        compiler_params=limited,
         name="send",
     )(gathered)
 
@@ -227,6 +249,7 @@
         out_specs=vmem,
         scratch_shapes=[pltpu.VMEM((MOM, 2, 2, RY, NZ), jnp.float32)],
         cost_estimate=pl.CostEstimate(flops=400_000_000, bytes_accessed=8_000_000, transcendentals=0),
+        compiler_params=limited,
         name="own",
     )(gathered)
 
@@ -237,12 +260,15 @@
     core = lax.rem(lax.axis_index("dom"), 2)
     x = make_terms(weights, moments, block_tile, block_slab, block_count)
     gathered = lax.all_gather(x, "dom", tiled=True)
-    first, second = make_send(gathered)
-    first = lax.ppermute(first, ("dom", "slab"), swap_pairs(n_slabs, n_doms, 1))
-    second = lax.ppermute(second, ("dom", "slab"), swap_pairs(n_slabs, n_doms, 0))
+    early, outer, late = make_send(gathered)
+    both = ("dom", "slab")
+    half = lambda low: lambda s: ((s // 4) % 8 < 4) == low
+    early = lax.ppermute(early, both, swap_pairs(n_slabs, n_doms, 0, half(True)))
+    outer = lax.ppermute(outer, both, swap_pairs(n_slabs, n_doms, 1, lambda s: True))
+    late = lax.ppermute(late, both, swap_pairs(n_slabs, n_doms, 0, half(False)))
     own = make_own(gathered)
-    first, second, own = lax.optimization_barrier((first, second, own))
-    arrived = first + second
+    early, outer, late, own = lax.optimization_barrier((early, outer, late, own))
+    arrived = outer + (early + late)
     mine = lax.dynamic_index_in_dim(arrived, core, 0, keepdims=False) + own
     other = lax.dynamic_index_in_dim(arrived, 1 - core, 0, keepdims=False)
     other = lax.ppermute(other, "dom", [(i, i ^ 1) for i in range(n_doms)])

time: 54.9 us -> 47.1 us (0.86)
  Pallas kernels: 8.92 us -> 4.58 us
  starting transfers between devices: 16.3 us -> 14.4 us
  blocking collectives: 23.6 us -> 22.6 us
    pallas_call x1, Pallas kernels: 2.76 us -> 0.91 us  [make_send(): pl.pallas_call(send_kernel, out_shape=(message,) * 3, in_specs=[vmem], ou...]
    pallas_call x1, Pallas kernels: 2.64 us -> 0.85 us  [make_own(): pl.pallas_call(own_kernel, out_shape=jax.ShapeDtypeStruct((MOM, 2, RY, NZ...]
    ppermute x1, starting transfers between devices: 3.47 us -> 2.27 us  [local(): other = lax.ppermute(other, 'dom', [(i, i ^ 1) for i in range(n_doms)])]
    all_gather x1, blocking collectives: 23.6 us -> 22.6 us  [local(): gathered = lax.all_gather(x, 'dom', tiled=True)]
    pallas_call x1, Pallas kernels: 3.52 us -> 2.82 us  [make_terms(): pl.pallas_call(terms_kernel, out_shape=jax.ShapeDtypeStruct((ROWS, COLS),...]
    ppermute x2 -> x3, starting transfers between devices: 12.8 us -> 12.1 us  [the longest x1 9.55 us: local(): lax.ppermute(outer, both, swap_pairs(n_slabs, n_doms, 1, lambda s: True))]
    ppermute x2 -> x3, waiting for transfers between devices: 3.49 us -> 3.03 us  [the longest x1 3.03 us: local(): lax.ppermute(outer, both, swap_pairs(n_slabs, n_doms, 1, lambda s: True))]
  transfers between devices with their start and end apart: 3 -> 4, of which waited for: 3 -> 2; matrix products, arithmetic and copies ran while one was open for 0% -> 0% of each run, Pallas kernels for 5% -> 2%
where the time goes in v3:
time: 47.1 us; the launch traced here: 46.9 us
  blocking collectives  22.6 us (48%)
  starting transfers between devices  14.4 us (31%)
  Pallas kernels  4.58 us (10%)
  waiting for transfers between devices  3.93 us (8%)
  between operations  0.73 us (2%)
  other arithmetic  0.68 us (1%)
    all_gather x1, blocking collectives, local(): gathered = lax.all_gather(x, 'dom', tiled=True)  22.6 us
    ppermute x1, starting transfers between devices, local(): lax.ppermute(outer, both, swap_pairs(n_slabs, n_doms, 1, lambda s: True))  9.55 us
    ppermute x1, waiting for transfers between devices, local(): lax.ppermute(outer, both, swap_pairs(n_slabs, n_doms, 1, lambda s: True))  3.03 us
    pallas_call x1, Pallas kernels, make_terms(): pl.pallas_call(terms_kernel, out_shape=jax.ShapeDtypeStruct((ROWS, COLS),...  2.82 us
    ppermute x1, starting transfers between devices, local(): other = lax.ppermute(other, 'dom', [(i, i ^ 1) for i in range(n_doms)])  2.27 us
    ppermute x1, starting transfers between devices, local(): lax.ppermute(early, both, swap_pairs(n_slabs, n_doms, 0, half(True)))  1.92 us
  transfers between devices with their start and end apart: 4, of which 2 were waited for; matrix products, arithmetic and copies ran while one was open for 0% of the time, Pallas kernels for 2%

profile of v3, /device:TPU:1, one launch (start us, length us, event | category | flops | bytes accessed | tf_op | source)
XLA Modules:
  0.0 46.9 jit_solution(12066954166545519994)
XLA Ops:
  0.7 2.8 %terms.1 = bf16[80,640]{1,0:T(8,128)(2,1)} custom-call(s32[1,1]{1,0:T(1,128)S(6)} %copy.6.count_hbm, s32[1,32]{1,0:T(1,128)} %tile_hbm.1, s32[1,32]{1,0:T(1,128)} %slab_hbm.1, bf16[32,64,128]{2,1,0:T(8,128)(2,1)} %bitcast.10, bf16[10,32,128]{2,1,0:T(8,128)(2,1)} %bitcast.11), custom_call_target="tpu_custom_call" | custom-call | tf_op jit(solution)/shard_map/terms/pallas_call | solution.py:211
  3.5 22.6 %all_gather.3.x_ref = bf16[640,640]{1,0:T(8,128)(2,1)S(1)} all-gather(bf16[80,640]{1,0:T(8,128)(2,1)} %terms.1), channel_id=1, replica_groups=mesh['dom'=8,'slab'=64] {'dom'}, dimensions={0}, use_global_device_ids=true | all-gather | bytes 921600 | tf_op jit(solution)/shard_map/all_gather | solution.py:262
  26.0 0.9 %send.1 = (f32[2,10,2,8,128]{4,3,2,1,0:T(8,128)S(1)}, f32[2,10,2,8,128]{4,3,2,1,0:T(8,128)S(1)}, f32[2,10,2,8,128]{4,3,2,1,0:T(8,128)S(1)}) custom-call(bf16[640,640]{1,0:T(8,128)(2,1)S(1)} %all_gather.3.x_ref), custom_call_target="tpu_custom_call" | custom-call | tf_op jit(solution)/shard_map/send/pallas_call | solution.py:233
  26.9 1.9 %collective-permute-start = (f32[2,10,2,8,128]{4,3,2,1,0:T(8,128)S(1)}, f32[2,10,2,8,128]{4,3,2,1,0:T(8,128)S(1)}, u32[]{:S(2)}, u32[]{:S(2)}) collective-permute-start(f32[2,10,2,8,128]{4,3,2,1,0:T(8,128)S(1)} %get-tuple-element.12), channel_id=1, source_target_pairs={{0,2},{64,65},{128,130},{192,193},{256,258},{320,321},{384,386},{4... | collective-permute-start | bytes 491528 | tf_op jit(solution)/shard_map/ppermute | solution.py:266
  28.9 9.6 %collective-permute-start.1 = (f32[2,10,2,8,128]{4,3,2,1,0:T(8,128)S(1)}, f32[2,10,2,8,128]{4,3,2,1,0:T(8,128)S(1)}, u32[]{:S(2)}, u32[]{:S(2)}) collective-permute-start(f32[2,10,2,8,128]{4,3,2,1,0:T(8,128)S(1)} %get-tuple-element.13), channel_id=1, source_target_pairs={{0,62},{64,127},{128,190},{192,255},{256,318},{320,383},{384,446},... | collective-permute-start | bytes 491528 | tf_op jit(solution)/shard_map/ppermute | solution.py:267
  38.4 0.7 %collective-permute-start.2 = (f32[2,10,2,8,128]{4,3,2,1,0:T(8,128)S(1)}, f32[2,10,2,8,128]{4,3,2,1,0:T(8,128)S(1)}, u32[]{:S(2)}, u32[]{:S(2)}) collective-permute-start(f32[2,10,2,8,128]{4,3,2,1,0:T(8,128)S(1)} %get-tuple-element.14), channel_id=1, source_target_pairs={{16,18},{80,81},{144,146},{208,209},{272,274},{336,337},{400,402},... | collective-permute-start | bytes 491528 | tf_op jit(solution)/shard_map/ppermute | solution.py:268
  39.1 0.9 %own.1 = f32[10,2,8,128]{3,2,1,0:T(8,128)S(1)} custom-call(bf16[640,640]{1,0:T(8,128)(2,1)S(1)} %all_gather.3.x_ref), custom_call_target="tpu_custom_call" | custom-call | flops 400000000 | bytes 8000000 | tf_op jit(solution)/shard_map/own/pallas_call | solution.py:245
  40.0 0.0 collective-permute-done
  40.0 3.0 %collective-permute-done.1 = f32[2,10,2,8,128]{4,3,2,1,0:T(8,128)S(1)} collective-permute-done((f32[2,10,2,8,128]{4,3,2,1,0:T(8,128)S(1)}, f32[2,10,2,8,128]{4,3,2,1,0:T(8,128)S(1)}, u32[]{:S(2)}, u32[]{:S(2)}) %collective-permute-start.1) | collective-permute-done | bytes 163872 | tf_op jit(solution)/shard_map/ppermute | solution.py:267
  43.0 0.0 collective-permute-done.2
  43.1 2.3 %collective-permute-start.3 = (f32[10,2,8,128]{3,2,1,0:T(8,128)S(1)}, f32[10,2,8,128]{3,2,1,0:T(8,128)S(1)}, u32[]{:S(2)}, u32[]{:S(2)}) collective-permute-start(f32[10,2,8,128]{3,2,1,0:T(8,128)S(1)} %dynamic-slice_bitcast_fusion), channel_id=1, source_target_pairs={{0,64},{64,0},{128,192},{192,128},{256,320},{320,256},{384,448},{4... | collective-permute-start | bytes 245768 | tf_op jit(solution)/shard_map/ppermute | solution.py:274
  45.4 0.9 %collective-permute-done.3 = f32[10,2,8,128]{3,2,1,0:T(8,128)S(1)} collective-permute-done((f32[10,2,8,128]{3,2,1,0:T(8,128)S(1)}, f32[10,2,8,128]{3,2,1,0:T(8,128)S(1)}, u32[]{:S(2)}, u32[]{:S(2)}) %collective-permute-start.3) | collective-permute-done | bytes 81952 | tf_op jit(solution)/shard_map/ppermute | solution.py:274
  46.3 0.6 %fusion = f32[10,2,8,128]{3,2,1,0:T(8,128)} fusion(f32[10,2,8,128]{3,2,1,0:T(8,128)S(1)} %collective-permute-done.3, f32[10,2,8,128]{3,2,1,0:T(8,128)S(1)} %own.1, f32[2,10,2,8,128]{4,3,2,1,0:T(8,128)S(1)} %add_add_fusion, s32[]{:T(128)S(6)} %select_n.7), kind=kLoop, calls=%fused_computation.2 | loop fusion | flops 40960 | bytes 327684 | tf_op jit(solution)/shard_map/add | solution.py:275
  (2 shorter events, 0.0 us)
Async XLA Ops:
  26.9 13.0 %collective-permute-start = (f32[2,10,2,8,128]{4,3,2,1,0:T(8,128)S(1)}, f32[2,10,2,8,128]{4,3,2,1,0:T(8,128)S(1)}, u32[]{:S(2)}, u32[]{:S(2)}) collective-permute-start(f32[2,10,2,8,128]{4,3,2,1,0:T(8,128)S(1)} %get-tuple-element.12), channel_id=1, source_target_pairs={{0,2},{64,65},{128,130},{192,193},{256,258},{320,321},{384,386},{4... | collective-permute-start | bytes 491528 | tf_op jit(solution)/shard_map/ppermute | solution.py:266
  28.9 14.1 %collective-permute-start.1 = (f32[2,10,2,8,128]{4,3,2,1,0:T(8,128)S(1)}, f32[2,10,2,8,128]{4,3,2,1,0:T(8,128)S(1)}, u32[]{:S(2)}, u32[]{:S(2)}) collective-permute-start(f32[2,10,2,8,128]{4,3,2,1,0:T(8,128)S(1)} %get-tuple-element.13), channel_id=1, source_target_pairs={{0,62},{64,127},{128,190},{192,255},{256,318},{320,383},{384,446},... | collective-permute-start | bytes 491528 | tf_op jit(solution)/shard_map/ppermute | solution.py:267
  38.4 4.6 %collective-permute-start.2 = (f32[2,10,2,8,128]{4,3,2,1,0:T(8,128)S(1)}, f32[2,10,2,8,128]{4,3,2,1,0:T(8,128)S(1)}, u32[]{:S(2)}, u32[]{:S(2)}) collective-permute-start(f32[2,10,2,8,128]{4,3,2,1,0:T(8,128)S(1)} %get-tuple-element.14), channel_id=1, source_target_pairs={{16,18},{80,81},{144,146},{208,209},{272,274},{336,337},{400,402},... | collective-permute-start | bytes 491528 | tf_op jit(solution)/shard_map/ppermute | solution.py:268
  43.1 3.2 %collective-permute-start.3 = (f32[10,2,8,128]{3,2,1,0:T(8,128)S(1)}, f32[10,2,8,128]{3,2,1,0:T(8,128)S(1)}, u32[]{:S(2)}, u32[]{:S(2)}) collective-permute-start(f32[10,2,8,128]{3,2,1,0:T(8,128)S(1)} %dynamic-slice_bitcast_fusion), channel_id=1, source_target_pairs={{0,64},{64,0},{128,192},{192,128},{256,320},{320,256},{384,448},{4... | collective-permute-start | bytes 245768 | tf_op jit(solution)/shard_map/ppermute | solution.py:274

commit v4 on v3

--- a/solution.py
+++ b/solution.py
@@ -1,3 +1,5 @@
+import functools
+
 import jax
 import jax.numpy as jnp
 from jax import lax
@@ -26,9 +28,13 @@
     return lax.broadcasted_iota(jnp.int32, shape, dim)
 
 
+def fixed_factor(top):
+    return jnp.exp2(14.9 - top)
+
+
 def terms_kernel(
-    count_hbm, tile_hbm, slab_hbm, weight_hbm, moment_hbm, out_ref,
-    count_ref, tile_ref, slab_ref, weight_ref, moment_ref, term_ref, mom_ref, sems,
+    count_ref, tile_hbm, slab_hbm, weight_hbm, moment_hbm, out_ref,
+    tile_ref, slab_ref, weight_ref, moment_ref, term_ref, mom_ref, sems,
 ):
     my_slab, my_dom, n_slabs = lax.axis_index("slab"), lax.axis_index("dom"), lax.axis_size("slab")
     size = BLK // CHUNKS
@@ -36,7 +42,6 @@
         pltpu.make_async_copy(moment_hbm, moment_ref, sems.at[CHUNKS]),
         pltpu.make_async_copy(tile_hbm, tile_ref, sems.at[CHUNKS + 1]),
         pltpu.make_async_copy(slab_hbm, slab_ref, sems.at[CHUNKS + 2]),
-        pltpu.make_async_copy(count_hbm, count_ref, sems.at[CHUNKS + 3]),
     ]
     copies = []
     for c in range(CHUNKS):
@@ -53,7 +58,7 @@
     step = jnp.where(step == n_slabs - 1, -1, jnp.where(step == 1 - n_slabs, 1, step))
     plane = 1 + lax.shift_right_logical(tile, 7) + 2 * step
     row = lax.shift_right_logical(tile & 127, 1)
-    used = iota((1, BLK), 1) < count_ref[...]
+    used = iota((1, BLK), 1) < count_ref[0, 0]
     code = jnp.where(used, plane * NY + row + 1, 0).astype(jnp.float32)
     half = (tile & 1).astype(jnp.float32)
     both = jnp.where(iota((8, BLK), 0) == 0, code, half).astype(jnp.bfloat16)
@@ -155,16 +160,47 @@
         near(g[3], g[2], g[1], 4, 3)
     part_ref[6] = jnp.zeros((MOM, 2, RY, NZ), jnp.float32)
 
+    sub = iota((RY, NZ), 0)
     for refs, odd_up in (((outer_ref,), 1), ((early_ref, late_ref), 0)):
         near_up = lax.rem(my_slab, 2) == odd_up
         far_up = lax.rem(lax.div(my_slab, 2), 2) == odd_up
         at = jnp.where(near_up, 3, 1)
         a = jnp.where(core == 1, at, jnp.where(far_up, 5, 6))
         b = jnp.where(core == 1, at + 1, jnp.where(far_up, 6, 0))
-        for p, i in ((0, a), (1, b)):
-            for h in range(2):
+        tops = [jnp.zeros((RY, NZ), jnp.float32)] * 2
+        for m in range(MOM):
+            values = [part_ref[i, m, h] for h in range(2) for i in (a, b)]
+            top = functools.reduce(jnp.maximum, [jnp.abs(v) for v in values])
+            for k in (4, 2, 1):
+                top = jnp.maximum(top, pltpu.roll(top, k, 0))
+            top = jnp.floor(jnp.log2(jnp.maximum(top, 1e-30))) + 1.0
+            factor = fixed_factor(top)
+            tops[m // RY] = jnp.where(sub == m % RY, top, tops[m // RY])
+            for k, v in enumerate(values):
+                q = jnp.floor(v * factor + 0.5).astype(jnp.int32).astype(jnp.int16)
                 for ref in refs:
-                    ref[h, :, p] = part_ref[i, :, h]
+                    ref[4 * m + k] = q
+        for k in range(2):
+            q = tops[k].astype(jnp.int32).astype(jnp.int16)
+            for ref in refs:
+                ref[4 * MOM + k] = q
+
+
+def join_kernel(early_ref, outer_ref, late_ref, own_ref, mine_ref, other_ref):
+    core = lax.rem(lax.axis_index("dom"), 2)
+    refs = (early_ref, outer_ref, late_ref)
+    tops = [[ref[4 * MOM + k].astype(jnp.float32) for k in range(2)] for ref in refs]
+    for m in range(MOM):
+        at = m % RY
+        scales = [1.0 / fixed_factor(top[m // RY][at : at + 1]) for top in tops]
+        for p in range(2):
+
+            def arrived(h):
+                parts = [ref[4 * m + 2 * h + p].astype(jnp.float32) * c for ref, c in zip(refs, scales)]
+                return parts[0] + parts[1] + parts[2]
+
+            other_ref[m, p] = arrived(1 - core)
+            mine_ref[m, p] = own_ref[m, p] + arrived(core)
 
 
 def own_kernel(x_ref, own_ref, part_ref):
@@ -203,6 +239,7 @@
 
 limited = pltpu.CompilerParams(vmem_limit_bytes=16 * 1024 * 1024)
 alone = pltpu.CompilerParams(vmem_limit_bytes=60 * 1024 * 1024)
+smem = pl.BlockSpec(memory_space=pltpu.SMEM)
 hbm = pl.BlockSpec(memory_space=pltpu.HBM)
 vmem = pl.BlockSpec(memory_space=pltpu.VMEM)
 
@@ -210,18 +247,17 @@
 def make_terms(weights, moments, block_tile, block_slab, block_count):
     return pl.pallas_call(
         terms_kernel,
-        out_shape=jax.ShapeDtypeStruct((ROWS, COLS), jnp.bfloat16),
-        in_specs=[hbm] * 5,
+        out_shape=pltpu.VMEM((ROWS, COLS), jnp.bfloat16),
+        in_specs=[smem] + [hbm] * 4,
         out_specs=vmem,
         scratch_shapes=[
-            pltpu.VMEM((1, 1), jnp.int32),
             pltpu.VMEM((1, BLK), jnp.int32),
             pltpu.VMEM((1, BLK), jnp.int32),
             pltpu.VMEM((BLK, TC, NZ), jnp.bfloat16),
             pltpu.VMEM((MOM, BLK, NZ), jnp.bfloat16),
             pltpu.VMEM((16 * BLK, NZ), jnp.float32),
             pltpu.VMEM((MOM * BLK, NZ), jnp.float32),
-            pltpu.SemaphoreType.DMA((CHUNKS + 4,)),
+            pltpu.SemaphoreType.DMA((CHUNKS + 3,)),
         ],
         compiler_params=alone,
         name="terms",
@@ -229,7 +265,7 @@
 
 
 def make_send(gathered):
-    message = jax.ShapeDtypeStruct((2, MOM, 2, RY, NZ), jnp.float32)
+    message = jax.ShapeDtypeStruct((4 * MOM + 2, RY, NZ), jnp.int16)
     return pl.pallas_call(
         send_kernel,
         out_shape=(message,) * 3,
@@ -257,7 +293,6 @@
 def local(weights, moments, block_tile, block_slab, block_count):
     n_slabs = lax.axis_size("slab")
     n_doms = lax.axis_size("dom")
-    core = lax.rem(lax.axis_index("dom"), 2)
     x = make_terms(weights, moments, block_tile, block_slab, block_count)
     gathered = lax.all_gather(x, "dom", tiled=True)
     early, outer, late = make_send(gathered)
@@ -268,9 +303,15 @@
     late = lax.ppermute(late, both, swap_pairs(n_slabs, n_doms, 0, half(False)))
     own = make_own(gathered)
     early, outer, late, own = lax.optimization_barrier((early, outer, late, own))
-    arrived = outer + (early + late)
-    mine = lax.dynamic_index_in_dim(arrived, core, 0, keepdims=False) + own
-    other = lax.dynamic_index_in_dim(arrived, 1 - core, 0, keepdims=False)
+    part = jax.ShapeDtypeStruct((MOM, 2, RY, NZ), jnp.float32)
+    mine, other = pl.pallas_call(
+        join_kernel,
+        out_shape=(part, part),
+        in_specs=[vmem] * 4,
+        out_specs=(vmem, vmem),
+        compiler_params=limited,
+        name="join",
+    )(early, outer, late, own)
     other = lax.ppermute(other, "dom", [(i, i ^ 1) for i in range(n_doms)])
     return mine + other
 

time: 47.1 us -> 44.9 us (0.953)
  waiting for transfers between devices: 3.93 us -> 2.25 us
  Pallas kernels: 4.58 us -> 4.01 us
    ppermute x1, waiting for transfers between devices: 3.03 us -> 1.35 us  [local(): lax.ppermute(outer, both, swap_pairs(n_slabs, n_doms, 1, lambda s: True))]
    pallas_call x1 -> x2, Pallas kernels: 2.82 us -> 2.2 us  [the longest x1 2.12 us: make_terms(): pl.pallas_call(terms_kernel, out_shape=pltpu.VMEM((ROWS, COLS), jnp.bfloa...]
where the time goes in v4:
time: 44.9 us; the launch traced here: 44.7 us
  blocking collectives  22.3 us (50%)
  starting transfers between devices  14.8 us (33%)
  Pallas kernels  4.01 us (9%)
  waiting for transfers between devices  2.25 us (5%)
  between operations  0.72 us (2%)
  other arithmetic  0.65 us (1%)
    all_gather x1, blocking collectives, local(): gathered = lax.all_gather(x, 'dom', tiled=True)  22.3 us
    ppermute x1, starting transfers between devices, local(): lax.ppermute(outer, both, swap_pairs(n_slabs, n_doms, 1, lambda s: True))  9.55 us
    ppermute x1, starting transfers between devices, local(): other = lax.ppermute(other, 'dom', [(i, i ^ 1) for i in range(n_doms)])  2.62 us
    pallas_call x1, Pallas kernels, make_terms(): pl.pallas_call(terms_kernel, out_shape=pltpu.VMEM((ROWS, COLS), jnp.bfloa...  2.12 us
    ppermute x1, starting transfers between devices, local(): lax.ppermute(early, both, swap_pairs(n_slabs, n_doms, 0, half(True)))  1.92 us
    ppermute x1, waiting for transfers between devices, local(): lax.ppermute(outer, both, swap_pairs(n_slabs, n_doms, 1, lambda s: True))  1.35 us
    pallas_call x1, Pallas kernels, make_send(): pl.pallas_call(send_kernel, out_shape=(message,) * 3, in_specs=[vmem], ou...  0.96 us
    ppermute x1, waiting for transfers between devices, local(): other = lax.ppermute(other, 'dom', [(i, i ^ 1) for i in range(n_doms)])  0.9 us
  transfers between devices with their start and end apart: 4, of which 2 were waited for; matrix products, arithmetic and copies ran while one was open for 0% of the time, Pallas kernels for 2%

profile of v4, /device:TPU:1, one launch (start us, length us, event | category | flops | bytes accessed | tf_op | source)
XLA Modules:
  0.0 44.7 jit_solution(18372037264414430755)
XLA Ops:
  0.7 2.1 %terms.1 = bf16[80,640]{1,0:T(8,128)(2,1)S(1)} custom-call(s32[1,1]{1,0:T(1,128)S(6)} %copy.6.count_ref, s32[1,32]{1,0:T(1,128)} %tile_hbm.1, s32[1,32]{1,0:T(1,128)} %slab_hbm.1, bf16[32,64,128]{2,1,0:T(8,128)(2,1)} %bitcast.4, bf16[10,32,128]{2,1,0:T(8,128)(2,1)} %bitcast.5), custom_call_target="tpu_custom_call" | custom-call | tf_op jit(solution)/shard_map/terms/pallas_call | solution.py:248
  2.8 22.3 %all_gather.3.x_ref = bf16[640,640]{1,0:T(8,128)(2,1)S(1)} all-gather(bf16[80,640]{1,0:T(8,128)(2,1)S(1)} %terms.1), channel_id=1, replica_groups=mesh['dom'=8,'slab'=64] {'dom'}, dimensions={0}, use_global_device_ids=true | all-gather | bytes 921600 | tf_op jit(solution)/shard_map/all_gather | solution.py:297
  25.1 1.0 %send.1 = (s16[42,8,128]{2,1,0:T(8,128)(2,1)S(1)}, s16[42,8,128]{2,1,0:T(8,128)(2,1)S(1)}, s16[42,8,128]{2,1,0:T(8,128)(2,1)S(1)}) custom-call(bf16[640,640]{1,0:T(8,128)(2,1)S(1)} %all_gather.3.x_ref), custom_call_target="tpu_custom_call" | custom-call | tf_op jit(solution)/shard_map/send/pallas_call | solution.py:269
  26.1 1.9 %collective-permute-start = (s16[42,8,128]{2,1,0:T(8,128)(2,1)S(1)}, s16[42,8,128]{2,1,0:T(8,128)(2,1)S(1)}, u32[]{:S(2)}, u32[]{:S(2)}) collective-permute-start(s16[42,8,128]{2,1,0:T(8,128)(2,1)S(1)} %get-tuple-element.14), channel_id=1, source_target_pairs={{0,2},{64,65},{128,130},{192,193},{256,258},{320,321},{384,386},{4... | collective-permute-start | bytes 258056 | tf_op jit(solution)/shard_map/ppermute | solution.py:301
  28.0 9.6 %collective-permute-start.1 = (s16[42,8,128]{2,1,0:T(8,128)(2,1)S(1)}, s16[42,8,128]{2,1,0:T(8,128)(2,1)S(1)}, u32[]{:S(2)}, u32[]{:S(2)}) collective-permute-start(s16[42,8,128]{2,1,0:T(8,128)(2,1)S(1)} %get-tuple-element.15), channel_id=1, source_target_pairs={{0,62},{64,127},{128,190},{192,255},{256,318},{320,383},{384,446},... | collective-permute-start | bytes 258056 | tf_op jit(solution)/shard_map/ppermute | solution.py:302
  37.6 0.7 %collective-permute-start.2 = (s16[42,8,128]{2,1,0:T(8,128)(2,1)S(1)}, s16[42,8,128]{2,1,0:T(8,128)(2,1)S(1)}, u32[]{:S(2)}, u32[]{:S(2)}) collective-permute-start(s16[42,8,128]{2,1,0:T(8,128)(2,1)S(1)} %get-tuple-element.16), channel_id=1, source_target_pairs={{16,18},{80,81},{144,146},{208,209},{272,274},{336,337},{400,402},... | collective-permute-start | bytes 258056 | tf_op jit(solution)/shard_map/ppermute | solution.py:303
  38.3 0.8 %own.1.own_ref = f32[10,2,8,128]{3,2,1,0:T(8,128)S(1)} custom-call(bf16[640,640]{1,0:T(8,128)(2,1)S(1)} %all_gather.3.x_ref), custom_call_target="tpu_custom_call" | custom-call | flops 400000000 | bytes 8000000 | tf_op jit(solution)/shard_map/own/pallas_call | solution.py:281
  39.1 0.0 collective-permute-done.early_ref
  39.1 1.3 %collective-permute-done.1.outer_ref = s16[42,8,128]{2,1,0:T(8,128)(2,1)S(1)} collective-permute-done((s16[42,8,128]{2,1,0:T(8,128)(2,1)S(1)}, s16[42,8,128]{2,1,0:T(8,128)(2,1)S(1)}, u32[]{:S(2)}, u32[]{:S(2)}) %collective-permute-start.1) | collective-permute-done | bytes 86048 | tf_op jit(solution)/shard_map/ppermute | solution.py:302
  40.5 0.0 collective-permute-done.2.late_ref
  40.5 0.1 join.1
  40.6 2.6 %collective-permute-start.3 = (f32[10,2,8,128]{3,2,1,0:T(8,128)S(1)}, f32[10,2,8,128]{3,2,1,0:T(8,128)S(1)}, u32[]{:S(2)}, u32[]{:S(2)}) collective-permute-start(f32[10,2,8,128]{3,2,1,0:T(8,128)S(1)} %get-tuple-element.22), channel_id=1, source_target_pairs={{0,64},{64,0},{128,192},{192,128},{256,320},{320,256},{384,448},{4... | collective-permute-start | bytes 245768 | tf_op jit(solution)/shard_map/ppermute | solution.py:315
  43.2 0.9 %collective-permute-done.3 = f32[10,2,8,128]{3,2,1,0:T(8,128)S(1)} collective-permute-done((f32[10,2,8,128]{3,2,1,0:T(8,128)S(1)}, f32[10,2,8,128]{3,2,1,0:T(8,128)S(1)}, u32[]{:S(2)}, u32[]{:S(2)}) %collective-permute-start.3) | collective-permute-done | bytes 81952 | tf_op jit(solution)/shard_map/ppermute | solution.py:315
  44.1 0.6 %add.3 = f32[10,2,8,128]{3,2,1,0:T(8,128)} add(f32[10,2,8,128]{3,2,1,0:T(8,128)S(1)} %get-tuple-element.21, f32[10,2,8,128]{3,2,1,0:T(8,128)S(1)} %collective-permute-done.3) | non-fusion elementwise | flops 20480 | bytes 245760 | tf_op jit(solution)/shard_map/add | solution.py:316
Async XLA Ops:
  26.1 13.0 %collective-permute-start = (s16[42,8,128]{2,1,0:T(8,128)(2,1)S(1)}, s16[42,8,128]{2,1,0:T(8,128)(2,1)S(1)}, u32[]{:S(2)}, u32[]{:S(2)}) collective-permute-start(s16[42,8,128]{2,1,0:T(8,128)(2,1)S(1)} %get-tuple-element.14), channel_id=1, source_target_pairs={{0,2},{64,65},{128,130},{192,193},{256,258},{320,321},{384,386},{4... | collective-permute-start | bytes 258056 | tf_op jit(solution)/shard_map/ppermute | solution.py:301
  28.0 12.4 %collective-permute-start.1 = (s16[42,8,128]{2,1,0:T(8,128)(2,1)S(1)}, s16[42,8,128]{2,1,0:T(8,128)(2,1)S(1)}, u32[]{:S(2)}, u32[]{:S(2)}) collective-permute-start(s16[42,8,128]{2,1,0:T(8,128)(2,1)S(1)} %get-tuple-element.15), channel_id=1, source_target_pairs={{0,62},{64,127},{128,190},{192,255},{256,318},{320,383},{384,446},... | collective-permute-start | bytes 258056 | tf_op jit(solution)/shard_map/ppermute | solution.py:302
  37.6 2.9 %collective-permute-start.2 = (s16[42,8,128]{2,1,0:T(8,128)(2,1)S(1)}, s16[42,8,128]{2,1,0:T(8,128)(2,1)S(1)}, u32[]{:S(2)}, u32[]{:S(2)}) collective-permute-start(s16[42,8,128]{2,1,0:T(8,128)(2,1)S(1)} %get-tuple-element.16), channel_id=1, source_target_pairs={{16,18},{80,81},{144,146},{208,209},{272,274},{336,337},{400,402},... | collective-permute-start | bytes 258056 | tf_op jit(solution)/shard_map/ppermute | solution.py:303
  40.6 3.5 %collective-permute-start.3 = (f32[10,2,8,128]{3,2,1,0:T(8,128)S(1)}, f32[10,2,8,128]{3,2,1,0:T(8,128)S(1)}, u32[]{:S(2)}, u32[]{:S(2)}) collective-permute-start(f32[10,2,8,128]{3,2,1,0:T(8,128)S(1)} %get-tuple-element.22), channel_id=1, source_target_pairs={{0,64},{64,0},{128,192},{192,128},{256,320},{320,256},{384,448},{4... | collective-permute-start | bytes 245768 | tf_op jit(solution)/shard_map/ppermute | solution.py:315

commit v5 on v4

--- a/solution.py
+++ b/solution.py
@@ -19,7 +19,9 @@
 PLANES = 4
 ROWS = 80
 COLS = MOM * TC
-CHUNKS = 4
+KEPT = 8 * 2 * BLK
+CHUNKS = 2
+GROUP = 4
 diffusion = 0.16
 keep_weight = 1.0 - 6.0 * diffusion
 
@@ -53,6 +55,7 @@
         copy.wait()
     for m in range(MOM):
         mom_ref[BLK * m : BLK * (m + 1), :] = moment_ref[m].astype(jnp.float32)
+    mom_ref[BLK * MOM :, :] = jnp.zeros((BLK * (16 - MOM), NZ), jnp.float32)
     tile, slab = tile_ref[...], slab_ref[...]
     step = slab - my_slab
     step = jnp.where(step == n_slabs - 1, -1, jnp.where(step == 1 - n_slabs, 1, step))
@@ -63,24 +66,31 @@
     half = (tile & 1).astype(jnp.float32)
     both = jnp.where(iota((8, BLK), 0) == 0, code, half).astype(jnp.bfloat16)
     slot = iota((BLK, COLS), 0)
-    lane = iota((BLK, COLS), 1) - my_dom * ROWS
+    slot = lax.shift_right_logical(slot, 1) + (slot & 1) * (BLK // 2)
+    lane = iota((BLK, COLS), 1) - my_dom * 2 * BLK
     spread = jnp.where((lane == slot) | (lane == slot + BLK), 1.0, 0.0).astype(jnp.bfloat16)
     codes = jnp.dot(both, spread, preferred_element_type=jnp.float32).astype(jnp.bfloat16)
     out_ref[2 * BLK : ROWS, :] = jnp.concatenate([codes, codes], axis=0)
-    for b in range(BLK):
+    low_half = iota((16, NZ), 1) < TC
+    for b in range(0, BLK, GROUP):
         if b % size == 0:
             copies[b // size].wait()
-        w = weight_ref[b]
-        pair = jnp.concatenate([w, w], axis=0)
-        mom = mom_ref[pl.ds(b, MOM, stride=BLK), :].astype(jnp.bfloat16)
-        term_ref[pl.ds(16 * b, MOM), :] = lax.dot_general(
-            mom, pair, (((1,), (1,)), ((), ())), preferred_element_type=jnp.float32
+        moms = [mom_ref[pl.ds(b + i, 16, stride=BLK), :] for i in range(GROUP)]
+        mom = jnp.concatenate(moms, axis=0).astype(jnp.bfloat16)
+        w = weight_ref[b : b + GROUP].reshape(GROUP * TC, NZ)
+        term = lax.dot_general(mom, w, (((1,), (1,)), ((), ())), preferred_element_type=jnp.float32)
+        for i in range(0, GROUP, 2):
+            cols = slice(TC * i, TC * (i + 2))
+            pair = jnp.where(low_half, term[16 * i : 16 * i + 16, cols], term[16 * i + 16 : 16 * i + 32, cols])
+            term_ref[8 * (b + i) : 8 * (b + i) + 16, :] = pair
+    for j in range(MOM // 2):
+        even = term_ref[pl.ds(2 * j, BLK // 2, stride=16), :]
+        odd = term_ref[pl.ds(2 * j + 1, BLK // 2, stride=16), :]
+        rows = (
+            jnp.where(low_half, even, pltpu.roll(odd, TC, 1)),
+            jnp.where(low_half, pltpu.roll(even, TC, 1), odd),
         )
-    low_half = iota((BLK, NZ), 1) < TC
-    for j in range(MOM // 2):
-        even = term_ref[pl.ds(2 * j, BLK, stride=16), :]
-        odd = term_ref[pl.ds(2 * j + 1, BLK, stride=16), :]
-        term = jnp.where(low_half, even, odd)
+        term = jnp.concatenate(rows, axis=0)
         high = term.astype(jnp.bfloat16)
         low = (term - high.astype(jnp.float32)).astype(jnp.bfloat16)
         out_ref[0:BLK, NZ * j : NZ * (j + 1)] = high
@@ -91,15 +101,16 @@
     codes = x_ref[2 * BLK : ROWS, :].astype(jnp.float32)
     for k in range(1, 8):
         codes += x_ref[ROWS * k + 2 * BLK : ROWS * (k + 1), :].astype(jnp.float32)
-    code = codes[0:1, :].astype(jnp.int32) - 1
-    half = codes[1:2, :].astype(jnp.int32)
+    code = codes[0:1, :KEPT].astype(jnp.int32) - 1
+    half = codes[1:2, :KEPT].astype(jnp.int32)
     plane = lax.shift_right_arithmetic(code, 6)
     rel = (code & (NY - 1)) - top_row
     valid = (code >= 0) & (rel >= -HALO) & (rel < CHIP_ROWS + HALO)
     spot = (half * PLANES + plane) * WIN + jnp.where(rel < 0, rel + WIN, rel)
     spot = jnp.where(valid, spot, -1)
-    chosen = jnp.where(iota((2 * PLANES * WIN, COLS), 0) == spot, 1.0, 0.0).astype(jnp.bfloat16)
-    return jnp.dot(chosen, x_ref[...], preferred_element_type=jnp.float32)
+    chosen = jnp.where(iota((2 * PLANES * WIN, KEPT), 0) == spot, 1.0, 0.0).astype(jnp.bfloat16)
+    terms = jnp.concatenate([x_ref[ROWS * k : ROWS * k + 2 * BLK, :] for k in range(8)], axis=0)
+    return jnp.dot(chosen, terms, preferred_element_type=jnp.float32)
 
 
 class Stencil:
@@ -255,8 +266,8 @@
             pltpu.VMEM((1, BLK), jnp.int32),
             pltpu.VMEM((BLK, TC, NZ), jnp.bfloat16),
             pltpu.VMEM((MOM, BLK, NZ), jnp.bfloat16),
+            pltpu.VMEM((8 * BLK, NZ), jnp.float32),
             pltpu.VMEM((16 * BLK, NZ), jnp.float32),
-            pltpu.VMEM((MOM * BLK, NZ), jnp.float32),
             pltpu.SemaphoreType.DMA((CHUNKS + 3,)),
         ],
         compiler_params=alone,

time: 44.9 us -> 44.3 us (0.987)
  Pallas kernels: 4.01 us -> 3.38 us
    pallas_call x1, Pallas kernels: 2.12 us -> 1.62 us  [make_terms(): pl.pallas_call(terms_kernel, out_shape=pltpu.VMEM((ROWS, COLS), jnp.bfloa...]
where the time goes in v5:
time: 44.3 us; the launch traced here: 44.1 us
  blocking collectives  22.3 us (50%)
  starting transfers between devices  14.8 us (33%)
  Pallas kernels  3.38 us (8%)
  waiting for transfers between devices  2.25 us (5%)
  between operations  0.72 us (2%)
  other arithmetic  0.65 us (1%)
    all_gather x1, blocking collectives, local(): gathered = lax.all_gather(x, 'dom', tiled=True)  22.3 us
    ppermute x1, starting transfers between devices, local(): lax.ppermute(outer, both, swap_pairs(n_slabs, n_doms, 1, lambda s: True))  9.43 us
    ppermute x1, starting transfers between devices, local(): other = lax.ppermute(other, 'dom', [(i, i ^ 1) for i in range(n_doms)])  2.76 us
    ppermute x1, starting transfers between devices, local(): lax.ppermute(early, both, swap_pairs(n_slabs, n_doms, 0, half(True)))  1.92 us
    pallas_call x1, Pallas kernels, make_terms(): pl.pallas_call(terms_kernel, out_shape=pltpu.VMEM((ROWS, COLS), jnp.bfloa...  1.62 us
    ppermute x1, waiting for transfers between devices, local(): lax.ppermute(outer, both, swap_pairs(n_slabs, n_doms, 1, lambda s: True))  1.34 us
    ppermute x1, waiting for transfers between devices, local(): other = lax.ppermute(other, 'dom', [(i, i ^ 1) for i in range(n_doms)])  0.9 us
    pallas_call x1, Pallas kernels, make_send(): pl.pallas_call(send_kernel, out_shape=(message,) * 3, in_specs=[vmem], ou...  0.89 us
  transfers between devices with their start and end apart: 4, of which 2 were waited for; matrix products, arithmetic and copies ran while one was open for 0% of the time, Pallas kernels for 2%

profile of v5, /device:TPU:1, one launch (start us, length us, event | category | flops | bytes accessed | tf_op | source)
XLA Modules:
  0.0 44.1 jit_solution(10307602627950418281)
XLA Ops:
  0.7 1.6 %terms.1 = bf16[80,640]{1,0:T(8,128)(2,1)S(1)} custom-call(s32[1,1]{1,0:T(1,128)S(6)} %copy.6.count_ref, s32[1,32]{1,0:T(1,128)} %tile_hbm.1, s32[1,32]{1,0:T(1,128)} %slab_hbm.1, bf16[32,64,128]{2,1,0:T(8,128)(2,1)} %bitcast.4, bf16[10,32,128]{2,1,0:T(8,128)(2,1)} %bitcast.5), custom_call_target="tpu_custom_call" | custom-call | tf_op jit(solution)/shard_map/terms/pallas_call | solution.py:259
  2.3 22.3 %all_gather.3.x_ref = bf16[640,640]{1,0:T(8,128)(2,1)S(1)} all-gather(bf16[80,640]{1,0:T(8,128)(2,1)S(1)} %terms.1), channel_id=1, replica_groups=mesh['dom'=8,'slab'=64] {'dom'}, dimensions={0}, use_global_device_ids=true | all-gather | bytes 921600 | tf_op jit(solution)/shard_map/all_gather | solution.py:308
  24.6 0.9 %send.1 = (s16[42,8,128]{2,1,0:T(8,128)(2,1)S(1)}, s16[42,8,128]{2,1,0:T(8,128)(2,1)S(1)}, s16[42,8,128]{2,1,0:T(8,128)(2,1)S(1)}) custom-call(bf16[640,640]{1,0:T(8,128)(2,1)S(1)} %all_gather.3.x_ref), custom_call_target="tpu_custom_call" | custom-call | tf_op jit(solution)/shard_map/send/pallas_call | solution.py:280
  25.5 1.9 %collective-permute-start = (s16[42,8,128]{2,1,0:T(8,128)(2,1)S(1)}, s16[42,8,128]{2,1,0:T(8,128)(2,1)S(1)}, u32[]{:S(2)}, u32[]{:S(2)}) collective-permute-start(s16[42,8,128]{2,1,0:T(8,128)(2,1)S(1)} %get-tuple-element.14), channel_id=1, source_target_pairs={{0,2},{64,65},{128,130},{192,193},{256,258},{320,321},{384,386},{4... | collective-permute-start | bytes 258056 | tf_op jit(solution)/shard_map/ppermute | solution.py:312
  27.5 9.4 %collective-permute-start.1 = (s16[42,8,128]{2,1,0:T(8,128)(2,1)S(1)}, s16[42,8,128]{2,1,0:T(8,128)(2,1)S(1)}, u32[]{:S(2)}, u32[]{:S(2)}) collective-permute-start(s16[42,8,128]{2,1,0:T(8,128)(2,1)S(1)} %get-tuple-element.15), channel_id=1, source_target_pairs={{0,62},{64,127},{128,190},{192,255},{256,318},{320,383},{384,446},... | collective-permute-start | bytes 258056 | tf_op jit(solution)/shard_map/ppermute | solution.py:313
  36.9 0.7 %collective-permute-start.2 = (s16[42,8,128]{2,1,0:T(8,128)(2,1)S(1)}, s16[42,8,128]{2,1,0:T(8,128)(2,1)S(1)}, u32[]{:S(2)}, u32[]{:S(2)}) collective-permute-start(s16[42,8,128]{2,1,0:T(8,128)(2,1)S(1)} %get-tuple-element.16), channel_id=1, source_target_pairs={{16,18},{80,81},{144,146},{208,209},{272,274},{336,337},{400,402},... | collective-permute-start | bytes 258056 | tf_op jit(solution)/shard_map/ppermute | solution.py:314
  37.6 0.8 %own.1.own_ref = f32[10,2,8,128]{3,2,1,0:T(8,128)S(1)} custom-call(bf16[640,640]{1,0:T(8,128)(2,1)S(1)} %all_gather.3.x_ref), custom_call_target="tpu_custom_call" | custom-call | flops 400000000 | bytes 8000000 | tf_op jit(solution)/shard_map/own/pallas_call | solution.py:292
  38.4 0.0 collective-permute-done.early_ref
  38.4 1.3 %collective-permute-done.1.outer_ref = s16[42,8,128]{2,1,0:T(8,128)(2,1)S(1)} collective-permute-done((s16[42,8,128]{2,1,0:T(8,128)(2,1)S(1)}, s16[42,8,128]{2,1,0:T(8,128)(2,1)S(1)}, u32[]{:S(2)}, u32[]{:S(2)}) %collective-permute-start.1) | collective-permute-done | bytes 86048 | tf_op jit(solution)/shard_map/ppermute | solution.py:313
  39.7 0.0 collective-permute-done.2.late_ref
  39.7 0.1 join.1
  39.8 2.8 %collective-permute-start.3 = (f32[10,2,8,128]{3,2,1,0:T(8,128)S(1)}, f32[10,2,8,128]{3,2,1,0:T(8,128)S(1)}, u32[]{:S(2)}, u32[]{:S(2)}) collective-permute-start(f32[10,2,8,128]{3,2,1,0:T(8,128)S(1)} %get-tuple-element.22), channel_id=1, source_target_pairs={{0,64},{64,0},{128,192},{192,128},{256,320},{320,256},{384,448},{4... | collective-permute-start | bytes 245768 | tf_op jit(solution)/shard_map/ppermute | solution.py:326
  42.6 0.9 %collective-permute-done.3 = f32[10,2,8,128]{3,2,1,0:T(8,128)S(1)} collective-permute-done((f32[10,2,8,128]{3,2,1,0:T(8,128)S(1)}, f32[10,2,8,128]{3,2,1,0:T(8,128)S(1)}, u32[]{:S(2)}, u32[]{:S(2)}) %collective-permute-start.3) | collective-permute-done | bytes 81952 | tf_op jit(solution)/shard_map/ppermute | solution.py:326
  43.5 0.6 %add.3 = f32[10,2,8,128]{3,2,1,0:T(8,128)} add(f32[10,2,8,128]{3,2,1,0:T(8,128)S(1)} %get-tuple-element.21, f32[10,2,8,128]{3,2,1,0:T(8,128)S(1)} %collective-permute-done.3) | non-fusion elementwise | flops 20480 | bytes 245760 | tf_op jit(solution)/shard_map/add | solution.py:327
Async XLA Ops:
  25.5 12.8 %collective-permute-start = (s16[42,8,128]{2,1,0:T(8,128)(2,1)S(1)}, s16[42,8,128]{2,1,0:T(8,128)(2,1)S(1)}, u32[]{:S(2)}, u32[]{:S(2)}) collective-permute-start(s16[42,8,128]{2,1,0:T(8,128)(2,1)S(1)} %get-tuple-element.14), channel_id=1, source_target_pairs={{0,2},{64,65},{128,130},{192,193},{256,258},{320,321},{384,386},{4... | collective-permute-start | bytes 258056 | tf_op jit(solution)/shard_map/ppermute | solution.py:312
  27.5 12.2 %collective-permute-start.1 = (s16[42,8,128]{2,1,0:T(8,128)(2,1)S(1)}, s16[42,8,128]{2,1,0:T(8,128)(2,1)S(1)}, u32[]{:S(2)}, u32[]{:S(2)}) collective-permute-start(s16[42,8,128]{2,1,0:T(8,128)(2,1)S(1)} %get-tuple-element.15), channel_id=1, source_target_pairs={{0,62},{64,127},{128,190},{192,255},{256,318},{320,383},{384,446},... | collective-permute-start | bytes 258056 | tf_op jit(solution)/shard_map/ppermute | solution.py:313
  36.9 2.8 %collective-permute-start.2 = (s16[42,8,128]{2,1,0:T(8,128)(2,1)S(1)}, s16[42,8,128]{2,1,0:T(8,128)(2,1)S(1)}, u32[]{:S(2)}, u32[]{:S(2)}) collective-permute-start(s16[42,8,128]{2,1,0:T(8,128)(2,1)S(1)} %get-tuple-element.16), channel_id=1, source_target_pairs={{16,18},{80,81},{144,146},{208,209},{272,274},{336,337},{400,402},... | collective-permute-start | bytes 258056 | tf_op jit(solution)/shard_map/ppermute | solution.py:314
  39.8 3.7 %collective-permute-start.3 = (f32[10,2,8,128]{3,2,1,0:T(8,128)S(1)}, f32[10,2,8,128]{3,2,1,0:T(8,128)S(1)}, u32[]{:S(2)}, u32[]{:S(2)}) collective-permute-start(f32[10,2,8,128]{3,2,1,0:T(8,128)S(1)} %get-tuple-element.22), channel_id=1, source_target_pairs={{0,64},{64,0},{128,192},{192,128},{256,320},{320,256},{384,448},{4... | collective-permute-start | bytes 245768 | tf_op jit(solution)/shard_map/ppermute | solution.py:326

commit v6 on v5

--- a/solution.py
+++ b/solution.py
@@ -17,9 +17,9 @@
 HALO = 4
 WIN = CHIP_ROWS + 2 * HALO
 PLANES = 4
-ROWS = 80
+ROWS = 40
 COLS = MOM * TC
-KEPT = 8 * 2 * BLK
+KEPT = 8 * BLK
 CHUNKS = 2
 GROUP = 4
 diffusion = 0.16
@@ -32,6 +32,10 @@
 
 def fixed_factor(top):
     return jnp.exp2(14.9 - top)
+
+
+def power(exponent):
+    return jnp.exp2(exponent).astype(jnp.bfloat16).astype(jnp.float32)
 
 
 def terms_kernel(
@@ -67,10 +71,9 @@
     both = jnp.where(iota((8, BLK), 0) == 0, code, half).astype(jnp.bfloat16)
     slot = iota((BLK, COLS), 0)
     slot = lax.shift_right_logical(slot, 1) + (slot & 1) * (BLK // 2)
-    lane = iota((BLK, COLS), 1) - my_dom * 2 * BLK
-    spread = jnp.where((lane == slot) | (lane == slot + BLK), 1.0, 0.0).astype(jnp.bfloat16)
-    codes = jnp.dot(both, spread, preferred_element_type=jnp.float32).astype(jnp.bfloat16)
-    out_ref[2 * BLK : ROWS, :] = jnp.concatenate([codes, codes], axis=0)
+    lane = iota((BLK, COLS), 1) - my_dom * BLK
+    spread = jnp.where(lane == slot, 1.0, 0.0).astype(jnp.bfloat16)
+    codes = jnp.dot(both, spread, preferred_element_type=jnp.float32)
     low_half = iota((16, NZ), 1) < TC
     for b in range(0, BLK, GROUP):
         if b % size == 0:
@@ -83,6 +86,7 @@
             cols = slice(TC * i, TC * (i + 2))
             pair = jnp.where(low_half, term[16 * i : 16 * i + 16, cols], term[16 * i + 16 : 16 * i + 32, cols])
             term_ref[8 * (b + i) : 8 * (b + i) + 16, :] = pair
+    terms = []
     for j in range(MOM // 2):
         even = term_ref[pl.ds(2 * j, BLK // 2, stride=16), :]
         odd = term_ref[pl.ds(2 * j + 1, BLK // 2, stride=16), :]
@@ -90,27 +94,37 @@
             jnp.where(low_half, even, pltpu.roll(odd, TC, 1)),
             jnp.where(low_half, pltpu.roll(even, TC, 1), odd),
         )
-        term = jnp.concatenate(rows, axis=0)
-        high = term.astype(jnp.bfloat16)
-        low = (term - high.astype(jnp.float32)).astype(jnp.bfloat16)
-        out_ref[0:BLK, NZ * j : NZ * (j + 1)] = high
-        out_ref[BLK : 2 * BLK, NZ * j : NZ * (j + 1)] = low
+        terms.append(jnp.concatenate(rows, axis=0))
+    top = functools.reduce(jnp.maximum, [jnp.abs(term) for term in terms])
+    top = jnp.max(top, axis=1, keepdims=True)
+    top = jnp.floor(jnp.log2(jnp.maximum(top, 1e-30))) + 1.0
+    factor = power(15.0 - top)
+    for j, term in enumerate(terms):
+        q = jnp.clip(jnp.floor(term * factor + 0.5), -32767.0, 32767.0)
+        out_ref[0:BLK, NZ * j : NZ * (j + 1)] = q.astype(jnp.int32).astype(jnp.int16)
+    tops = jnp.sum(jnp.where(lane == iota((BLK, COLS), 0), top, 0.0), axis=0, keepdims=True)
+    codes = jnp.where(iota((8, COLS), 0) == 2, tops, codes)
+    out_ref[BLK:ROWS, :] = codes.astype(jnp.int32).astype(jnp.int16)
 
 
 def deposit(x_ref, top_row):
-    codes = x_ref[2 * BLK : ROWS, :].astype(jnp.float32)
-    for k in range(1, 8):
-        codes += x_ref[ROWS * k + 2 * BLK : ROWS * (k + 1), :].astype(jnp.float32)
-    code = codes[0:1, :KEPT].astype(jnp.int32) - 1
-    half = codes[1:2, :KEPT].astype(jnp.int32)
+    codes = functools.reduce(
+        jnp.add, [x_ref[ROWS * k + BLK : ROWS * (k + 1), :KEPT].astype(jnp.int32) for k in range(8)]
+    )
+    code = codes[0:1, :] - 1
+    half = codes[1:2, :]
+    scale = power(codes[2:3, :].astype(jnp.float32) - 15.0)
     plane = lax.shift_right_arithmetic(code, 6)
     rel = (code & (NY - 1)) - top_row
     valid = (code >= 0) & (rel >= -HALO) & (rel < CHIP_ROWS + HALO)
     spot = (half * PLANES + plane) * WIN + jnp.where(rel < 0, rel + WIN, rel)
     spot = jnp.where(valid, spot, -1)
-    chosen = jnp.where(iota((2 * PLANES * WIN, KEPT), 0) == spot, 1.0, 0.0).astype(jnp.bfloat16)
-    terms = jnp.concatenate([x_ref[ROWS * k : ROWS * k + 2 * BLK, :] for k in range(8)], axis=0)
-    return jnp.dot(chosen, terms, preferred_element_type=jnp.float32)
+    chosen = jnp.where(iota((2 * PLANES * WIN, KEPT), 0) == spot, scale, 0.0)
+    chosen = jnp.concatenate([256.0 * chosen, chosen], axis=1).astype(jnp.bfloat16)
+    terms = [x_ref[ROWS * k : ROWS * k + BLK, :].astype(jnp.int32) for k in range(8)]
+    high = [lax.shift_right_arithmetic(q, 8).astype(jnp.float32).astype(jnp.bfloat16) for q in terms]
+    low = [(q & 255).astype(jnp.float32).astype(jnp.bfloat16) for q in terms]
+    return jnp.dot(chosen, jnp.concatenate(high + low, axis=0), preferred_element_type=jnp.float32)
 
 
 class Stencil:
@@ -258,7 +272,7 @@
 def make_terms(weights, moments, block_tile, block_slab, block_count):
     return pl.pallas_call(
         terms_kernel,
-        out_shape=pltpu.VMEM((ROWS, COLS), jnp.bfloat16),
+        out_shape=pltpu.VMEM((ROWS, COLS), jnp.int16),
         in_specs=[smem] + [hbm] * 4,
         out_specs=vmem,
         scratch_shapes=[

time: 44.3 us -> 43.1 us (0.973)
  blocking collectives: 22.3 us -> 21.5 us
  starting transfers between devices: 14.8 us -> 14.2 us
    all_gather x1, blocking collectives: 22.3 us -> 21.5 us  [local(): gathered = lax.all_gather(x, 'dom', tiled=True)]
    ppermute x1, starting transfers between devices: 9.43 us -> 8.96 us  [local(): lax.ppermute(outer, both, swap_pairs(n_slabs, n_doms, 1, lambda s: True))]
where the time goes in v6:
time: 43.1 us; the launch traced here: 42.9 us
  blocking collectives  21.5 us (50%)
  starting transfers between devices  14.2 us (33%)
  Pallas kernels  3.63 us (8%)
  waiting for transfers between devices  2.25 us (5%)
  between operations  0.72 us (2%)
  other arithmetic  0.65 us (2%)
    all_gather x1, blocking collectives, local(): gathered = lax.all_gather(x, 'dom', tiled=True)  21.5 us
    ppermute x1, starting transfers between devices, local(): lax.ppermute(outer, both, swap_pairs(n_slabs, n_doms, 1, lambda s: True))  8.96 us
    ppermute x1, starting transfers between devices, local(): other = lax.ppermute(other, 'dom', [(i, i ^ 1) for i in range(n_doms)])  2.63 us
    ppermute x1, starting transfers between devices, local(): lax.ppermute(early, both, swap_pairs(n_slabs, n_doms, 0, half(True)))  1.92 us
    pallas_call x1, Pallas kernels, make_terms(): pl.pallas_call(terms_kernel, out_shape=pltpu.VMEM((ROWS, COLS), jnp.int16...  1.74 us
    ppermute x1, waiting for transfers between devices, local(): lax.ppermute(outer, both, swap_pairs(n_slabs, n_doms, 1, lambda s: True))  1.34 us
    pallas_call x1, Pallas kernels, make_send(): pl.pallas_call(send_kernel, out_shape=(message,) * 3, in_specs=[vmem], ou...  0.95 us
    ppermute x1, waiting for transfers between devices, local(): other = lax.ppermute(other, 'dom', [(i, i ^ 1) for i in range(n_doms)])  0.9 us
  transfers between devices with their start and end apart: 4, of which 2 were waited for; matrix products, arithmetic and copies ran while one was open for 0% of the time, Pallas kernels for 2%

profile of v6, /device:TPU:1, one launch (start us, length us, event | category | flops | bytes accessed | tf_op | source)
XLA Modules:
  0.0 42.9 jit_solution(10724201612557670131)
XLA Ops:
  0.7 1.7 %terms.1 = s16[40,640]{1,0:T(8,128)(2,1)S(1)} custom-call(s32[1,1]{1,0:T(1,128)S(6)} %copy.6.count_ref, s32[1,32]{1,0:T(1,128)} %tile_hbm.1, s32[1,32]{1,0:T(1,128)} %slab_hbm.1, bf16[32,64,128]{2,1,0:T(8,128)(2,1)} %bitcast.4, bf16[10,32,128]{2,1,0:T(8,128)(2,1)} %bitcast.5), custom_call_target="tpu_custom_call" | custom-call | tf_op jit(solution)/shard_map/terms/pallas_call | solution.py:273
  2.4 21.5 %all_gather.3.x_ref = s16[320,640]{1,0:T(8,128)(2,1)S(1)} all-gather(s16[40,640]{1,0:T(8,128)(2,1)S(1)} %terms.1), channel_id=1, replica_groups=mesh['dom'=8,'slab'=64] {'dom'}, dimensions={0}, use_global_device_ids=true | all-gather | bytes 460800 | tf_op jit(solution)/shard_map/all_gather | solution.py:322
  23.9 1.0 %send.1 = (s16[42,8,128]{2,1,0:T(8,128)(2,1)S(1)}, s16[42,8,128]{2,1,0:T(8,128)(2,1)S(1)}, s16[42,8,128]{2,1,0:T(8,128)(2,1)S(1)}) custom-call(s16[320,640]{1,0:T(8,128)(2,1)S(1)} %all_gather.3.x_ref), custom_call_target="tpu_custom_call" | custom-call | tf_op jit(solution)/shard_map/send/pallas_call | solution.py:294
  24.9 1.9 %collective-permute-start = (s16[42,8,128]{2,1,0:T(8,128)(2,1)S(1)}, s16[42,8,128]{2,1,0:T(8,128)(2,1)S(1)}, u32[]{:S(2)}, u32[]{:S(2)}) collective-permute-start(s16[42,8,128]{2,1,0:T(8,128)(2,1)S(1)} %get-tuple-element.14), channel_id=1, source_target_pairs={{0,2},{64,65},{128,130},{192,193},{256,258},{320,321},{384,386},{4... | collective-permute-start | bytes 258056 | tf_op jit(solution)/shard_map/ppermute | solution.py:326
  26.8 9.0 %collective-permute-start.1 = (s16[42,8,128]{2,1,0:T(8,128)(2,1)S(1)}, s16[42,8,128]{2,1,0:T(8,128)(2,1)S(1)}, u32[]{:S(2)}, u32[]{:S(2)}) collective-permute-start(s16[42,8,128]{2,1,0:T(8,128)(2,1)S(1)} %get-tuple-element.15), channel_id=1, source_target_pairs={{0,62},{64,127},{128,190},{192,255},{256,318},{320,383},{384,446},... | collective-permute-start | bytes 258056 | tf_op jit(solution)/shard_map/ppermute | solution.py:327
  35.8 0.7 %collective-permute-start.2 = (s16[42,8,128]{2,1,0:T(8,128)(2,1)S(1)}, s16[42,8,128]{2,1,0:T(8,128)(2,1)S(1)}, u32[]{:S(2)}, u32[]{:S(2)}) collective-permute-start(s16[42,8,128]{2,1,0:T(8,128)(2,1)S(1)} %get-tuple-element.16), channel_id=1, source_target_pairs={{16,18},{80,81},{144,146},{208,209},{272,274},{336,337},{400,402},... | collective-permute-start | bytes 258056 | tf_op jit(solution)/shard_map/ppermute | solution.py:328
  36.4 0.9 %own.1.own_ref = f32[10,2,8,128]{3,2,1,0:T(8,128)S(1)} custom-call(s16[320,640]{1,0:T(8,128)(2,1)S(1)} %all_gather.3.x_ref), custom_call_target="tpu_custom_call" | custom-call | flops 400000000 | bytes 8000000 | tf_op jit(solution)/shard_map/own/pallas_call | solution.py:306
  37.3 0.0 collective-permute-done.early_ref
  37.3 1.3 %collective-permute-done.1.outer_ref = s16[42,8,128]{2,1,0:T(8,128)(2,1)S(1)} collective-permute-done((s16[42,8,128]{2,1,0:T(8,128)(2,1)S(1)}, s16[42,8,128]{2,1,0:T(8,128)(2,1)S(1)}, u32[]{:S(2)}, u32[]{:S(2)}) %collective-permute-start.1) | collective-permute-done | bytes 86048 | tf_op jit(solution)/shard_map/ppermute | solution.py:327
  38.7 0.0 collective-permute-done.2.late_ref
  38.7 0.1 join.1
  38.7 2.6 %collective-permute-start.3 = (f32[10,2,8,128]{3,2,1,0:T(8,128)S(1)}, f32[10,2,8,128]{3,2,1,0:T(8,128)S(1)}, u32[]{:S(2)}, u32[]{:S(2)}) collective-permute-start(f32[10,2,8,128]{3,2,1,0:T(8,128)S(1)} %get-tuple-element.22), channel_id=1, source_target_pairs={{0,64},{64,0},{128,192},{192,128},{256,320},{320,256},{384,448},{4... | collective-permute-start | bytes 245768 | tf_op jit(solution)/shard_map/ppermute | solution.py:340
  41.4 0.9 %collective-permute-done.3 = f32[10,2,8,128]{3,2,1,0:T(8,128)S(1)} collective-permute-done((f32[10,2,8,128]{3,2,1,0:T(8,128)S(1)}, f32[10,2,8,128]{3,2,1,0:T(8,128)S(1)}, u32[]{:S(2)}, u32[]{:S(2)}) %collective-permute-start.3) | collective-permute-done | bytes 81952 | tf_op jit(solution)/shard_map/ppermute | solution.py:340
  42.3 0.6 %add.3 = f32[10,2,8,128]{3,2,1,0:T(8,128)} add(f32[10,2,8,128]{3,2,1,0:T(8,128)S(1)} %get-tuple-element.21, f32[10,2,8,128]{3,2,1,0:T(8,128)S(1)} %collective-permute-done.3) | non-fusion elementwise | flops 20480 | bytes 245760 | tf_op jit(solution)/shard_map/add | solution.py:341
Async XLA Ops:
  24.9 12.4 %collective-permute-start = (s16[42,8,128]{2,1,0:T(8,128)(2,1)S(1)}, s16[42,8,128]{2,1,0:T(8,128)(2,1)S(1)}, u32[]{:S(2)}, u32[]{:S(2)}) collective-permute-start(s16[42,8,128]{2,1,0:T(8,128)(2,1)S(1)} %get-tuple-element.14), channel_id=1, source_target_pairs={{0,2},{64,65},{128,130},{192,193},{256,258},{320,321},{384,386},{4... | collective-permute-start | bytes 258056 | tf_op jit(solution)/shard_map/ppermute | solution.py:326
  26.8 11.8 %collective-permute-start.1 = (s16[42,8,128]{2,1,0:T(8,128)(2,1)S(1)}, s16[42,8,128]{2,1,0:T(8,128)(2,1)S(1)}, u32[]{:S(2)}, u32[]{:S(2)}) collective-permute-start(s16[42,8,128]{2,1,0:T(8,128)(2,1)S(1)} %get-tuple-element.15), channel_id=1, source_target_pairs={{0,62},{64,127},{128,190},{192,255},{256,318},{320,383},{384,446},... | collective-permute-start | bytes 258056 | tf_op jit(solution)/shard_map/ppermute | solution.py:327
  35.8 2.9 %collective-permute-start.2 = (s16[42,8,128]{2,1,0:T(8,128)(2,1)S(1)}, s16[42,8,128]{2,1,0:T(8,128)(2,1)S(1)}, u32[]{:S(2)}, u32[]{:S(2)}) collective-permute-start(s16[42,8,128]{2,1,0:T(8,128)(2,1)S(1)} %get-tuple-element.16), channel_id=1, source_target_pairs={{16,18},{80,81},{144,146},{208,209},{272,274},{336,337},{400,402},... | collective-permute-start | bytes 258056 | tf_op jit(solution)/shard_map/ppermute | solution.py:328
  38.7 3.5 %collective-permute-start.3 = (f32[10,2,8,128]{3,2,1,0:T(8,128)S(1)}, f32[10,2,8,128]{3,2,1,0:T(8,128)S(1)}, u32[]{:S(2)}, u32[]{:S(2)}) collective-permute-start(f32[10,2,8,128]{3,2,1,0:T(8,128)S(1)} %get-tuple-element.22), channel_id=1, source_target_pairs={{0,64},{64,0},{128,192},{192,128},{256,320},{320,256},{384,448},{4... | collective-permute-start | bytes 245768 | tf_op jit(solution)/shard_map/ppermute | solution.py:340

commit v7 on v6

--- a/solution.py
+++ b/solution.py
@@ -97,7 +97,7 @@
         terms.append(jnp.concatenate(rows, axis=0))
     top = functools.reduce(jnp.maximum, [jnp.abs(term) for term in terms])
     top = jnp.max(top, axis=1, keepdims=True)
-    top = jnp.floor(jnp.log2(jnp.maximum(top, 1e-30))) + 1.0
+    top = jnp.floor(jnp.log2(jnp.maximum(top, 1e-33))) + 1.0
     factor = power(15.0 - top)
     for j, term in enumerate(terms):
         q = jnp.clip(jnp.floor(term * factor + 0.5), -32767.0, 32767.0)
@@ -107,7 +107,7 @@
     out_ref[BLK:ROWS, :] = codes.astype(jnp.int32).astype(jnp.int16)
 
 
-def deposit(x_ref, top_row):
+def deposit(x_ref, top_row, flip):
     codes = functools.reduce(
         jnp.add, [x_ref[ROWS * k + BLK : ROWS * (k + 1), :KEPT].astype(jnp.int32) for k in range(8)]
     )
@@ -115,6 +115,8 @@
     half = codes[1:2, :]
     scale = power(codes[2:3, :].astype(jnp.float32) - 15.0)
     plane = lax.shift_right_arithmetic(code, 6)
+    if flip is not False:
+        plane = jnp.where(flip, PLANES - 1 - plane, plane)
     rel = (code & (NY - 1)) - top_row
     valid = (code >= 0) & (rel >= -HALO) & (rel < CHIP_ROWS + HALO)
     spot = (half * PLANES + plane) * WIN + jnp.where(rel < 0, rel + WIN, rel)
@@ -158,81 +160,75 @@
         return jnp.where(self.inside, f, 0.0)
 
 
-def send_kernel(x_ref, early_ref, outer_ref, late_ref, part_ref):
+def make_message(planes_of, st, core, far_up, near_up, ref, part_ref):
+    for m in range(MOM):
+        g0, g1, g2, g3 = planes_of(m)
+        l0 = st.flat(g0)
+        once0 = st.kept(l0 + diffusion * g1)
+        once1 = st.kept(st.flat(g1) + diffusion * (g0 + g2))
+        parts = (
+            diffusion * diffusion * g0,
+            diffusion * (l0 + once0),
+            st.flat(once0) + diffusion * (diffusion * g0 + once1),
+            diffusion * diffusion * g3,
+        )
+        for i, f in enumerate(parts):
+            part_ref[i, m, 0] = f[0:RY]
+            part_ref[i, m, 1] = f[RY : 2 * RY]
+    part_ref[4] = jnp.zeros((MOM, 2, RY, NZ), jnp.float32)
+    a = jnp.where(core == 1, jnp.where(near_up, 2, 1), jnp.where(far_up, jnp.where(near_up, 0, 3), 4))
+    b = jnp.where(core == 1, jnp.where(near_up, 1, 2), jnp.where(far_up, 4, jnp.where(near_up, 3, 0)))
+    sub = iota((RY, NZ), 0)
+    tops = [jnp.zeros((RY, NZ), jnp.float32)] * 2
+    for m in range(MOM):
+        values = [part_ref[i, m, h] for h in range(2) for i in (a, b)]
+        top = functools.reduce(jnp.maximum, [jnp.abs(v) for v in values])
+        for k in (4, 2, 1):
+            top = jnp.maximum(top, pltpu.roll(top, k, 0))
+        top = jnp.floor(jnp.log2(jnp.maximum(top, 1e-33))) + 1.0
+        factor = fixed_factor(top)
+        tops[m // RY] = jnp.where(sub == m % RY, top, tops[m // RY])
+        for k, v in enumerate(values):
+            ref[4 * m + k] = jnp.floor(v * factor + 0.5).astype(jnp.int32).astype(jnp.int16)
+    for k in range(2):
+        ref[4 * MOM + k] = tops[k].astype(jnp.int32).astype(jnp.int16)
+
+
+def where_am_i():
     my_slab, my_dom = lax.axis_index("slab"), lax.axis_index("dom")
     core = lax.rem(my_dom, 2)
-    top_row = (my_dom - core) * RY
-    cells = deposit(x_ref, top_row)
+    odd = lax.rem(my_slab, 2) == 1
+    upper = lax.rem(lax.div(my_slab, 2), 2) == 1
+    early = lax.rem(lax.div(my_slab, 4), 8) < 4
+    return core, (my_dom - core) * RY, odd, upper, early
+
+
+def send_kernel(x_ref, early_ref, outer_ref, part_ref):
+    core, top_row, odd, upper, early = where_am_i()
+    cells = deposit(x_ref, top_row, odd)
     st = Stencil(top_row)
-
-    def put(i, m, f):
-        part_ref[i, m, 0] = f[0:RY]
-        part_ref[i, m, 1] = f[RY : 2 * RY]
-
-    for m in range(MOM):
-        g = st.planes(cells, m)
-        put(0, m, diffusion * diffusion * g[0])
-        put(5, m, diffusion * diffusion * g[3])
-
-        def near(g0, g1, g2, i_far, i_near):
-            l0 = st.flat(g0)
-            once0 = st.kept(l0 + diffusion * g1)
-            once1 = st.kept(st.flat(g1) + diffusion * (g0 + g2))
-            put(i_far, m, diffusion * (l0 + once0))
-            put(i_near, m, st.flat(once0) + diffusion * (diffusion * g0 + once1))
-
-        near(g[0], g[1], g[2], 1, 2)
-        near(g[3], g[2], g[1], 4, 3)
-    part_ref[6] = jnp.zeros((MOM, 2, RY, NZ), jnp.float32)
-
-    sub = iota((RY, NZ), 0)
-    for refs, odd_up in (((outer_ref,), 1), ((early_ref, late_ref), 0)):
-        near_up = lax.rem(my_slab, 2) == odd_up
-        far_up = lax.rem(lax.div(my_slab, 2), 2) == odd_up
-        at = jnp.where(near_up, 3, 1)
-        a = jnp.where(core == 1, at, jnp.where(far_up, 5, 6))
-        b = jnp.where(core == 1, at + 1, jnp.where(far_up, 6, 0))
-        tops = [jnp.zeros((RY, NZ), jnp.float32)] * 2
-        for m in range(MOM):
-            values = [part_ref[i, m, h] for h in range(2) for i in (a, b)]
-            top = functools.reduce(jnp.maximum, [jnp.abs(v) for v in values])
-            for k in (4, 2, 1):
-                top = jnp.maximum(top, pltpu.roll(top, k, 0))
-            top = jnp.floor(jnp.log2(jnp.maximum(top, 1e-30))) + 1.0
-            factor = fixed_factor(top)
-            tops[m // RY] = jnp.where(sub == m % RY, top, tops[m // RY])
-            for k, v in enumerate(values):
-                q = jnp.floor(v * factor + 0.5).astype(jnp.int32).astype(jnp.int16)
-                for ref in refs:
-                    ref[4 * m + k] = q
-        for k in range(2):
-            q = tops[k].astype(jnp.int32).astype(jnp.int16)
-            for ref in refs:
-                ref[4 * MOM + k] = q
-
-
-def join_kernel(early_ref, outer_ref, late_ref, own_ref, mine_ref, other_ref):
-    core = lax.rem(lax.axis_index("dom"), 2)
-    refs = (early_ref, outer_ref, late_ref)
-    tops = [[ref[4 * MOM + k].astype(jnp.float32) for k in range(2)] for ref in refs]
-    for m in range(MOM):
-        at = m % RY
-        scales = [1.0 / fixed_factor(top[m // RY][at : at + 1]) for top in tops]
-        for p in range(2):
-
-            def arrived(h):
-                parts = [ref[4 * m + 2 * h + p].astype(jnp.float32) * c for ref, c in zip(refs, scales)]
-                return parts[0] + parts[1] + parts[2]
-
-            other_ref[m, p] = arrived(1 - core)
-            mine_ref[m, p] = own_ref[m, p] + arrived(core)
+    make_message(lambda m: st.planes(cells, m), st, core, upper, odd, outer_ref, part_ref)
+
+    @pl.when(early)
+    def _():
+        inner = lambda m: st.planes(cells, m)[::-1]
+        make_message(inner, st, core, jnp.logical_not(upper), jnp.logical_not(odd), early_ref, part_ref)
+
+
+def late_kernel(x_ref, late_ref, part_ref):
+    core, top_row, odd, upper, early = where_am_i()
+
+    @pl.when(jnp.logical_not(early))
+    def _():
+        cells = deposit(x_ref, top_row, jnp.logical_not(odd))
+        st = Stencil(top_row)
+        planes = lambda m: st.planes(cells, m)
+        make_message(planes, st, core, jnp.logical_not(upper), jnp.logical_not(odd), late_ref, part_ref)
 
 
 def own_kernel(x_ref, own_ref, part_ref):
-    my_dom = lax.axis_index("dom")
-    core = lax.rem(my_dom, 2)
-    top_row = (my_dom - core) * RY
-    cells = deposit(x_ref, top_row)
+    core, top_row, _, _, _ = where_am_i()
+    cells = deposit(x_ref, top_row, False)
     st = Stencil(top_row)
     for m in range(MOM):
         g = st.planes(cells, m)
@@ -246,6 +242,23 @@
             part_ref[m, p, 0] = f[0:RY]
             part_ref[m, p, 1] = f[RY : 2 * RY]
     own_ref[...] = part_ref[:, :, core]
+
+
+def join_kernel(early_ref, outer_ref, late_ref, own_ref, mine_ref, other_ref):
+    core = lax.rem(lax.axis_index("dom"), 2)
+    refs = (early_ref, outer_ref, late_ref)
+    tops = [[ref[4 * MOM + k].astype(jnp.float32) for k in range(2)] for ref in refs]
+    for m in range(MOM):
+        at = m % RY
+        scales = [1.0 / fixed_factor(top[m // RY][at : at + 1]) for top in tops]
+        for p in range(2):
+
+            def arrived(h):
+                parts = [ref[4 * m + 2 * h + p].astype(jnp.float32) * c for ref, c in zip(refs, scales)]
+                return parts[0] + parts[1] + parts[2]
+
+            other_ref[m, p] = arrived(1 - core)
+            mine_ref[m, p] = own_ref[m, p] + arrived(core)
 
 
 def swap_pairs(n_slabs, n_doms, odd_up, chosen):
@@ -289,28 +302,44 @@
     )(block_count, block_tile, block_slab, weights[0], moments[0].transpose(1, 0, 2))
 
 
+message = jax.ShapeDtypeStruct((4 * MOM + 2, RY, NZ), jnp.int16)
+part = jax.ShapeDtypeStruct((MOM, 2, RY, NZ), jnp.float32)
+
+
 def make_send(gathered):
-    message = jax.ShapeDtypeStruct((4 * MOM + 2, RY, NZ), jnp.int16)
     return pl.pallas_call(
         send_kernel,
-        out_shape=(message,) * 3,
+        out_shape=(message, message),
         in_specs=[vmem],
-        out_specs=(vmem,) * 3,
-        scratch_shapes=[pltpu.VMEM((7, MOM, 2, RY, NZ), jnp.float32)],
+        out_specs=(vmem, vmem),
+        scratch_shapes=[pltpu.VMEM((5, MOM, 2, RY, NZ), jnp.float32)],
         compiler_params=limited,
         name="send",
     )(gathered)
 
 
+def make_late(gathered):
+    return pl.pallas_call(
+        late_kernel,
+        out_shape=message,
+        in_specs=[vmem],
+        out_specs=vmem,
+        scratch_shapes=[pltpu.VMEM((5, MOM, 2, RY, NZ), jnp.float32)],
+        compiler_params=limited,
+        cost_estimate=pl.CostEstimate(flops=400_000_000, bytes_accessed=8_000_000, transcendentals=0),
+        name="late",
+    )(gathered)
+
+
 def make_own(gathered):
     return pl.pallas_call(
         own_kernel,
-        out_shape=jax.ShapeDtypeStruct((MOM, 2, RY, NZ), jnp.float32),
+        out_shape=part,
         in_specs=[vmem],
         out_specs=vmem,
         scratch_shapes=[pltpu.VMEM((MOM, 2, 2, RY, NZ), jnp.float32)],
+        compiler_params=limited,
         cost_estimate=pl.CostEstimate(flops=400_000_000, bytes_accessed=8_000_000, transcendentals=0),
-        compiler_params=limited,
         name="own",
     )(gathered)
 
@@ -320,15 +349,15 @@
     n_doms = lax.axis_size("dom")
     x = make_terms(weights, moments, block_tile, block_slab, block_count)
     gathered = lax.all_gather(x, "dom", tiled=True)
-    early, outer, late = make_send(gathered)
+    early, outer = make_send(gathered)
+    late = make_late(gathered)
+    own = make_own(gathered)
     both = ("dom", "slab")
     half = lambda low: lambda s: ((s // 4) % 8 < 4) == low
     early = lax.ppermute(early, both, swap_pairs(n_slabs, n_doms, 0, half(True)))
     outer = lax.ppermute(outer, both, swap_pairs(n_slabs, n_doms, 1, lambda s: True))
     late = lax.ppermute(late, both, swap_pairs(n_slabs, n_doms, 0, half(False)))
-    own = make_own(gathered)
     early, outer, late, own = lax.optimization_barrier((early, outer, late, own))
-    part = jax.ShapeDtypeStruct((MOM, 2, RY, NZ), jnp.float32)
     mine, other = pl.pallas_call(
         join_kernel,
         out_shape=(part, part),

time: 43.1 us -> 42.9 us (level)
    pallas_call x2 -> x3, Pallas kernels: 1.81 us -> 1.96 us  [the longest x1 1.09 us: make_send(): pl.pallas_call(send_kernel, out_shape=(message, message), in_specs=[vmem]...]
where the time goes in v7:
time: 42.9 us; the launch traced here: 42.7 us
  blocking collectives  21.5 us (50%)
  starting transfers between devices  13.8 us (32%)
  Pallas kernels  3.78 us (9%)
  waiting for transfers between devices  2.22 us (5%)
  between operations  0.72 us (2%)
  other arithmetic  0.65 us (2%)
    all_gather x1, blocking collectives, local(): gathered = lax.all_gather(x, 'dom', tiled=True)  21.5 us
    ppermute x1, starting transfers between devices, local(): lax.ppermute(outer, both, swap_pairs(n_slabs, n_doms, 1, lambda s: True))  8.62 us
    ppermute x1, starting transfers between devices, local(): other = lax.ppermute(other, 'dom', [(i, i ^ 1) for i in range(n_doms)])  2.63 us
    ppermute x1, starting transfers between devices, local(): lax.ppermute(early, both, swap_pairs(n_slabs, n_doms, 0, half(True)))  1.92 us
    pallas_call x1, Pallas kernels, make_terms(): pl.pallas_call(terms_kernel, out_shape=pltpu.VMEM((ROWS, COLS), jnp.int16...  1.74 us
    ppermute x1, waiting for transfers between devices, local(): lax.ppermute(outer, both, swap_pairs(n_slabs, n_doms, 1, lambda s: True))  1.31 us
    pallas_call x1, Pallas kernels, make_send(): pl.pallas_call(send_kernel, out_shape=(message, message), in_specs=[vmem]...  1.09 us
    ppermute x1, waiting for transfers between devices, local(): other = lax.ppermute(other, 'dom', [(i, i ^ 1) for i in range(n_doms)])  0.9 us
  transfers between devices with their start and end apart: 4, of which 2 were waited for; matrix products, arithmetic and copies ran while one was open for 0% of the time, Pallas kernels for 2%

profile of v7, /device:TPU:1, one launch (start us, length us, event | category | flops | bytes accessed | tf_op | source)
XLA Modules:
  0.0 42.7 jit_solution(3817444434951708954)
XLA Ops:
  0.7 1.7 %terms.1 = s16[40,640]{1,0:T(8,128)(2,1)S(1)} custom-call(s32[1,1]{1,0:T(1,128)S(6)} %copy.6.count_ref, s32[1,32]{1,0:T(1,128)} %tile_hbm.1, s32[1,32]{1,0:T(1,128)} %slab_hbm.1, bf16[32,64,128]{2,1,0:T(8,128)(2,1)} %bitcast.4, bf16[10,32,128]{2,1,0:T(8,128)(2,1)} %bitcast.5), custom_call_target="tpu_custom_call" | custom-call | tf_op jit(solution)/shard_map/terms/pallas_call | solution.py:286
  2.4 21.5 %all_gather.3.x_ref = s16[320,640]{1,0:T(8,128)(2,1)S(1)} all-gather(s16[40,640]{1,0:T(8,128)(2,1)S(1)} %terms.1), channel_id=1, replica_groups=mesh['dom'=8,'slab'=64] {'dom'}, dimensions={0}, use_global_device_ids=true | all-gather | bytes 460800 | tf_op jit(solution)/shard_map/all_gather | solution.py:351
  23.9 1.1 %send.1 = (s16[42,8,128]{2,1,0:T(8,128)(2,1)S(1)}, s16[42,8,128]{2,1,0:T(8,128)(2,1)S(1)}) custom-call(s16[320,640]{1,0:T(8,128)(2,1)S(1)} %all_gather.3.x_ref), custom_call_target="tpu_custom_call" | custom-call | tf_op jit(solution)/shard_map/send/pallas_call | solution.py:310
  25.0 1.9 %collective-permute-start = (s16[42,8,128]{2,1,0:T(8,128)(2,1)S(1)}, s16[42,8,128]{2,1,0:T(8,128)(2,1)S(1)}, u32[]{:S(2)}, u32[]{:S(2)}) collective-permute-start(s16[42,8,128]{2,1,0:T(8,128)(2,1)S(1)} %get-tuple-element.13), channel_id=1, source_target_pairs={{0,2},{64,65},{128,130},{192,193},{256,258},{320,321},{384,386},{4... | collective-permute-start | bytes 258056 | tf_op jit(solution)/shard_map/ppermute | solution.py:357
  26.9 8.6 %collective-permute-start.1 = (s16[42,8,128]{2,1,0:T(8,128)(2,1)S(1)}, s16[42,8,128]{2,1,0:T(8,128)(2,1)S(1)}, u32[]{:S(2)}, u32[]{:S(2)}) collective-permute-start(s16[42,8,128]{2,1,0:T(8,128)(2,1)S(1)} %get-tuple-element.14), channel_id=1, source_target_pairs={{0,62},{64,127},{128,190},{192,255},{256,318},{320,383},{384,446},... | collective-permute-start | bytes 258056 | tf_op jit(solution)/shard_map/ppermute | solution.py:358
  35.6 0.7 %collective-permute-start.2 = (s16[42,8,128]{2,1,0:T(8,128)(2,1)S(1)}, s16[42,8,128]{2,1,0:T(8,128)(2,1)S(1)}, u32[]{:S(2)}, u32[]{:S(2)}) collective-permute-start(s16[42,8,128]{2,1,0:T(8,128)(2,1)S(1)} %late.1), channel_id=1, source_target_pairs={{16,18},{80,81},{144,146},{208,209},{272,274},{336,337},{400,402},... | collective-permute-start | bytes 258056 | tf_op jit(solution)/shard_map/ppermute | solution.py:359
  36.3 0.9 %own.1.own_ref = f32[10,2,8,128]{3,2,1,0:T(8,128)S(1)} custom-call(s16[320,640]{1,0:T(8,128)(2,1)S(1)} %all_gather.3.x_ref), custom_call_target="tpu_custom_call" | custom-call | flops 400000000 | bytes 8000000 | tf_op jit(solution)/shard_map/own/pallas_call | solution.py:335
  37.1 0.0 collective-permute-done.early_ref
  37.1 1.3 %collective-permute-done.1.outer_ref = s16[42,8,128]{2,1,0:T(8,128)(2,1)S(1)} collective-permute-done((s16[42,8,128]{2,1,0:T(8,128)(2,1)S(1)}, s16[42,8,128]{2,1,0:T(8,128)(2,1)S(1)}, u32[]{:S(2)}, u32[]{:S(2)}) %collective-permute-start.1) | collective-permute-done | bytes 86048 | tf_op jit(solution)/shard_map/ppermute | solution.py:358
  38.4 0.0 collective-permute-done.2.late_ref
  38.4 0.1 join.1
  38.5 2.6 %collective-permute-start.3 = (f32[10,2,8,128]{3,2,1,0:T(8,128)S(1)}, f32[10,2,8,128]{3,2,1,0:T(8,128)S(1)}, u32[]{:S(2)}, u32[]{:S(2)}) collective-permute-start(f32[10,2,8,128]{3,2,1,0:T(8,128)S(1)} %get-tuple-element.20), channel_id=1, source_target_pairs={{0,64},{64,0},{128,192},{192,128},{256,320},{320,256},{384,448},{4... | collective-permute-start | bytes 245768 | tf_op jit(solution)/shard_map/ppermute | solution.py:369
  41.2 0.9 %collective-permute-done.3 = f32[10,2,8,128]{3,2,1,0:T(8,128)S(1)} collective-permute-done((f32[10,2,8,128]{3,2,1,0:T(8,128)S(1)}, f32[10,2,8,128]{3,2,1,0:T(8,128)S(1)}, u32[]{:S(2)}, u32[]{:S(2)}) %collective-permute-start.3) | collective-permute-done | bytes 81952 | tf_op jit(solution)/shard_map/ppermute | solution.py:369
  42.1 0.6 %add.3 = f32[10,2,8,128]{3,2,1,0:T(8,128)} add(f32[10,2,8,128]{3,2,1,0:T(8,128)S(1)} %get-tuple-element.19, f32[10,2,8,128]{3,2,1,0:T(8,128)S(1)} %collective-permute-done.3) | non-fusion elementwise | flops 20480 | bytes 245760 | tf_op jit(solution)/shard_map/add | solution.py:370
  (1 shorter events, 0.0 us)
Async XLA Ops:
  25.0 12.1 %collective-permute-start = (s16[42,8,128]{2,1,0:T(8,128)(2,1)S(1)}, s16[42,8,128]{2,1,0:T(8,128)(2,1)S(1)}, u32[]{:S(2)}, u32[]{:S(2)}) collective-permute-start(s16[42,8,128]{2,1,0:T(8,128)(2,1)S(1)} %get-tuple-element.13), channel_id=1, source_target_pairs={{0,2},{64,65},{128,130},{192,193},{256,258},{320,321},{384,386},{4... | collective-permute-start | bytes 258056 | tf_op jit(solution)/shard_map/ppermute | solution.py:357
  26.9 11.5 %collective-permute-start.1 = (s16[42,8,128]{2,1,0:T(8,128)(2,1)S(1)}, s16[42,8,128]{2,1,0:T(8,128)(2,1)S(1)}, u32[]{:S(2)}, u32[]{:S(2)}) collective-permute-start(s16[42,8,128]{2,1,0:T(8,128)(2,1)S(1)} %get-tuple-element.14), channel_id=1, source_target_pairs={{0,62},{64,127},{128,190},{192,255},{256,318},{320,383},{384,446},... | collective-permute-start | bytes 258056 | tf_op jit(solution)/shard_map/ppermute | solution.py:358
  35.6 2.9 %collective-permute-start.2 = (s16[42,8,128]{2,1,0:T(8,128)(2,1)S(1)}, s16[42,8,128]{2,1,0:T(8,128)(2,1)S(1)}, u32[]{:S(2)}, u32[]{:S(2)}) collective-permute-start(s16[42,8,128]{2,1,0:T(8,128)(2,1)S(1)} %late.1), channel_id=1, source_target_pairs={{16,18},{80,81},{144,146},{208,209},{272,274},{336,337},{400,402},... | collective-permute-start | bytes 258056 | tf_op jit(solution)/shard_map/ppermute | solution.py:359
  38.5 3.5 %collective-permute-start.3 = (f32[10,2,8,128]{3,2,1,0:T(8,128)S(1)}, f32[10,2,8,128]{3,2,1,0:T(8,128)S(1)}, u32[]{:S(2)}, u32[]{:S(2)}) collective-permute-start(f32[10,2,8,128]{3,2,1,0:T(8,128)S(1)} %get-tuple-element.20), channel_id=1, source_target_pairs={{0,64},{64,0},{128,192},{192,128},{256,320},{320,256},{384,448},{4... | collective-permute-start | bytes 245768 | tf_op jit(solution)/shard_map/ppermute | solution.py:369

commit v8 on v7

--- a/solution.py
+++ b/solution.py
@@ -20,7 +20,7 @@
 ROWS = 40
 COLS = MOM * TC
 KEPT = 8 * BLK
-CHUNKS = 2
+CHUNKS = 1
 GROUP = 4
 diffusion = 0.16
 keep_weight = 1.0 - 6.0 * diffusion
@@ -107,26 +107,32 @@
     out_ref[BLK:ROWS, :] = codes.astype(jnp.int32).astype(jnp.int16)
 
 
-def deposit(x_ref, top_row, flip):
+def gathered_codes(x_ref):
     codes = functools.reduce(
         jnp.add, [x_ref[ROWS * k + BLK : ROWS * (k + 1), :KEPT].astype(jnp.int32) for k in range(8)]
     )
     code = codes[0:1, :] - 1
-    half = codes[1:2, :]
     scale = power(codes[2:3, :].astype(jnp.float32) - 15.0)
-    plane = lax.shift_right_arithmetic(code, 6)
-    if flip is not False:
-        plane = jnp.where(flip, PLANES - 1 - plane, plane)
-    rel = (code & (NY - 1)) - top_row
-    valid = (code >= 0) & (rel >= -HALO) & (rel < CHIP_ROWS + HALO)
-    spot = (half * PLANES + plane) * WIN + jnp.where(rel < 0, rel + WIN, rel)
-    spot = jnp.where(valid, spot, -1)
-    chosen = jnp.where(iota((2 * PLANES * WIN, KEPT), 0) == spot, scale, 0.0)
+    return code, lax.shift_right_arithmetic(code, 6), code & (NY - 1), codes[1:2, :], scale
+
+
+def gather_cells(x_ref, spot, scale, count):
+    chosen = jnp.where(iota((count, KEPT), 0) == spot, scale, 0.0)
     chosen = jnp.concatenate([256.0 * chosen, chosen], axis=1).astype(jnp.bfloat16)
     terms = [x_ref[ROWS * k : ROWS * k + BLK, :].astype(jnp.int32) for k in range(8)]
     high = [lax.shift_right_arithmetic(q, 8).astype(jnp.float32).astype(jnp.bfloat16) for q in terms]
     low = [(q & 255).astype(jnp.float32).astype(jnp.bfloat16) for q in terms]
     return jnp.dot(chosen, jnp.concatenate(high + low, axis=0), preferred_element_type=jnp.float32)
+
+
+def deposit(x_ref, top_row, flip):
+    code, plane, row, half, scale = gathered_codes(x_ref)
+    if flip is not False:
+        plane = jnp.where(flip, PLANES - 1 - plane, plane)
+    rel = row - top_row
+    valid = (code >= 0) & (rel >= -HALO) & (rel < CHIP_ROWS + HALO)
+    spot = (half * PLANES + plane) * WIN + jnp.where(rel < 0, rel + WIN, rel)
+    return gather_cells(x_ref, jnp.where(valid, spot, -1), scale, 2 * PLANES * WIN)
 
 
 class Stencil:
@@ -160,28 +166,11 @@
         return jnp.where(self.inside, f, 0.0)
 
 
-def make_message(planes_of, st, core, far_up, near_up, ref, part_ref):
-    for m in range(MOM):
-        g0, g1, g2, g3 = planes_of(m)
-        l0 = st.flat(g0)
-        once0 = st.kept(l0 + diffusion * g1)
-        once1 = st.kept(st.flat(g1) + diffusion * (g0 + g2))
-        parts = (
-            diffusion * diffusion * g0,
-            diffusion * (l0 + once0),
-            st.flat(once0) + diffusion * (diffusion * g0 + once1),
-            diffusion * diffusion * g3,
-        )
-        for i, f in enumerate(parts):
-            part_ref[i, m, 0] = f[0:RY]
-            part_ref[i, m, 1] = f[RY : 2 * RY]
-    part_ref[4] = jnp.zeros((MOM, 2, RY, NZ), jnp.float32)
-    a = jnp.where(core == 1, jnp.where(near_up, 2, 1), jnp.where(far_up, jnp.where(near_up, 0, 3), 4))
-    b = jnp.where(core == 1, jnp.where(near_up, 1, 2), jnp.where(far_up, 4, jnp.where(near_up, 3, 0)))
+def quantize(values_of, ref):
     sub = iota((RY, NZ), 0)
     tops = [jnp.zeros((RY, NZ), jnp.float32)] * 2
     for m in range(MOM):
-        values = [part_ref[i, m, h] for h in range(2) for i in (a, b)]
+        values = values_of(m)
         top = functools.reduce(jnp.maximum, [jnp.abs(v) for v in values])
         for k in (4, 2, 1):
             top = jnp.maximum(top, pltpu.roll(top, k, 0))
@@ -194,6 +183,49 @@
         ref[4 * MOM + k] = tops[k].astype(jnp.int32).astype(jnp.int16)
 
 
+def make_message(x_ref, core, top_row, far_up, near_up, ref, active):
+    @pl.when(active & (core == 1))
+    def _():
+        cells = deposit(x_ref, top_row, near_up)
+        st = Stencil(top_row)
+
+        def values_of(m):
+            g0, g1, g2, _ = st.planes(cells, m)
+            l0 = st.flat(g0)
+            once0 = st.kept(l0 + diffusion * g1)
+            once1 = st.kept(st.flat(g1) + diffusion * (g0 + g2))
+            outer = diffusion * (l0 + once0)
+            inner = st.flat(once0) + diffusion * (diffusion * g0 + once1)
+            first = jnp.where(near_up, inner, outer)
+            second = jnp.where(near_up, outer, inner)
+            return [f[RY * h : RY * (h + 1)] for h in range(2) for f in (first, second)]
+
+        quantize(values_of, ref)
+
+    @pl.when(active & (core == 0))
+    def _():
+        code, plane, row, half, scale = gathered_codes(x_ref)
+        rel = row - top_row
+        wanted = jnp.where(far_up, PLANES - 1, 0)
+        valid = (code >= 0) & (plane == wanted) & (rel >= 0) & (rel < CHIP_ROWS)
+        spot = jnp.where(valid, half * CHIP_ROWS + rel, -1)
+        cells = gather_cells(x_ref, spot, scale, 2 * CHIP_ROWS)
+        lane = iota((CHIP_ROWS, NZ), 1)
+
+        def values_of(m):
+            chunk = slice(NZ * (m // 2), NZ * (m // 2 + 1))
+            lower, upper = cells[:CHIP_ROWS, chunk], cells[CHIP_ROWS:, chunk]
+            if m % 2 == 0:
+                upper = pltpu.roll(upper, TC, 1)
+            else:
+                lower = pltpu.roll(lower, TC, 1)
+            f = diffusion * diffusion * jnp.where(lane < TC, lower, upper)
+            pair = (jnp.where(far_up, f, 0.0), jnp.where(far_up, 0.0, f))
+            return [g[RY * h : RY * (h + 1)] for h in range(2) for g in pair]
+
+        quantize(values_of, ref)
+
+
 def where_am_i():
     my_slab, my_dom = lax.axis_index("slab"), lax.axis_index("dom")
     core = lax.rem(my_dom, 2)
@@ -203,27 +235,16 @@
     return core, (my_dom - core) * RY, odd, upper, early
 
 
-def send_kernel(x_ref, early_ref, outer_ref, part_ref):
+def send_kernel(x_ref, early_ref, outer_ref):
     core, top_row, odd, upper, early = where_am_i()
-    cells = deposit(x_ref, top_row, odd)
-    st = Stencil(top_row)
-    make_message(lambda m: st.planes(cells, m), st, core, upper, odd, outer_ref, part_ref)
-
-    @pl.when(early)
-    def _():
-        inner = lambda m: st.planes(cells, m)[::-1]
-        make_message(inner, st, core, jnp.logical_not(upper), jnp.logical_not(odd), early_ref, part_ref)
-
-
-def late_kernel(x_ref, late_ref, part_ref):
+    make_message(x_ref, core, top_row, upper, odd, outer_ref, True)
+    make_message(x_ref, core, top_row, jnp.logical_not(upper), jnp.logical_not(odd), early_ref, early)
+
+
+def late_kernel(x_ref, late_ref):
     core, top_row, odd, upper, early = where_am_i()
-
-    @pl.when(jnp.logical_not(early))
-    def _():
-        cells = deposit(x_ref, top_row, jnp.logical_not(odd))
-        st = Stencil(top_row)
-        planes = lambda m: st.planes(cells, m)
-        make_message(planes, st, core, jnp.logical_not(upper), jnp.logical_not(odd), late_ref, part_ref)
+    late = jnp.logical_not(early)
+    make_message(x_ref, core, top_row, jnp.logical_not(upper), jnp.logical_not(odd), late_ref, late)
 
 
 def own_kernel(x_ref, own_ref, part_ref):
@@ -312,7 +333,6 @@
         out_shape=(message, message),
         in_specs=[vmem],
         out_specs=(vmem, vmem),
-        scratch_shapes=[pltpu.VMEM((5, MOM, 2, RY, NZ), jnp.float32)],
         compiler_params=limited,
         name="send",
     )(gathered)
@@ -324,7 +344,6 @@
         out_shape=message,
         in_specs=[vmem],
         out_specs=vmem,
-        scratch_shapes=[pltpu.VMEM((5, MOM, 2, RY, NZ), jnp.float32)],
         compiler_params=limited,
         cost_estimate=pl.CostEstimate(flops=400_000_000, bytes_accessed=8_000_000, transcendentals=0),
         name="late",

time: 42.9 us -> 42.6 us (level)
  starting transfers between devices: 13.8 us -> 13.2 us
where the time goes in v8:
time: 42.6 us; the launch traced here: 42.4 us
  blocking collectives  21.5 us (50%)
  starting transfers between devices  13.2 us (31%)
  Pallas kernels  4.04 us (9%)
  waiting for transfers between devices  2.24 us (5%)
  between operations  0.72 us (2%)
  other arithmetic  0.65 us (2%)
    all_gather x1, blocking collectives, local(): gathered = lax.all_gather(x, 'dom', tiled=True)  21.5 us
    ppermute x1, starting transfers between devices, local(): lax.ppermute(outer, both, swap_pairs(n_slabs, n_doms, 1, lambda s: True))  8.28 us
    ppermute x1, starting transfers between devices, local(): other = lax.ppermute(other, 'dom', [(i, i ^ 1) for i in range(n_doms)])  2.33 us
    ppermute x1, starting transfers between devices, local(): lax.ppermute(early, both, swap_pairs(n_slabs, n_doms, 0, half(True)))  1.92 us
    pallas_call x1, Pallas kernels, make_terms(): pl.pallas_call(terms_kernel, out_shape=pltpu.VMEM((ROWS, COLS), jnp.int16...  1.69 us
    pallas_call x1, Pallas kernels, make_send(): pl.pallas_call(send_kernel, out_shape=(message, message), in_specs=[vmem]...  1.38 us
    ppermute x1, waiting for transfers between devices, local(): lax.ppermute(outer, both, swap_pairs(n_slabs, n_doms, 1, lambda s: True))  1.34 us
    ppermute x1, waiting for transfers between devices, local(): other = lax.ppermute(other, 'dom', [(i, i ^ 1) for i in range(n_doms)])  0.9 us
  transfers between devices with their start and end apart: 4, of which 2 were waited for; matrix products, arithmetic and copies ran while one was open for 0% of the time, Pallas kernels for 2%

profile of v8, /device:TPU:1, one launch (start us, length us, event | category | flops | bytes accessed | tf_op | source)
XLA Modules:
  0.0 42.4 jit_solution(3686704446532421292)
XLA Ops:
  0.7 1.7 %terms.1 = s16[40,640]{1,0:T(8,128)(2,1)S(1)} custom-call(s32[1,1]{1,0:T(1,128)S(6)} %copy.6.count_ref, s32[1,32]{1,0:T(1,128)} %tile_hbm.1, s32[1,32]{1,0:T(1,128)} %slab_hbm.1, bf16[32,64,128]{2,1,0:T(8,128)(2,1)} %bitcast.4, bf16[10,32,128]{2,1,0:T(8,128)(2,1)} %bitcast.5), custom_call_target="tpu_custom_call" | custom-call | tf_op jit(solution)/shard_map/terms/pallas_call | solution.py:307
  2.4 21.5 %all_gather.3.x_ref = s16[320,640]{1,0:T(8,128)(2,1)S(1)} all-gather(s16[40,640]{1,0:T(8,128)(2,1)S(1)} %terms.1), channel_id=1, replica_groups=mesh['dom'=8,'slab'=64] {'dom'}, dimensions={0}, use_global_device_ids=true | all-gather | bytes 460800 | tf_op jit(solution)/shard_map/all_gather | solution.py:370
  23.9 1.4 %send.1 = (s16[42,8,128]{2,1,0:T(8,128)(2,1)S(1)}, s16[42,8,128]{2,1,0:T(8,128)(2,1)S(1)}) custom-call(s16[320,640]{1,0:T(8,128)(2,1)S(1)} %all_gather.3.x_ref), custom_call_target="tpu_custom_call" | custom-call | tf_op jit(solution)/shard_map/send/pallas_call | solution.py:331
  25.3 1.9 %collective-permute-start = (s16[42,8,128]{2,1,0:T(8,128)(2,1)S(1)}, s16[42,8,128]{2,1,0:T(8,128)(2,1)S(1)}, u32[]{:S(2)}, u32[]{:S(2)}) collective-permute-start(s16[42,8,128]{2,1,0:T(8,128)(2,1)S(1)} %get-tuple-element.13), channel_id=1, source_target_pairs={{0,2},{64,65},{128,130},{192,193},{256,258},{320,321},{384,386},{4... | collective-permute-start | bytes 258056 | tf_op jit(solution)/shard_map/ppermute | solution.py:376
  27.2 8.3 %collective-permute-start.1 = (s16[42,8,128]{2,1,0:T(8,128)(2,1)S(1)}, s16[42,8,128]{2,1,0:T(8,128)(2,1)S(1)}, u32[]{:S(2)}, u32[]{:S(2)}) collective-permute-start(s16[42,8,128]{2,1,0:T(8,128)(2,1)S(1)} %get-tuple-element.14), channel_id=1, source_target_pairs={{0,62},{64,127},{128,190},{192,255},{256,318},{320,383},{384,446},... | collective-permute-start | bytes 258056 | tf_op jit(solution)/shard_map/ppermute | solution.py:377
  35.5 0.7 %collective-permute-start.2 = (s16[42,8,128]{2,1,0:T(8,128)(2,1)S(1)}, s16[42,8,128]{2,1,0:T(8,128)(2,1)S(1)}, u32[]{:S(2)}, u32[]{:S(2)}) collective-permute-start(s16[42,8,128]{2,1,0:T(8,128)(2,1)S(1)} %late.1), channel_id=1, source_target_pairs={{16,18},{80,81},{144,146},{208,209},{272,274},{336,337},{400,402},... | collective-permute-start | bytes 258056 | tf_op jit(solution)/shard_map/ppermute | solution.py:378
  36.2 0.9 %own.1.own_ref = f32[10,2,8,128]{3,2,1,0:T(8,128)S(1)} custom-call(s16[320,640]{1,0:T(8,128)(2,1)S(1)} %all_gather.3.x_ref), custom_call_target="tpu_custom_call" | custom-call | flops 400000000 | bytes 8000000 | tf_op jit(solution)/shard_map/own/pallas_call | solution.py:354
  37.0 0.0 collective-permute-done.early_ref
  37.0 1.3 %collective-permute-done.1.outer_ref = s16[42,8,128]{2,1,0:T(8,128)(2,1)S(1)} collective-permute-done((s16[42,8,128]{2,1,0:T(8,128)(2,1)S(1)}, s16[42,8,128]{2,1,0:T(8,128)(2,1)S(1)}, u32[]{:S(2)}, u32[]{:S(2)}) %collective-permute-start.1) | collective-permute-done | bytes 86048 | tf_op jit(solution)/shard_map/ppermute | solution.py:377
  38.4 0.0 collective-permute-done.2.late_ref
  38.4 0.1 join.1
  38.5 2.3 %collective-permute-start.3 = (f32[10,2,8,128]{3,2,1,0:T(8,128)S(1)}, f32[10,2,8,128]{3,2,1,0:T(8,128)S(1)}, u32[]{:S(2)}, u32[]{:S(2)}) collective-permute-start(f32[10,2,8,128]{3,2,1,0:T(8,128)S(1)} %get-tuple-element.20), channel_id=1, source_target_pairs={{0,64},{64,0},{128,192},{192,128},{256,320},{320,256},{384,448},{4... | collective-permute-start | bytes 245768 | tf_op jit(solution)/shard_map/ppermute | solution.py:388
  40.8 0.9 %collective-permute-done.3 = f32[10,2,8,128]{3,2,1,0:T(8,128)S(1)} collective-permute-done((f32[10,2,8,128]{3,2,1,0:T(8,128)S(1)}, f32[10,2,8,128]{3,2,1,0:T(8,128)S(1)}, u32[]{:S(2)}, u32[]{:S(2)}) %collective-permute-start.3) | collective-permute-done | bytes 81952 | tf_op jit(solution)/shard_map/ppermute | solution.py:388
  41.7 0.6 %add.3 = f32[10,2,8,128]{3,2,1,0:T(8,128)} add(f32[10,2,8,128]{3,2,1,0:T(8,128)S(1)} %get-tuple-element.19, f32[10,2,8,128]{3,2,1,0:T(8,128)S(1)} %collective-permute-done.3) | non-fusion elementwise | flops 20480 | bytes 245760 | tf_op jit(solution)/shard_map/add | solution.py:389
  (1 shorter events, 0.0 us)
Async XLA Ops:
  25.3 11.8 %collective-permute-start = (s16[42,8,128]{2,1,0:T(8,128)(2,1)S(1)}, s16[42,8,128]{2,1,0:T(8,128)(2,1)S(1)}, u32[]{:S(2)}, u32[]{:S(2)}) collective-permute-start(s16[42,8,128]{2,1,0:T(8,128)(2,1)S(1)} %get-tuple-element.13), channel_id=1, source_target_pairs={{0,2},{64,65},{128,130},{192,193},{256,258},{320,321},{384,386},{4... | collective-permute-start | bytes 258056 | tf_op jit(solution)/shard_map/ppermute | solution.py:376
  27.2 11.2 %collective-permute-start.1 = (s16[42,8,128]{2,1,0:T(8,128)(2,1)S(1)}, s16[42,8,128]{2,1,0:T(8,128)(2,1)S(1)}, u32[]{:S(2)}, u32[]{:S(2)}) collective-permute-start(s16[42,8,128]{2,1,0:T(8,128)(2,1)S(1)} %get-tuple-element.14), channel_id=1, source_target_pairs={{0,62},{64,127},{128,190},{192,255},{256,318},{320,383},{384,446},... | collective-permute-start | bytes 258056 | tf_op jit(solution)/shard_map/ppermute | solution.py:377
  35.5 2.9 %collective-permute-start.2 = (s16[42,8,128]{2,1,0:T(8,128)(2,1)S(1)}, s16[42,8,128]{2,1,0:T(8,128)(2,1)S(1)}, u32[]{:S(2)}, u32[]{:S(2)}) collective-permute-start(s16[42,8,128]{2,1,0:T(8,128)(2,1)S(1)} %late.1), channel_id=1, source_target_pairs={{16,18},{80,81},{144,146},{208,209},{272,274},{336,337},{400,402},... | collective-permute-start | bytes 258056 | tf_op jit(solution)/shard_map/ppermute | solution.py:378
  38.5 3.2 %collective-permute-start.3 = (f32[10,2,8,128]{3,2,1,0:T(8,128)S(1)}, f32[10,2,8,128]{3,2,1,0:T(8,128)S(1)}, u32[]{:S(2)}, u32[]{:S(2)}) collective-permute-start(f32[10,2,8,128]{3,2,1,0:T(8,128)S(1)} %get-tuple-element.20), channel_id=1, source_target_pairs={{0,64},{64,0},{128,192},{192,128},{256,320},{320,256},{384,448},{4... | collective-permute-start | bytes 245768 | tf_op jit(solution)/shard_map/ppermute | solution.py:388

commit v9 on v8

--- a/solution.py
+++ b/solution.py
@@ -125,14 +125,14 @@
     return jnp.dot(chosen, jnp.concatenate(high + low, axis=0), preferred_element_type=jnp.float32)
 
 
-def deposit(x_ref, top_row, flip):
+def deposit(x_ref, top_row, flip, planes=PLANES):
     code, plane, row, half, scale = gathered_codes(x_ref)
     if flip is not False:
         plane = jnp.where(flip, PLANES - 1 - plane, plane)
     rel = row - top_row
-    valid = (code >= 0) & (rel >= -HALO) & (rel < CHIP_ROWS + HALO)
-    spot = (half * PLANES + plane) * WIN + jnp.where(rel < 0, rel + WIN, rel)
-    return gather_cells(x_ref, jnp.where(valid, spot, -1), scale, 2 * PLANES * WIN)
+    valid = (code >= 0) & (plane < planes) & (rel >= -HALO) & (rel < CHIP_ROWS + HALO)
+    spot = (half * planes + plane) * WIN + jnp.where(rel < 0, rel + WIN, rel)
+    return gather_cells(x_ref, jnp.where(valid, spot, -1), scale, 2 * planes * WIN)
 
 
 class Stencil:
@@ -142,12 +142,12 @@
         at_row = top_row + jnp.where(ring < CHIP_ROWS + HALO, ring, ring - WIN)
         self.inside = (at_row >= 0) & (at_row < NY)
 
-    def planes(self, cells, m):
+    def planes(self, cells, m, count=PLANES):
         chunk = slice(NZ * (m // 2), NZ * (m // 2 + 1))
         out = []
-        for q in range(PLANES):
+        for q in range(count):
             lower = cells[WIN * q : WIN * (q + 1), chunk]
-            upper = cells[WIN * (PLANES + q) : WIN * (PLANES + q + 1), chunk]
+            upper = cells[WIN * (count + q) : WIN * (count + q + 1), chunk]
             if m % 2 == 0:
                 upper = pltpu.roll(upper, TC, 1)
             else:
@@ -186,11 +186,11 @@
 def make_message(x_ref, core, top_row, far_up, near_up, ref, active):
     @pl.when(active & (core == 1))
     def _():
-        cells = deposit(x_ref, top_row, near_up)
+        cells = deposit(x_ref, top_row, near_up, 3)
         st = Stencil(top_row)
 
         def values_of(m):
-            g0, g1, g2, _ = st.planes(cells, m)
+            g0, g1, g2 = st.planes(cells, m, 3)
             l0 = st.flat(g0)
             once0 = st.kept(l0 + diffusion * g1)
             once1 = st.kept(st.flat(g1) + diffusion * (g0 + g2))

time: 42.6 us -> 42.6 us (level)
  no operation moved by 1% of the time
where the time goes in v9:
time: 42.6 us; the launch traced here: 42.4 us
  blocking collectives  21.5 us (50%)
  starting transfers between devices  13.2 us (31%)
  Pallas kernels  4.02 us (9%)
  waiting for transfers between devices  2.25 us (5%)
  between operations  0.72 us (2%)
  other arithmetic  0.65 us (2%)
    all_gather x1, blocking collectives, local(): gathered = lax.all_gather(x, 'dom', tiled=True)  21.5 us
    ppermute x1, starting transfers between devices, local(): lax.ppermute(outer, both, swap_pairs(n_slabs, n_doms, 1, lambda s: True))  8.29 us
    ppermute x1, starting transfers between devices, local(): other = lax.ppermute(other, 'dom', [(i, i ^ 1) for i in range(n_doms)])  2.35 us
    ppermute x1, starting transfers between devices, local(): lax.ppermute(early, both, swap_pairs(n_slabs, n_doms, 0, half(True)))  1.92 us
    pallas_call x1, Pallas kernels, make_terms(): pl.pallas_call(terms_kernel, out_shape=pltpu.VMEM((ROWS, COLS), jnp.int16...  1.69 us
    pallas_call x1, Pallas kernels, make_send(): pl.pallas_call(send_kernel, out_shape=(message, message), in_specs=[vmem]...  1.36 us
    ppermute x1, waiting for transfers between devices, local(): lax.ppermute(outer, both, swap_pairs(n_slabs, n_doms, 1, lambda s: True))  1.34 us
    ppermute x1, waiting for transfers between devices, local(): other = lax.ppermute(other, 'dom', [(i, i ^ 1) for i in range(n_doms)])  0.9 us
  transfers between devices with their start and end apart: 4, of which 2 were waited for; matrix products, arithmetic and copies ran while one was open for 0% of the time, Pallas kernels for 2%

profile of v9, /device:TPU:1, one launch (start us, length us, event | category | flops | bytes accessed | tf_op | source)
XLA Modules:
  0.0 42.4 jit_solution(3790849884827054470)
XLA Ops:
  0.7 1.7 %terms.1 = s16[40,640]{1,0:T(8,128)(2,1)S(1)} custom-call(s32[1,1]{1,0:T(1,128)S(6)} %copy.6.count_ref, s32[1,32]{1,0:T(1,128)} %tile_hbm.1, s32[1,32]{1,0:T(1,128)} %slab_hbm.1, bf16[32,64,128]{2,1,0:T(8,128)(2,1)} %bitcast.4, bf16[10,32,128]{2,1,0:T(8,128)(2,1)} %bitcast.5), custom_call_target="tpu_custom_call" | custom-call | tf_op jit(solution)/shard_map/terms/pallas_call | solution.py:307
  2.4 21.5 %all_gather.3.x_ref = s16[320,640]{1,0:T(8,128)(2,1)S(1)} all-gather(s16[40,640]{1,0:T(8,128)(2,1)S(1)} %terms.1), channel_id=1, replica_groups=mesh['dom'=8,'slab'=64] {'dom'}, dimensions={0}, use_global_device_ids=true | all-gather | bytes 460800 | tf_op jit(solution)/shard_map/all_gather | solution.py:370
  23.9 1.4 %send.1 = (s16[42,8,128]{2,1,0:T(8,128)(2,1)S(1)}, s16[42,8,128]{2,1,0:T(8,128)(2,1)S(1)}) custom-call(s16[320,640]{1,0:T(8,128)(2,1)S(1)} %all_gather.3.x_ref), custom_call_target="tpu_custom_call" | custom-call | tf_op jit(solution)/shard_map/send/pallas_call | solution.py:331
  25.2 1.9 %collective-permute-start = (s16[42,8,128]{2,1,0:T(8,128)(2,1)S(1)}, s16[42,8,128]{2,1,0:T(8,128)(2,1)S(1)}, u32[]{:S(2)}, u32[]{:S(2)}) collective-permute-start(s16[42,8,128]{2,1,0:T(8,128)(2,1)S(1)} %get-tuple-element.13), channel_id=1, source_target_pairs={{0,2},{64,65},{128,130},{192,193},{256,258},{320,321},{384,386},{4... | collective-permute-start | bytes 258056 | tf_op jit(solution)/shard_map/ppermute | solution.py:376
  27.2 8.3 %collective-permute-start.1 = (s16[42,8,128]{2,1,0:T(8,128)(2,1)S(1)}, s16[42,8,128]{2,1,0:T(8,128)(2,1)S(1)}, u32[]{:S(2)}, u32[]{:S(2)}) collective-permute-start(s16[42,8,128]{2,1,0:T(8,128)(2,1)S(1)} %get-tuple-element.14), channel_id=1, source_target_pairs={{0,62},{64,127},{128,190},{192,255},{256,318},{320,383},{384,446},... | collective-permute-start | bytes 258056 | tf_op jit(solution)/shard_map/ppermute | solution.py:377
  35.5 0.7 %collective-permute-start.2 = (s16[42,8,128]{2,1,0:T(8,128)(2,1)S(1)}, s16[42,8,128]{2,1,0:T(8,128)(2,1)S(1)}, u32[]{:S(2)}, u32[]{:S(2)}) collective-permute-start(s16[42,8,128]{2,1,0:T(8,128)(2,1)S(1)} %late.1), channel_id=1, source_target_pairs={{16,18},{80,81},{144,146},{208,209},{272,274},{336,337},{400,402},... | collective-permute-start | bytes 258056 | tf_op jit(solution)/shard_map/ppermute | solution.py:378
  36.2 0.9 %own.1.own_ref = f32[10,2,8,128]{3,2,1,0:T(8,128)S(1)} custom-call(s16[320,640]{1,0:T(8,128)(2,1)S(1)} %all_gather.3.x_ref), custom_call_target="tpu_custom_call" | custom-call | flops 400000000 | bytes 8000000 | tf_op jit(solution)/shard_map/own/pallas_call | solution.py:354
  37.0 0.0 collective-permute-done.early_ref
  37.0 1.3 %collective-permute-done.1.outer_ref = s16[42,8,128]{2,1,0:T(8,128)(2,1)S(1)} collective-permute-done((s16[42,8,128]{2,1,0:T(8,128)(2,1)S(1)}, s16[42,8,128]{2,1,0:T(8,128)(2,1)S(1)}, u32[]{:S(2)}, u32[]{:S(2)}) %collective-permute-start.1) | collective-permute-done | bytes 86048 | tf_op jit(solution)/shard_map/ppermute | solution.py:377
  38.4 0.0 collective-permute-done.2.late_ref
  38.4 0.1 join.1
  38.5 2.3 %collective-permute-start.3 = (f32[10,2,8,128]{3,2,1,0:T(8,128)S(1)}, f32[10,2,8,128]{3,2,1,0:T(8,128)S(1)}, u32[]{:S(2)}, u32[]{:S(2)}) collective-permute-start(f32[10,2,8,128]{3,2,1,0:T(8,128)S(1)} %get-tuple-element.20), channel_id=1, source_target_pairs={{0,64},{64,0},{128,192},{192,128},{256,320},{320,256},{384,448},{4... | collective-permute-start | bytes 245768 | tf_op jit(solution)/shard_map/ppermute | solution.py:388
  40.8 0.9 %collective-permute-done.3 = f32[10,2,8,128]{3,2,1,0:T(8,128)S(1)} collective-permute-done((f32[10,2,8,128]{3,2,1,0:T(8,128)S(1)}, f32[10,2,8,128]{3,2,1,0:T(8,128)S(1)}, u32[]{:S(2)}, u32[]{:S(2)}) %collective-permute-start.3) | collective-permute-done | bytes 81952 | tf_op jit(solution)/shard_map/ppermute | solution.py:388
  41.7 0.6 %add.3 = f32[10,2,8,128]{3,2,1,0:T(8,128)} add(f32[10,2,8,128]{3,2,1,0:T(8,128)S(1)} %get-tuple-element.19, f32[10,2,8,128]{3,2,1,0:T(8,128)S(1)} %collective-permute-done.3) | non-fusion elementwise | flops 20480 | bytes 245760 | tf_op jit(solution)/shard_map/add | solution.py:389
  (1 shorter events, 0.0 us)
Async XLA Ops:
  25.2 11.8 %collective-permute-start = (s16[42,8,128]{2,1,0:T(8,128)(2,1)S(1)}, s16[42,8,128]{2,1,0:T(8,128)(2,1)S(1)}, u32[]{:S(2)}, u32[]{:S(2)}) collective-permute-start(s16[42,8,128]{2,1,0:T(8,128)(2,1)S(1)} %get-tuple-element.13), channel_id=1, source_target_pairs={{0,2},{64,65},{128,130},{192,193},{256,258},{320,321},{384,386},{4... | collective-permute-start | bytes 258056 | tf_op jit(solution)/shard_map/ppermute | solution.py:376
  27.2 11.2 %collective-permute-start.1 = (s16[42,8,128]{2,1,0:T(8,128)(2,1)S(1)}, s16[42,8,128]{2,1,0:T(8,128)(2,1)S(1)}, u32[]{:S(2)}, u32[]{:S(2)}) collective-permute-start(s16[42,8,128]{2,1,0:T(8,128)(2,1)S(1)} %get-tuple-element.14), channel_id=1, source_target_pairs={{0,62},{64,127},{128,190},{192,255},{256,318},{320,383},{384,446},... | collective-permute-start | bytes 258056 | tf_op jit(solution)/shard_map/ppermute | solution.py:377
  35.5 2.9 %collective-permute-start.2 = (s16[42,8,128]{2,1,0:T(8,128)(2,1)S(1)}, s16[42,8,128]{2,1,0:T(8,128)(2,1)S(1)}, u32[]{:S(2)}, u32[]{:S(2)}) collective-permute-start(s16[42,8,128]{2,1,0:T(8,128)(2,1)S(1)} %late.1), channel_id=1, source_target_pairs={{16,18},{80,81},{144,146},{208,209},{272,274},{336,337},{400,402},... | collective-permute-start | bytes 258056 | tf_op jit(solution)/shard_map/ppermute | solution.py:378
  38.5 3.3 %collective-permute-start.3 = (f32[10,2,8,128]{3,2,1,0:T(8,128)S(1)}, f32[10,2,8,128]{3,2,1,0:T(8,128)S(1)}, u32[]{:S(2)}, u32[]{:S(2)}) collective-permute-start(f32[10,2,8,128]{3,2,1,0:T(8,128)S(1)} %get-tuple-element.20), channel_id=1, source_target_pairs={{0,64},{64,0},{128,192},{192,128},{256,320},{320,256},{384,448},{4... | collective-permute-start | bytes 245768 | tf_op jit(solution)/shard_map/ppermute | solution.py:388

commit v10 on v8

--- a/solution.py
+++ b/solution.py
@@ -231,7 +231,7 @@
     core = lax.rem(my_dom, 2)
     odd = lax.rem(my_slab, 2) == 1
     upper = lax.rem(lax.div(my_slab, 2), 2) == 1
-    early = lax.rem(lax.div(my_slab, 4), 8) < 4
+    early = lax.rem(lax.div(my_slab, 4), 8) < 1
     return core, (my_dom - core) * RY, odd, upper, early
 
 
@@ -372,7 +372,7 @@
     late = make_late(gathered)
     own = make_own(gathered)
     both = ("dom", "slab")
-    half = lambda low: lambda s: ((s // 4) % 8 < 4) == low
+    half = lambda low: lambda s: ((s // 4) % 8 < 1) == low
     early = lax.ppermute(early, both, swap_pairs(n_slabs, n_doms, 0, half(True)))
     outer = lax.ppermute(outer, both, swap_pairs(n_slabs, n_doms, 1, lambda s: True))
     late = lax.ppermute(late, both, swap_pairs(n_slabs, n_doms, 0, half(False)))

time: 42.6 us -> 42.6 us (level)
  no operation moved by 1% of the time
where the time goes in v10:
time: 42.6 us; the launch traced here: 42.4 us
  blocking collectives  21.5 us (50%)
  starting transfers between devices  13.2 us (31%)
  Pallas kernels  4.04 us (9%)
  waiting for transfers between devices  2.24 us (5%)
  between operations  0.72 us (2%)
  other arithmetic  0.65 us (2%)
    all_gather x1, blocking collectives, local(): gathered = lax.all_gather(x, 'dom', tiled=True)  21.5 us
    ppermute x1, starting transfers between devices, local(): lax.ppermute(outer, both, swap_pairs(n_slabs, n_doms, 1, lambda s: True))  8.28 us
    ppermute x1, starting transfers between devices, local(): other = lax.ppermute(other, 'dom', [(i, i ^ 1) for i in range(n_doms)])  2.33 us
    ppermute x1, starting transfers between devices, local(): lax.ppermute(early, both, swap_pairs(n_slabs, n_doms, 0, half(True)))  1.92 us
    pallas_call x1, Pallas kernels, make_terms(): pl.pallas_call(terms_kernel, out_shape=pltpu.VMEM((ROWS, COLS), jnp.int16...  1.69 us
    pallas_call x1, Pallas kernels, make_send(): pl.pallas_call(send_kernel, out_shape=(message, message), in_specs=[vmem]...  1.38 us
    ppermute x1, waiting for transfers between devices, local(): lax.ppermute(outer, both, swap_pairs(n_slabs, n_doms, 1, lambda s: True))  1.34 us
    ppermute x1, waiting for transfers between devices, local(): other = lax.ppermute(other, 'dom', [(i, i ^ 1) for i in range(n_doms)])  0.9 us
  transfers between devices with their start and end apart: 4, of which 2 were waited for; matrix products, arithmetic and copies ran while one was open for 0% of the time, Pallas kernels for 2%

profile of v10, /device:TPU:1, one launch (start us, length us, event | category | flops | bytes accessed | tf_op | source)
XLA Modules:
  0.0 42.4 jit_solution(7518012459955965906)
XLA Ops:
  0.7 1.7 %terms.1 = s16[40,640]{1,0:T(8,128)(2,1)S(1)} custom-call(s32[1,1]{1,0:T(1,128)S(6)} %copy.6.count_ref, s32[1,32]{1,0:T(1,128)} %tile_hbm.1, s32[1,32]{1,0:T(1,128)} %slab_hbm.1, bf16[32,64,128]{2,1,0:T(8,128)(2,1)} %bitcast.4, bf16[10,32,128]{2,1,0:T(8,128)(2,1)} %bitcast.5), custom_call_target="tpu_custom_call" | custom-call | tf_op jit(solution)/shard_map/terms/pallas_call | solution.py:307
  2.4 21.5 %all_gather.3.x_ref = s16[320,640]{1,0:T(8,128)(2,1)S(1)} all-gather(s16[40,640]{1,0:T(8,128)(2,1)S(1)} %terms.1), channel_id=1, replica_groups=mesh['dom'=8,'slab'=64] {'dom'}, dimensions={0}, use_global_device_ids=true | all-gather | bytes 460800 | tf_op jit(solution)/shard_map/all_gather | solution.py:370
  23.9 1.4 %send.1 = (s16[42,8,128]{2,1,0:T(8,128)(2,1)S(1)}, s16[42,8,128]{2,1,0:T(8,128)(2,1)S(1)}) custom-call(s16[320,640]{1,0:T(8,128)(2,1)S(1)} %all_gather.3.x_ref), custom_call_target="tpu_custom_call" | custom-call | tf_op jit(solution)/shard_map/send/pallas_call | solution.py:331
  25.3 1.9 %collective-permute-start = (s16[42,8,128]{2,1,0:T(8,128)(2,1)S(1)}, s16[42,8,128]{2,1,0:T(8,128)(2,1)S(1)}, u32[]{:S(2)}, u32[]{:S(2)}) collective-permute-start(s16[42,8,128]{2,1,0:T(8,128)(2,1)S(1)} %get-tuple-element.13), channel_id=1, source_target_pairs={{0,2},{64,65},{128,130},{192,193},{256,258},{320,321},{384,386},{4... | collective-permute-start | bytes 258056 | tf_op jit(solution)/shard_map/ppermute | solution.py:376
  27.2 8.3 %collective-permute-start.1 = (s16[42,8,128]{2,1,0:T(8,128)(2,1)S(1)}, s16[42,8,128]{2,1,0:T(8,128)(2,1)S(1)}, u32[]{:S(2)}, u32[]{:S(2)}) collective-permute-start(s16[42,8,128]{2,1,0:T(8,128)(2,1)S(1)} %get-tuple-element.14), channel_id=1, source_target_pairs={{0,62},{64,127},{128,190},{192,255},{256,318},{320,383},{384,446},... | collective-permute-start | bytes 258056 | tf_op jit(solution)/shard_map/ppermute | solution.py:377
  35.5 0.7 %collective-permute-start.2 = (s16[42,8,128]{2,1,0:T(8,128)(2,1)S(1)}, s16[42,8,128]{2,1,0:T(8,128)(2,1)S(1)}, u32[]{:S(2)}, u32[]{:S(2)}) collective-permute-start(s16[42,8,128]{2,1,0:T(8,128)(2,1)S(1)} %late.1), channel_id=1, source_target_pairs={{4,6},{68,69},{132,134},{196,197},{260,262},{324,325},{388,390},{4... | collective-permute-start | bytes 258056 | tf_op jit(solution)/shard_map/ppermute | solution.py:378
  36.2 0.9 %own.1.own_ref = f32[10,2,8,128]{3,2,1,0:T(8,128)S(1)} custom-call(s16[320,640]{1,0:T(8,128)(2,1)S(1)} %all_gather.3.x_ref), custom_call_target="tpu_custom_call" | custom-call | flops 400000000 | bytes 8000000 | tf_op jit(solution)/shard_map/own/pallas_call | solution.py:354
  37.0 0.0 collective-permute-done.early_ref
  37.0 1.3 %collective-permute-done.1.outer_ref = s16[42,8,128]{2,1,0:T(8,128)(2,1)S(1)} collective-permute-done((s16[42,8,128]{2,1,0:T(8,128)(2,1)S(1)}, s16[42,8,128]{2,1,0:T(8,128)(2,1)S(1)}, u32[]{:S(2)}, u32[]{:S(2)}) %collective-permute-start.1) | collective-permute-done | bytes 86048 | tf_op jit(solution)/shard_map/ppermute | solution.py:377
  38.4 0.0 collective-permute-done.2.late_ref
  38.4 0.1 join.1
  38.5 2.3 %collective-permute-start.3 = (f32[10,2,8,128]{3,2,1,0:T(8,128)S(1)}, f32[10,2,8,128]{3,2,1,0:T(8,128)S(1)}, u32[]{:S(2)}, u32[]{:S(2)}) collective-permute-start(f32[10,2,8,128]{3,2,1,0:T(8,128)S(1)} %get-tuple-element.20), channel_id=1, source_target_pairs={{0,64},{64,0},{128,192},{192,128},{256,320},{320,256},{384,448},{4... | collective-permute-start | bytes 245768 | tf_op jit(solution)/shard_map/ppermute | solution.py:388
  40.8 0.9 %collective-permute-done.3 = f32[10,2,8,128]{3,2,1,0:T(8,128)S(1)} collective-permute-done((f32[10,2,8,128]{3,2,1,0:T(8,128)S(1)}, f32[10,2,8,128]{3,2,1,0:T(8,128)S(1)}, u32[]{:S(2)}, u32[]{:S(2)}) %collective-permute-start.3) | collective-permute-done | bytes 81952 | tf_op jit(solution)/shard_map/ppermute | solution.py:388
  41.7 0.6 %add.3 = f32[10,2,8,128]{3,2,1,0:T(8,128)} add(f32[10,2,8,128]{3,2,1,0:T(8,128)S(1)} %get-tuple-element.19, f32[10,2,8,128]{3,2,1,0:T(8,128)S(1)} %collective-permute-done.3) | non-fusion elementwise | flops 20480 | bytes 245760 | tf_op jit(solution)/shard_map/add | solution.py:389
  (1 shorter events, 0.0 us)
Async XLA Ops:
  25.3 11.8 %collective-permute-start = (s16[42,8,128]{2,1,0:T(8,128)(2,1)S(1)}, s16[42,8,128]{2,1,0:T(8,128)(2,1)S(1)}, u32[]{:S(2)}, u32[]{:S(2)}) collective-permute-start(s16[42,8,128]{2,1,0:T(8,128)(2,1)S(1)} %get-tuple-element.13), channel_id=1, source_target_pairs={{0,2},{64,65},{128,130},{192,193},{256,258},{320,321},{384,386},{4... | collective-permute-start | bytes 258056 | tf_op jit(solution)/shard_map/ppermute | solution.py:376
  27.2 11.2 %collective-permute-start.1 = (s16[42,8,128]{2,1,0:T(8,128)(2,1)S(1)}, s16[42,8,128]{2,1,0:T(8,128)(2,1)S(1)}, u32[]{:S(2)}, u32[]{:S(2)}) collective-permute-start(s16[42,8,128]{2,1,0:T(8,128)(2,1)S(1)} %get-tuple-element.14), channel_id=1, source_target_pairs={{0,62},{64,127},{128,190},{192,255},{256,318},{320,383},{384,446},... | collective-permute-start | bytes 258056 | tf_op jit(solution)/shard_map/ppermute | solution.py:377
  35.5 2.9 %collective-permute-start.2 = (s16[42,8,128]{2,1,0:T(8,128)(2,1)S(1)}, s16[42,8,128]{2,1,0:T(8,128)(2,1)S(1)}, u32[]{:S(2)}, u32[]{:S(2)}) collective-permute-start(s16[42,8,128]{2,1,0:T(8,128)(2,1)S(1)} %late.1), channel_id=1, source_target_pairs={{4,6},{68,69},{132,134},{196,197},{260,262},{324,325},{388,390},{4... | collective-permute-start | bytes 258056 | tf_op jit(solution)/shard_map/ppermute | solution.py:378
  38.5 3.2 %collective-permute-start.3 = (f32[10,2,8,128]{3,2,1,0:T(8,128)S(1)}, f32[10,2,8,128]{3,2,1,0:T(8,128)S(1)}, u32[]{:S(2)}, u32[]{:S(2)}) collective-permute-start(f32[10,2,8,128]{3,2,1,0:T(8,128)S(1)} %get-tuple-element.20), channel_id=1, source_target_pairs={{0,64},{64,0},{128,192},{192,128},{256,320},{320,256},{384,448},{4... | collective-permute-start | bytes 245768 | tf_op jit(solution)/shard_map/ppermute | solution.py:388
